TPU v7x, 256 devices: a whole 4x4x8 slice. The times are simulated.
256 devices in a mesh: expert: 32 (over z, x), tensor: 8 (over y, core).
Axes of the slice: x: 4, y: 4, z: 8, core: 2. Of those that a mesh axis runs over, the one named last changes fastest.
Arguments:
- query_latent: bfloat16 [1024, 64, 576], P(('expert', 'tensor')), may hold values from -9 to 9
- kv_cache: bfloat16 [1024, 768, 576], P(('expert', 'tensor')), may hold values from -4 to 4
- cache_len: int32 [1024], P(('expert', 'tensor')), may hold values from 192 to 768, as said below
- value_up: bfloat16 [64, 512, 128], P('tensor'), may hold values from -0.25 to 0.25
- hidden_in: bfloat16 [1024, 7168], P('expert', 'tensor'), may hold values from -6 to 6
- norm_gain: bfloat16 [7168], P('tensor'), may hold values from 0.099609375 to 1.8984375
- expert_ids: int32 [1024, 8], P('expert'), may hold values from 0 to 29, all different within a row; in each aligned block of 32 rows (0 to 31, 32 to 63, ...) at most 18 rows name the same one
- route_weight: int32 [1024, 8], P('expert'), may hold values from 1 to 4095
- placement_plan: int32 [32], replicated, may hold values from 0 to 29, as said below
- updated_list: int32 [30], replicated, may hold values from 0 to 29, each once
- learner_gate: bfloat16 [30, 7168, 1024], P(None, 'expert', 'tensor'), may hold values from -0.0625 to 0.0625
- learner_up: bfloat16 [30, 7168, 1024], P(None, 'expert', 'tensor'), may hold values from -0.0625 to 0.0625
- learner_down: bfloat16 [30, 7168, 1024], P(None, 'expert', 'tensor'), may hold values from -0.1875 to 0.1875
Outputs:
- attn_values: bfloat16 [1024, 8192], P('expert', 'tensor')
- moe_out: bfloat16 [1024, 7168], P('expert', 'tensor')
- slot_gate: bfloat16 [32, 7168, 1024], P('expert', None, 'tensor')
Inputs may be any that keep to these rules, and one draw needn't show every extreme that they name: `cache_len`: some row has all 768 positions valid. `placement_plan`: every expert is held by one or two slots; 2 experts by two. `expert_ids`: each row names 8 different experts; among the 32 rows of one device no expert is named more than 18 times. `updated_list`: each expert once.
All inputs are finite; a program needn't handle non-finite values.
Results may differ from a plain program's by a relative error of at most 0.015.
Values may be sent and summed in bfloat16 or wider, within the bound.
No kernel may reach another device: no remote copies, remote signals or barrier semaphores. Data moves between devices by JAX's collectives and lax.ppermute only.
A program may use at most 128 MiB of HBM per device.

v0:
```python
import jax
import jax.numpy as jnp
from jax import lax
from jax.sharding import PartitionSpec as P

KVL = 512


SCORE_SCALE = 192.0 ** (-0.5)
ROUTE_SCALE = 2.5
NORM_EPSILON = 1e-06


def attend(query_latent, kv_cache, cache_len):
    scores = (
        jnp.einsum("rhc,rpc->rhp", query_latent, kv_cache, preferred_element_type=jnp.float32)
        * SCORE_SCALE
    )
    allowed = (jnp.arange(kv_cache.shape[1], dtype=jnp.int32)[None, :] < cache_len[:, None])[
        :, None, :
    ]
    scores = jnp.where(allowed, scores, -1e30)
    highest = jnp.max(scores, axis=2, keepdims=True)
    lifted = jnp.where(allowed, jnp.exp(scores - highest), 0.0)
    totals = jnp.sum(lifted, axis=2, keepdims=True)
    mixed = jnp.einsum(
        "rhp,rpc->rhc",
        lifted.astype(jnp.bfloat16),
        kv_cache[:, :, :KVL],
        preferred_element_type=jnp.float32,
    )
    return (mixed / totals).astype(jnp.bfloat16)


def route_targets(expert_ids, placement_plan, expert_total, capacity):
    row_count, choose_count = expert_ids.shape
    entries = row_count * choose_count
    slot_total = placement_plan.shape[0]
    flat_ids = expert_ids.reshape(entries)
    expert_range = jnp.arange(expert_total, dtype=jnp.int32)
    holders = (placement_plan[None, :] == expert_range[:, None]).astype(jnp.int32)
    holder_rank = jnp.cumsum(holders, axis=1) - 1
    picked = (flat_ids[:, None] == expert_range[None, :]).astype(jnp.int32)
    entry_hold = jnp.dot(picked, holders)
    entry_rank = jnp.dot(picked, holder_rank)
    matched = entry_hold * (entry_rank == 0).astype(jnp.int32)
    slot_index = jnp.sum(matched * jnp.arange(slot_total, dtype=jnp.int32)[None, :], axis=1)
    position = jnp.sum(matched * (jnp.cumsum(matched, axis=0) - 1), axis=1)
    return slot_index * capacity + position


def per_device(
    query_latent,
    kv_cache,
    cache_len,
    value_up,
    hidden_in,
    norm_gain,
    expert_ids,
    route_weight,
    placement_plan,
    updated_list,
    learner_gate,
    learner_up,
    learner_down,
):
    expert_total = updated_list.shape[0]
    entry_range = jnp.arange(expert_total, dtype=jnp.int32)
    learner_entry = jnp.sum(
        entry_range[None, :] * (updated_list[None, :] == placement_plan[:, None]).astype(jnp.int32),
        axis=1,
    )
    held_gate, held_up = (
        lax.all_to_all(
            jnp.take(learner_gate, learner_entry, axis=0),
            "expert",
            split_axis=0,
            concat_axis=1,
            tiled=True,
        ),
        lax.all_to_all(
            jnp.take(learner_up, learner_entry, axis=0),
            "expert",
            split_axis=0,
            concat_axis=1,
            tiled=True,
        ),
    )
    chosen_down = jnp.take(learner_down, learner_entry, axis=0)
    held_down = lax.all_to_all(chosen_down, "expert", split_axis=0, concat_axis=1, tiled=True)
    latent = attend(query_latent, kv_cache, cache_len)
    head_rows = lax.all_to_all(latent, "tensor", split_axis=1, concat_axis=0, tiled=True)
    projected = jnp.einsum("rhc,hcv->rhv", head_rows, value_up, preferred_element_type=jnp.float32)
    attn_values = projected.astype(jnp.bfloat16).reshape(
        head_rows.shape[0], projected.shape[1] * projected.shape[2]
    )
    row_count, choose_count = expert_ids.shape
    slot_total = placement_plan.shape[0]
    capacity = min(row_count, 2 * ((row_count * choose_count + expert_total - 1) // expert_total))
    targets = route_targets(expert_ids, placement_plan, expert_total, capacity)
    entry_row = jnp.arange(row_count * choose_count, dtype=jnp.int32) // choose_count
    whole_rows, whole_gain = (
        lax.all_gather(hidden_in, "tensor", axis=1, tiled=True),
        lax.all_gather(norm_gain.reshape(1, norm_gain.shape[0]), "tensor", axis=1, tiled=True),
    )
    widened = whole_rows.astype(jnp.float32)
    normed = (
        widened
        * lax.rsqrt(jnp.mean(widened * widened, axis=1, keepdims=True) + NORM_EPSILON)
        * whole_gain.astype(jnp.float32)
    ).astype(jnp.bfloat16)
    outbound = (
        jnp.zeros((slot_total * capacity, normed.shape[1]), jnp.bfloat16)
        .at[targets]
        .set(normed[entry_row])
    )
    arrived = lax.all_to_all(outbound, "expert", split_axis=0, concat_axis=0, tiled=True)
    gate_proj = jnp.dot(arrived, held_gate[0], preferred_element_type=jnp.float32)
    up_proj = jnp.dot(arrived, held_up[0], preferred_element_type=jnp.float32)
    activated = (jax.nn.silu(gate_proj) * up_proj).astype(jnp.bfloat16)
    partial_out = lax.dot_general(
        activated, held_down[0], (((1,), (1,)), ((), ())), preferred_element_type=jnp.float32
    )
    shared = lax.psum_scatter(
        partial_out.astype(jnp.bfloat16), "tensor", scatter_dimension=1, tiled=True
    )
    returned = lax.all_to_all(shared, "expert", split_axis=0, concat_axis=0, tiled=True)
    entry_out = (
        returned[targets].astype(jnp.float32).reshape(row_count, choose_count, returned.shape[1])
    )
    weights_float = route_weight.astype(jnp.float32)
    gates = ROUTE_SCALE * weights_float / jnp.sum(weights_float, axis=1, keepdims=True)
    moe_out = jnp.sum(gates[:, :, None] * entry_out, axis=1).astype(jnp.bfloat16)
    return (attn_values, moe_out, held_gate)


def solution(mesh):
    in_specs = (
        P(("expert", "tensor"), None, None),
        P(("expert", "tensor"), None, None),
        P(("expert", "tensor")),
        P("tensor", None, None),
        P("expert", "tensor"),
        P("tensor"),
        P("expert", None),
        P("expert", None),
        P(),
        P(),
        P(None, "expert", "tensor"),
        P(None, "expert", "tensor"),
        P(None, "expert", "tensor"),
    )
    out_specs = (P("expert", "tensor"), P("expert", "tensor"), P("expert", None, "tensor"))
    return jax.shard_map(
        per_device, mesh=mesh, in_specs=in_specs, out_specs=out_specs, check_vma=False
    )
```

profile of v0, /device:TPU:2, one launch (start us, length us, event | category | flops | bytes accessed | tf_op | source)
XLA Modules:
  0.0 589.7 jit_solution(17599667615994118623)
XLA Ops:
  7.2 1.0 select_reduce_fusion
  9.3 1.0 gather_fusion.1
  10.3 3.7 gather_fusion.2
  14.1 2.1 gather_fusion.3
  16.2 4.8 broadcast_select_fusion.2
  21.0 11.7 %all-to-all-start.2 = ((bf16[32,224,128]{2,1,0:T(8,128)(2,1)}), bf16[32,224,128]{2,1,0:T(8,128)(2,1)S(1)}, u32[]{:S(2)}, u32[]{:S(2)}) async-start(bf16[32,224,128]{2,1,0:T(8,128)(2,1)} %get-tuple-element.6), calls=%async_computation.2 | async-start | bytes 3670016 | tf_op jit(solution)/shard_map/all_to_all | solution.py:74
  33.1 43.4 %all-to-all-done.2 = bf16[32,224,128]{2,1,0:T(8,128)(2,1)S(1)} async-done(((bf16[32,224,128]{2,1,0:T(8,128)(2,1)}), bf16[32,224,128]{2,1,0:T(8,128)(2,1)S(1)}, u32[]{:S(2)}, u32[]{:S(2)}) %all-to-all-start.2) | async-done | bytes 1835040 | tf_op jit(solution)/shard_map/all_to_all | solution.py:74
  76.5 1.2 copy-done.2
  77.8 6.7 %all-to-all-start.3 = ((bf16[32,224,128]{2,1,0:T(8,128)(2,1)}), bf16[32,224,128]{2,1,0:T(8,128)(2,1)S(1)}, u32[]{:S(2)}, u32[]{:S(2)}) async-start(bf16[32,224,128]{2,1,0:T(8,128)(2,1)} %get-tuple-element.7), calls=%async_computation.3 | async-start | bytes 3670016 | tf_op jit(solution)/shard_map/all_to_all | solution.py:81
  85.8 13.4 %all-gather.1 = bf16[8,1,896]{2,1,0:T(2,128)(2,1)S(1)} all-gather(bf16[1,1,896]{2,1,0:T(2,128)(2,1)S(1)} %reshape.212), channel_id=2, replica_groups=mesh['expert'=32,'tensor'=8] {'tensor'}, dimensions={0}, use_global_device_ids=true | all-gather | bytes 16128 | tf_op jit(solution)/shard_map/all_gather | solution.py:104
  99.4 13.6 %all_gather.6 = bf16[32,7168]{1,0:T(8,128)(2,1)S(1)} all-gather(bf16[32,896]{1,0:T(8,128)(2,1)S(1)} %copy-done.6), channel_id=1, replica_groups=mesh['expert'=32,'tensor'=8] {'tensor'}, dimensions={1}, use_global_device_ids=true | all-gather | bytes 516096 | tf_op jit(solution)/shard_map/all_gather | solution.py:103
  113.4 20.7 %scatter_custom_fusion = bf16[576,7168]{1,0:T(8,128)(2,1)} fusion(s32[256]{0:T(256)S(1)} %bitcast.65, bf16[]{:T(256)} %constant.57.clone.1, bf16[32,7168]{1,0:T(8,128)(2,1)S(1)} %fusion.20, s32[1024]{0:T(1024)S(1)} %pad_clamp_fusion.2), kind=kCustom, calls=%fused_computation.8 | custom fusion | bytes 8257538 | tf_op jit(solution)/shard_map/scatter | solution.py:115
  134.1 10.4 %all_to_all.56 = bf16[32,18,7168]{2,1,0:T(8,128)(2,1)} reshape(bf16[576,7168]{1,0:T(8,128)(2,1)} %scatter_custom_fusion) | data formatting | bytes 16515072 | tf_op jit(solution)/shard_map/all_to_all | solution.py:117
  144.5 251.9 %all_to_all.72 = bf16[32,18,7168]{2,1,0:T(8,128)(2,1)} all-to-all(bf16[32,18,7168]{2,1,0:T(8,128)(2,1)} %all_to_all.56), channel_id=1, replica_groups=mesh['expert'=32,'tensor'=8] {'expert'}, dimensions={0} | all-to-all | bytes 16515072 | tf_op jit(solution)/shard_map/all_to_all | solution.py:117
  396.4 5.6 all-to-all-start.4
  402.3 10.5 %all_to_all.58 = bf16[576,7168]{1,0:T(8,128)(2,1)} reshape(bf16[32,18,7168]{2,1,0:T(8,128)(2,1)} %all_to_all.72) | data formatting | bytes 16515072 | tf_op jit(solution)/shard_map/all_to_all | solution.py:117
  412.8 6.1 %fusion.40 = f32[576,128]{1,0:T(8,128)S(1)} fusion(bf16[576,7168]{1,0:T(8,128)(2,1)} %all_to_all.58, bf16[7168,128]{1,0:T(8,128)(2,1)} %bitcast.58), kind=kOutput, calls=%fused_computation.80 | convolution fusion | flops 1056964608 | bytes 10387456 | tf_op jit(solution)/shard_map/dot_general | solution.py:118
  419.0 27.4 %all-to-all-done.4 = bf16[32,224,128]{2,1,0:T(8,128)(2,1)} async-done(((bf16[32,224,128]{2,1,0:T(8,128)(2,1)}), bf16[32,224,128]{2,1,0:T(8,128)(2,1)}, u32[]{:S(2)}, u32[]{:S(2)}) %all-to-all-start.4) | async-done | bytes 1835040 | tf_op jit(solution)/shard_map/all_to_all | solution.py:90
  446.3 13.6 %convolution_convert_fusion = bf16[576,7168]{1,0:T(8,128)(2,1)} fusion(bf16[7168,128]{1,0:T(8,128)(2,1)} %bitcast.11, bf16[576,7168]{1,0:T(8,128)(2,1)} %all_to_all.58, bf16[7168,128]{1,0:T(8,128)(2,1)S(1)} %bitcast.57, f32[576,128]{1,0:T(8,128)S(1)} %fusion.40), kind=kOutput, calls=%fused_computation.7 | convolution fusion | flops 2118500352 | bytes 20480000 | tf_op jit(solution)/shard_map/dot_general | solution.py:121
  459.9 12.4 %copy.44 = bf16[576,7168]{0,1:T(8,128)(2,1)} copy(bf16[576,7168]{1,0:T(8,128)(2,1)} %convolution_convert_fusion) | data formatting | bytes 16515072
  473.3 3.0 fusion.39
  476.3 3.0 fusion.13
  479.3 0.9 copy.37
  480.2 3.6 all-to-all-start
  483.8 46.4 %reduce-scatter.4.cloned.1.call-done = bf16[896,576]{1,0:T(8,128)(2,1)} async-done(((bf16[7168,576]{1,0:T(8,128)(2,1)}), bf16[896,576]{1,0:T(8,128)(2,1)}) %reduce-scatter.4.cloned.1.call-update) | async-done | bytes 1032208
  530.2 1.7 copy.45
  531.9 1.3 all_to_all.62
  533.2 10.2 %all-to-all-start.5 = ((bf16[32,18,896]{2,1,0:T(8,128)(2,1)}), bf16[32,18,896]{2,1,0:T(8,128)(2,1)S(1)}, u32[]{:S(2)}, u32[]{:S(2)}) async-start(bf16[32,18,896]{2,1,0:T(8,128)(2,1)} %all_to_all.62), calls=%async_computation.5 | async-start | bytes 2752512 | tf_op jit(solution)/shard_map/all_to_all | solution.py:127
  544.6 33.3 %all-to-all-done.5 = bf16[32,18,896]{2,1,0:T(8,128)(2,1)S(1)} async-done(((bf16[32,18,896]{2,1,0:T(8,128)(2,1)}), bf16[32,18,896]{2,1,0:T(8,128)(2,1)S(1)}, u32[]{:S(2)}, u32[]{:S(2)}) %all-to-all-start.5) | async-done | bytes 1032224 | tf_op jit(solution)/shard_map/all_to_all | solution.py:127
  578.3 1.2 gather_fusion
  579.5 1.0 fusion.21
  580.5 1.2 copy.59
  (63 shorter events, 7.1 us)
Async XLA Ops:
  7.2 2.1 copy-start
  10.3 3.7 copy-start.4
  21.0 11.8 %copy-start.8 = (s32[32,8]{0,1:T(8,128)S(1)}, s32[32,8]{0,1:T(8,128)}, u32[]{:S(2)}) copy-start(s32[32,8]{0,1:T(8,128)} %param.21) | copy-start | bytes 3076
  21.0 11.9 %copy-start.10 = (s32[32]{0:T(128)S(1)}, s32[32]{0:T(128)}, u32[]{:S(2)}) copy-start(s32[32]{0:T(128)} %param.23) | copy-start | bytes 388
  21.0 55.5 %all-to-all-start.2 = ((bf16[32,224,128]{2,1,0:T(8,128)(2,1)}), bf16[32,224,128]{2,1,0:T(8,128)(2,1)S(1)}, u32[]{:S(2)}, u32[]{:S(2)}) async-start(bf16[32,224,128]{2,1,0:T(8,128)(2,1)} %get-tuple-element.6), calls=%async_computation.2 | async-start | bytes 3670016 | tf_op jit(solution)/shard_map/all_to_all | solution.py:74
  76.5 1.2 copy-start.2
  76.5 9.3 %copy-start.9 = (bf16[896]{0:T(1024)(128)(2,1)S(1)}, bf16[896]{0:T(1024)(128)(2,1)}, u32[]{:S(2)}) copy-start(bf16[896]{0:T(1024)(128)(2,1)} %param.20) | copy-start | bytes 5380
  76.5 22.9 %copy-start.6 = (bf16[32,896]{1,0:T(8,128)(2,1)S(1)}, bf16[32,896]{1,0:T(8,128)(2,1)}, u32[]{:S(2)}) copy-start(bf16[32,896]{1,0:T(8,128)(2,1)} %param.19) | copy-start | bytes 172036
  77.8 66.7 %all-to-all-start.3 = ((bf16[32,224,128]{2,1,0:T(8,128)(2,1)}), bf16[32,224,128]{2,1,0:T(8,128)(2,1)S(1)}, u32[]{:S(2)}, u32[]{:S(2)}) async-start(bf16[32,224,128]{2,1,0:T(8,128)(2,1)} %get-tuple-element.7), calls=%async_computation.3 | async-start | bytes 3670016 | tf_op jit(solution)/shard_map/all_to_all | solution.py:81
  396.4 49.9 %all-to-all-start.4 = ((bf16[32,224,128]{2,1,0:T(8,128)(2,1)}), bf16[32,224,128]{2,1,0:T(8,128)(2,1)}, u32[]{:S(2)}, u32[]{:S(2)}) async-start(bf16[32,224,128]{2,1,0:T(8,128)(2,1)} %get-tuple-element.8), calls=%async_computation.4 | async-start | bytes 3670016 | tf_op jit(solution)/shard_map/all_to_all | solution.py:90
  402.1 128.1 %reduce-scatter.4.cloned.1.call-start = ((), (), s32[]{:S(2)}) async-start(), calls=%async_computation.7 | async-start | bytes 10321920
  472.3 0.7 copy-start.11
  472.3 1.0 copy-start.12
  480.2 53.0 %all-to-all-start = ((bf16[4,64,512]{2,0,1:T(4,128)(2,1)}), bf16[4,64,512]{2,0,1:T(4,128)(2,1)S(1)}, u32[]{:S(2)}, u32[]{:S(2)}) async-start(bf16[4,64,512]{2,0,1:T(4,128)(2,1)} %copy.37), calls=%async_computation | async-start | bytes 524288 | tf_op jit(solution)/shard_map/all_to_all | solution.py:92
  533.2 10.3 %copy-start.7 = (s32[32,8]{0,1:T(8,128)S(1)}, s32[32,8]{0,1:T(8,128)}, u32[]{:S(2)}) copy-start(s32[32,8]{0,1:T(8,128)} %param.22) | copy-start | bytes 3076
  533.2 10.6 %copy-start.5 = (bf16[8,512,128]{2,1,0:T(8,128)(2,1)S(1)}, bf16[8,512,128]{2,1,0:T(8,128)(2,1)}, u32[]{:S(2)}) copy-start(bf16[8,512,128]{2,1,0:T(8,128)(2,1)} %param.18) | copy-start | bytes 3145732
  533.2 44.8 %all-to-all-start.5 = ((bf16[32,18,896]{2,1,0:T(8,128)(2,1)}), bf16[32,18,896]{2,1,0:T(8,128)(2,1)S(1)}, u32[]{:S(2)}, u32[]{:S(2)}) async-start(bf16[32,18,896]{2,1,0:T(8,128)(2,1)} %all_to_all.62), calls=%async_computation.5 | async-start | bytes 2752512 | tf_op jit(solution)/shard_map/all_to_all | solution.py:127
  578.3 2.2 copy-start.3
  580.5 2.1 copy-start.1
Sparse Core Ops, SparseCore 0:
  472.5 57.6 reduce-scatter.3
where the time goes:
time: 595 us; the launch traced here: 590 us
  blocking collectives  279 us (47%)
  waiting for transfers between devices  150 us (25%)
  local copies, waits for them, and re-layouts  71.8 us (12%)
  starting transfers between devices  38.2 us (6%)
  matrix products  26.5 us (4%)
  between operations  14.5 us (2%)
  other arithmetic  9.34 us (2%)
    all_to_all x1, blocking collectives, per_device(): lax.all_to_all(outbound, 'expert', split_axis=0, concat_axis=0, tiled=True)  252 us
    unnamed x2, waiting for transfers between devices  46.4 us
    all_to_all x1, waiting for transfers between devices, per_device(): lax.all_to_all(jnp.take(learner_gate, learner_entry, axis=0), 'expert', s...  43.4 us
    all_to_all x1, waiting for transfers between devices, per_device(): lax.all_to_all(shared, 'expert', split_axis=0, concat_axis=0, tiled=True)  33.3 us
    all_to_all x1, waiting for transfers between devices, per_device(): lax.all_to_all(chosen_down, 'expert', split_axis=0, concat_axis=1, tiled=...  27.4 us
    all_to_all x2, local copies, waits for them, and re-layouts, per_device(): lax.all_to_all(outbound, 'expert', split_axis=0, concat_axis=0, tiled=True)  20.9 us
    scatter x1, local copies, waits for them, and re-layouts, per_device(): outbound = jnp.zeros((slot_total * capacity, normed.shape[1]), jnp.bfloat...  20.7 us
    unnamed x31, local copies, waits for them, and re-layouts  18.5 us
  transfers between devices with their start and end apart: 6, of which 4 were waited for; matrix products, arithmetic and copies ran while one was open for 7% of the time, Pallas kernels for 0%

commit v1 on v0

v1 whole, which is shorter than its diff:
```python
import jax
import jax.numpy as jnp
from jax import lax
from jax.experimental import pallas as pl
from jax.experimental.pallas import tpu as pltpu
from jax.sharding import PartitionSpec as P

KVL = 512
SCORE_SCALE = 192.0 ** (-0.5)
ROUTE_SCALE = 2.5
NORM_EPSILON = 1e-06

NZ, NX, NT = 8, 4, 8
RB = 32
ZR = NX * RB
ROWS = NZ * ZR
SLICE = 224
WIDE = NX * SLICE
GL = 256
FT = 128
FX = FT // NX
NE = 30
TOP = 8
DIM = 7168

X_GROUPS = [[z * NX + x for x in range(NX)] for z in range(NZ)]
Z_GROUPS = [[z * NX + x for z in range(NZ)] for x in range(NX)]
SWAP = [
    ((z * NX + x) * NT + t, (t * NX + x) * NT + z)
    for z in range(NZ)
    for x in range(NX)
    for t in range(NT)
]
BF = jnp.bfloat16
F32 = jnp.float32


def swap_zt(value):
    return lax.ppermute(value, ("expert", "tensor"), SWAP)


def exchange(value, axis, groups=None):
    return lax.all_to_all(
        value, axis, split_axis=0, concat_axis=0, tiled=True, axis_index_groups=groups
    )


def attend(query_latent, kv_cache, cache_len):
    scores = (
        jnp.einsum("rhc,rpc->rhp", query_latent, kv_cache, preferred_element_type=F32)
        * SCORE_SCALE
    )
    allowed = (jnp.arange(kv_cache.shape[1], dtype=jnp.int32)[None, :] < cache_len[:, None])[
        :, None, :
    ]
    scores = jnp.where(allowed, scores, -1e30)
    highest = jnp.max(scores, axis=2, keepdims=True)
    lifted = jnp.where(allowed, jnp.exp(scores - highest), 0.0)
    totals = jnp.sum(lifted, axis=2, keepdims=True)
    mixed = jnp.einsum(
        "rhp,rpc->rhc",
        lifted.astype(BF),
        kv_cache[:, :, :KVL],
        preferred_element_type=F32,
    )
    return (mixed / totals).astype(BF)


def iota(shape, axis):
    return lax.broadcasted_iota(jnp.int32, shape, axis)


def flip(block):
    turned = jnp.transpose(block.astype(F32))
    return jnp.concatenate([turned, jnp.zeros((FT, GL - SLICE), F32)], axis=1).astype(BF)


def gate_up_body(g_ref, u_ref, o_ref):
    for e in range(g_ref.shape[0]):
        g = flip(g_ref[e])
        u = flip(u_ref[e])
        for x in range(NX):
            o_ref[x, e, 0:FX, :] = g[x * FX : (x + 1) * FX]
            o_ref[x, e, FX : 2 * FX, :] = u[x * FX : (x + 1) * FX]


def down_body(d_ref, o_ref):
    for e in range(d_ref.shape[0]):
        d = flip(d_ref[e])
        for x in range(NX):
            o_ref[x, e] = d[x * FX : (x + 1) * FX]


STEP_E = 5


def turn_gate_up(gate, up):
    spec = pl.BlockSpec((STEP_E, SLICE, FT), lambda i: (i, 0, 0))
    return pl.pallas_call(
        gate_up_body,
        grid=(NE // STEP_E,),
        in_specs=[spec, spec],
        out_specs=pl.BlockSpec((NX, STEP_E, 2 * FX, GL), lambda i: (0, i, 0, 0)),
        out_shape=jax.ShapeDtypeStruct((NX, NE, 2 * FX, GL), BF),
        name="turn_gate_up",
    )(gate, up)


def turn_down(down):
    return pl.pallas_call(
        down_body,
        grid=(NE // STEP_E,),
        in_specs=[pl.BlockSpec((STEP_E, SLICE, FT), lambda i: (i, 0, 0))],
        out_specs=pl.BlockSpec((NX, STEP_E, FX, GL), lambda i: (0, i, 0, 0)),
        out_shape=jax.ShapeDtypeStruct((NX, NE, FX, GL), BF),
        name="turn_down",
    )(down)


META = 96
HIGH, LOW, SQ = META + 8, META + 16, META + 24
PR = 4 * ZR
PB = PR + 16


def project_body(x_ref, w_ref, p_ref, id_ref, y_ref):
    meta = x_ref[:, 128:256]
    col = iota((128, TOP * 128), 1)
    pick = (iota((128, TOP * 128), 0) - META == col // 128).astype(F32).astype(BF)
    spread = jnp.dot(meta, pick, preferred_element_type=F32)
    half = (iota((1, TOP * 128), 1) % 128 // 64).astype(F32)
    id_ref[...] = (spread - half).astype(BF)
    for start in range(0, NE * 2 * FX, 256):
        size = min(256, NE * 2 * FX - start)
        total = None
        for k in range(NX):
            part = lax.dot_general(
                x_ref[:, k * GL : (k + 1) * GL],
                w_ref[k, start : start + size, :],
                (((1,), (1,)), ((), ())),
                preferred_element_type=F32,
            )
            total = part if total is None else total + part
        y_ref[:, start : start + size] = total.astype(BF)
    low_half = iota((16, 128), 1) < 64

    def body(s, carry):
        r = pl.multiple_of(s * 16, 16)
        z = s // 8
        rr = pl.multiple_of((s % 8) * 16, 16)
        ids = [id_ref[pl.ds(r, 16), j * 128 : (j + 1) * 128] for j in range(TOP)]
        kept = [jnp.zeros((16, 128), BF) for _ in range(TOP)]
        for tile in range(NE // 2):
            y = y_ref[pl.ds(r, 16), tile * 128 : (tile + 1) * 128]
            for j in range(TOP):
                kept[j] = jnp.where(ids[j] == jnp.asarray(2.0 * tile, BF), y, kept[j])
        for q in range(TOP // 2):
            a = kept[2 * q].astype(F32)
            b = kept[2 * q + 1].astype(F32)
            a = a + pltpu.roll(a, 64, 1)
            b = b + pltpu.roll(b, 64, 1)
            p_ref[z, pl.ds(q * ZR + rr, 16), :] = jnp.where(low_half, a, b).astype(BF)
        return carry

    lax.fori_loop(0, ROWS // 16, body, 0)
    for z in range(NZ):
        turned = jnp.transpose(x_ref[z * ZR : (z + 1) * ZR, 128:256].astype(F32))
        p_ref[z, PR:PB, :] = turned[112:128].astype(BF)


def project(rows, weights):
    return pl.pallas_call(
        project_body,
        out_shape=jax.ShapeDtypeStruct((NZ, PB, 128), BF),
        scratch_shapes=[
            pltpu.VMEM((ROWS, TOP * 128), BF),
            pltpu.VMEM((ROWS, NE * 2 * FX), BF),
        ],
        name="project",
    )(rows, weights)


def activate_body(p_ref, m_ref, o_ref):
    row = iota((128, 5 * 128), 0)
    col = iota((128, 5 * 128), 1)
    j = 2 * (col // 128) + (col % 128) // 64
    single = jnp.where(row == HIGH + j, 64.0, jnp.where(row == LOW + j, 1.0, 0.0))
    every = jnp.where(
        (row >= HIGH) & (row < LOW), 64.0, jnp.where((row >= LOW) & (row < SQ), 1.0, 0.0)
    )
    pick = jnp.where(col < 512, single, every).astype(BF)
    weights = jnp.dot(m_ref[...], pick, preferred_element_type=F32)
    scale = ROUTE_SCALE / weights[:, 512:640]
    squares = jnp.zeros((16, 128), F32)
    for z in range(NZ):
        squares = squares + p_ref[z, PR:PB, :].astype(F32)
    total = squares[8:9] + squares[9:10]
    inv = lax.rsqrt(total * (1.0 / DIM) + NORM_EPSILON)
    inv = jnp.transpose(jnp.broadcast_to(inv, (128, 128)))
    acts = []
    for q in range(TOP // 2):
        v = jnp.zeros((ZR, 128), F32)
        for z in range(NZ):
            v = v + p_ref[z, q * ZR : (q + 1) * ZR, :].astype(F32)
        v = v * inv
        u = pltpu.roll(v, 128 - FX, 1)
        gate = weights[:, q * 128 : (q + 1) * 128] * scale
        acts.append(v / (1.0 + jnp.exp(-v)) * u * gate)
    first = iota((ZR, 128), 1) % 64 < FX
    for q in range(2):
        packed = jnp.where(first, acts[2 * q], pltpu.roll(acts[2 * q + 1], FX, 1)).astype(BF)
        for z in range(NZ):
            o_ref[z, q * ZR : (q + 1) * ZR, :] = packed


def activate(parts, meta):
    return pl.pallas_call(
        activate_body,
        out_shape=jax.ShapeDtypeStruct((NZ, 2 * ZR, 128), BF),
        name="activate",
    )(parts, meta)


def combine_body(a_ref, x_ref, d_ref, o_ref, id_ref, wide_ref):
    meta = x_ref[:, 128:256]
    row = iota((128, TOP * 128), 0) - META
    col = iota((128, TOP * 128), 1)
    q = col // 512
    k = col // 128 % 4
    block = col % 128 // FX
    origin = (block - k + 4) % 4
    j = 4 * q + jnp.where(origin == 1, 2, jnp.where(origin == 2, 1, origin))
    spread = jnp.dot(meta, (row == j).astype(F32).astype(BF), preferred_element_type=F32)
    id_ref[...] = (spread - (iota((1, TOP * 128), 1) % 128 // FX).astype(F32)).astype(BF)

    def body(s, carry):
        r = pl.multiple_of(s * 16, 16)
        z = s // 8
        rr = pl.multiple_of((s % 8) * 16, 16)
        ids = [id_ref[pl.ds(r, 16), n * 128 : (n + 1) * 128] for n in range(TOP)]
        turned = []
        for n in range(2):
            a = a_ref[z, pl.ds(n * ZR + rr, 16), :].astype(F32)
            for shift in range(4):
                moved = a if shift == 0 else pltpu.roll(a, shift * FX, 1)
                turned.append(moved.astype(BF))
        for g in range(8):
            kept = jnp.zeros((16, 128), BF)
            for n in range(TOP):
                kept = jnp.where(ids[n] == jnp.asarray(4.0 * g, BF), turned[n], kept)
            wide_ref[pl.ds(r, 16), g * 128 : (g + 1) * 128] = kept
        return carry

    lax.fori_loop(0, ROWS // 16, body, 0)
    for x in range(NX):
        out = lax.dot_general(
            wide_ref[:, : NE * FX],
            d_ref[x],
            (((1,), (0,)), ((), ())),
            preferred_element_type=F32,
        )
        o_ref[:, x * SLICE : (x + 1) * SLICE] = out[:, :SLICE].astype(BF)


def combine(acts, rows, down):
    return pl.pallas_call(
        combine_body,
        out_shape=jax.ShapeDtypeStruct((ROWS, WIDE), BF),
        scratch_shapes=[
            pltpu.VMEM((ROWS, TOP * 128), BF),
            pltpu.VMEM((ROWS, 1024), BF),
        ],
        name="combine",
    )(acts, rows, down)


def pack_rows(hidden_in, norm_gain, expert_ids, route_weight, updated_list):
    named = updated_list[None, None, :] == expert_ids[:, :, None]
    entries = jnp.sum(
        jnp.where(named, jnp.arange(NE, dtype=jnp.int32)[None, None, :], 0), axis=2
    )
    widened = hidden_in.astype(F32)
    scaled = (widened * norm_gain.astype(F32)[None, :]).astype(BF)
    squares = jnp.sum(widened * widened, axis=1, keepdims=True)
    high = lax.reduce_precision(squares, 8, 7)
    meta = jnp.concatenate(
        [
            entries.astype(F32),
            (route_weight // 64).astype(F32),
            (route_weight % 64).astype(F32),
            high,
            squares - high,
            jnp.zeros((RB, GL - SLICE - 26), F32),
        ],
        axis=1,
    ).astype(BF)
    pad = jnp.zeros((RB, GL - SLICE), BF)
    pieces = []
    for k in range(NX):
        pieces += [scaled[:, k * SLICE : (k + 1) * SLICE], meta if k == 0 else pad]
    return jnp.concatenate(pieces, axis=1)


def gather_rows(packed):
    moved = swap_zt(packed)
    copies = [moved] + [
        lax.ppermute(
            moved,
            "expert",
            [(z * NX + x, z * NX + (x + s) % NX) for z in range(NZ) for x in range(NX)],
        )
        for s in range(1, NX)
    ]
    own = lax.axis_index("expert") % NX
    stacked = jnp.concatenate(copies, axis=0)
    order = (own - jnp.arange(NX, dtype=jnp.int32)) % NX
    ring = jnp.take(
        stacked.reshape(NX, RB, stacked.shape[1]), order, axis=0, mode="clip"
    ).reshape(ZR, stacked.shape[1])
    spread = exchange(jnp.broadcast_to(ring[None], (NT,) + ring.shape), "tensor")
    return spread.reshape(ROWS, spread.shape[2])


def per_device(
    query_latent,
    kv_cache,
    cache_len,
    value_up,
    hidden_in,
    norm_gain,
    expert_ids,
    route_weight,
    placement_plan,
    updated_list,
    learner_gate,
    learner_up,
    learner_down,
):
    turned = turn_gate_up(learner_gate, learner_up)
    held = exchange(turned.reshape(NX, NE * 2 * FX, GL), "expert", X_GROUPS)
    rows = gather_rows(pack_rows(hidden_in, norm_gain, expert_ids, route_weight, updated_list))
    held_down = exchange(
        turn_down(learner_down).reshape(NX, NE * FX, GL), "expert", X_GROUPS
    )
    parts = exchange(project(rows, held), "expert", Z_GROUPS)
    z = lax.axis_index("expert") // NX
    meta = lax.dynamic_slice(rows, (z * ZR, 128), (ZR, 128))
    acts = exchange(activate(parts, meta), "expert", Z_GROUPS)

    entry_range = jnp.arange(NE, dtype=jnp.int32)
    learner_entry = jnp.sum(
        entry_range[None, :] * (updated_list[None, :] == placement_plan[:, None]).astype(jnp.int32),
        axis=1,
    )
    chosen = jnp.take(learner_gate, learner_entry, axis=0, mode="clip")
    slot_gate = lax.all_to_all(chosen, "expert", split_axis=0, concat_axis=1, tiled=True)

    partial = combine(acts, rows, held_down)
    shared = exchange(partial.reshape(NT, ZR, WIDE), "tensor")
    summed = jnp.sum(shared.astype(F32), axis=0).astype(BF)
    crossed = exchange(summed.reshape(NX, RB, WIDE), "expert", X_GROUPS)
    moe_out = swap_zt(jnp.sum(crossed.astype(F32), axis=0).astype(BF))

    latent = attend(query_latent, kv_cache, cache_len)
    head_rows = lax.all_to_all(latent, "tensor", split_axis=1, concat_axis=0, tiled=True)
    projected = jnp.einsum("rhc,hcv->rhv", head_rows, value_up, preferred_element_type=F32)
    attn_values = projected.astype(BF).reshape(
        head_rows.shape[0], projected.shape[1] * projected.shape[2]
    )
    return (attn_values, moe_out, slot_gate)


def solution(mesh):
    in_specs = (
        P(("expert", "tensor"), None, None),
        P(("expert", "tensor"), None, None),
        P(("expert", "tensor")),
        P("tensor", None, None),
        P("expert", "tensor"),
        P("tensor"),
        P("expert", None),
        P("expert", None),
        P(),
        P(),
        P(None, "expert", "tensor"),
        P(None, "expert", "tensor"),
        P(None, "expert", "tensor"),
    )
    out_specs = (P("expert", "tensor"), P("expert", "tensor"), P("expert", None, "tensor"))
    return jax.shard_map(
        per_device, mesh=mesh, in_specs=in_specs, out_specs=out_specs, check_vma=False
    )
```

time: 595 us -> 332 us (0.56)
  blocking collectives: 279 us -> 72.8 us
  local copies, waits for them, and re-layouts: 71.8 us -> 10.8 us
  Pallas kernels: 0 us -> 45.2 us
  matrix products: 26.5 us -> 6.23 us
  waiting for transfers between devices: 150 us -> 134 us
  starting transfers between devices: 38.2 us -> 52.1 us
  between operations: 14.5 us -> 0.86 us
    all_to_all x1 -> x2, blocking collectives: 252 us -> 72.8 us  [exchange(): lax.all_to_all(value, axis, split_axis=0, concat_axis=0, tiled=True, axis...]
    unnamed x2 -> x0, waiting for transfers between devices: 46.4 us -> none
    pallas_call x0 -> x5, Pallas kernels: none -> 45.2 us  [the longest x1 18 us: project(): pl.pallas_call(project_body, out_shape=jax.ShapeDtypeStruct((NZ, PB, 128)...]
    all_gather x2 -> x0, blocking collectives: 26.9 us -> none  [the longest x1 13.6 us: per_device(): lax.all_gather(hidden_in, 'tensor', axis=1, tiled=True)]
    all_to_all x4 -> x0, local copies, waits for them, and re-layouts: 22.5 us -> none  [the longest x2 20.9 us: per_device(): lax.all_to_all(outbound, 'expert', split_axis=0, concat_axis=0, tiled=True)]
    all_to_all x4 -> x6, waiting for transfers between devices: 104 us -> 126 us  [the longest x5 84.5 us: exchange(): lax.all_to_all(value, axis, split_axis=0, concat_axis=0, tiled=True, axis...]
    scatter x1 -> x0, local copies, waits for them, and re-layouts: 20.7 us -> none  [per_device(): outbound = jnp.zeros((slot_total * capacity, normed.shape[1]), jnp.bfloat...]
    dot_general x6 -> x2, matrix products: 23.5 us -> 3.23 us  [the longest x1 2.97 us: attend(): jnp.einsum('rhp,rpc->rhc', lifted.astype(BF), kv_cache[:, :, :KVL], prefe...]
  transfers between devices with their start and end apart: 6 -> 12, of which waited for: 4 -> 9; matrix products, arithmetic and copies ran while one was open for 7% -> 5% of each run, Pallas kernels for 0% -> 4%
where the time goes in v1:
time: 332 us; the launch traced here: 329 us
  waiting for transfers between devices  134 us (40%)
  blocking collectives  72.8 us (22%)
  starting transfers between devices  52.1 us (16%)
  Pallas kernels  45.2 us (14%)
  local copies, waits for them, and re-layouts  10.8 us (3%)
  other arithmetic  6.98 us (2%)
  matrix products  6.23 us (2%)
    all_to_all x5, waiting for transfers between devices, exchange(): lax.all_to_all(value, axis, split_axis=0, concat_axis=0, tiled=True, axis...  84.5 us
    all_to_all x2, blocking collectives, exchange(): lax.all_to_all(value, axis, split_axis=0, concat_axis=0, tiled=True, axis...  72.8 us
    all_to_all x1, waiting for transfers between devices, per_device(): lax.all_to_all(chosen, 'expert', split_axis=0, concat_axis=1, tiled=True)  41.1 us
    all_to_all x5, starting transfers between devices, exchange(): lax.all_to_all(value, axis, split_axis=0, concat_axis=0, tiled=True, axis...  37.5 us
    pallas_call x1, Pallas kernels, project(): pl.pallas_call(project_body, out_shape=jax.ShapeDtypeStruct((NZ, PB, 128)...  18 us
    pallas_call x1, Pallas kernels, combine(): pl.pallas_call(combine_body, out_shape=jax.ShapeDtypeStruct((ROWS, WIDE),...  13.7 us
  transfers between devices with their start and end apart: 12, of which 9 were waited for; matrix products, arithmetic and copies ran while one was open for 5% of the time, Pallas kernels for 4%

profile of v1, /device:TPU:2, one launch (start us, length us, event | category | flops | bytes accessed | tf_op | source)
XLA Modules:
  0.0 329.4 jit_solution(10332804647708857488)
XLA Ops:
  5.3 1.6 collective-permute-start.1
  6.9 2.8 collective-permute-start.2
  10.1 2.5 collective-permute-done.2
  12.6 1.3 collective-permute-done.3
  14.5 1.6 broadcast_in_dim.70
  16.1 15.3 %all-to-all-start.1 = ((bf16[8,128,1024]{2,1,0:T(8,128)(2,1)}), bf16[8,128,1024]{2,1,0:T(8,128)(2,1)S(1)}, u32[]{:S(2)}, u32[]{:S(2)}) async-start(bf16[8,128,1024]{2,1,0:T(8,128)(2,1)} %broadcast_in_dim.70), calls=%async_computation.1 | async-start | bytes 4194304 | tf_op jit(solution)/shard_map/all_to_all | solution.py:43
  31.4 6.0 %turn_gate_up.1 = bf16[4,30,64,256]{3,2,1,0:T(8,128)(2,1)} custom-call(bf16[30,224,128]{2,1,0:T(8,128)(2,1)} %g_ref.1, bf16[30,224,128]{2,1,0:T(8,128)(2,1)} %u_ref.1), custom_call_target="tpu_custom_call" | custom-call | tf_op jit(solution)/shard_map/turn_gate_up/pallas_call | solution.py:99
  37.5 21.1 %all-to-all-done.1 = bf16[8,128,1024]{2,1,0:T(8,128)(2,1)S(1)} async-done(((bf16[8,128,1024]{2,1,0:T(8,128)(2,1)}), bf16[8,128,1024]{2,1,0:T(8,128)(2,1)S(1)}, u32[]{:S(2)}, u32[]{:S(2)}) %all-to-all-start.1) | async-done | bytes 2097184 | tf_op jit(solution)/shard_map/all_to_all | solution.py:43
  58.6 51.5 %all_to_all.65.w_ref = bf16[4,1920,256]{2,1,0:T(8,128)(2,1)} all-to-all(bf16[4,1920,256]{2,1,0:T(8,128)(2,1)} %bitcast.33), channel_id=1, replica_groups={{0,8,16,24},{32,40,48,56},{64,72,80,88},{96,104,112,120},{128,136,144,1..., dimensions={0} | all-to-all | bytes 7864320 | tf_op jit(solution)/shard_map/all_to_all | solution.py:43
  110.2 18.0 %project.1 = bf16[8,528,128]{2,1,0:T(8,128)(2,1)} custom-call(bf16[1024,1024]{1,0:T(8,128)(2,1)} %bitcast.30, bf16[4,1920,256]{2,1,0:T(8,128)(2,1)} %all_to_all.65.w_ref), custom_call_target="tpu_custom_call" | custom-call | tf_op jit(solution)/shard_map/project/pallas_call | solution.py:172
  128.2 7.7 %all-to-all-start.3 = ((bf16[8,528,128]{2,1,0:T(8,128)(2,1)}), bf16[8,528,128]{2,1,0:T(8,128)(2,1)S(1)}, u32[]{:S(2)}, u32[]{:S(2)}) async-start(bf16[8,528,128]{2,1,0:T(8,128)(2,1)} %project.1), calls=%async_computation.3 | async-start | bytes 2162688 | tf_op jit(solution)/shard_map/all_to_all | solution.py:43
  135.9 5.0 %turn_down.1 = bf16[4,30,32,256]{3,2,1,0:T(8,128)(2,1)} custom-call(bf16[30,224,128]{2,1,0:T(8,128)(2,1)} %d_ref.1), custom_call_target="tpu_custom_call" | custom-call | tf_op jit(solution)/shard_map/turn_down/pallas_call | solution.py:110
  140.9 23.2 %all-to-all-done.3.p_ref = bf16[8,528,128]{2,1,0:T(8,128)(2,1)S(1)} async-done(((bf16[8,528,128]{2,1,0:T(8,128)(2,1)}), bf16[8,528,128]{2,1,0:T(8,128)(2,1)S(1)}, u32[]{:S(2)}, u32[]{:S(2)}) %all-to-all-start.3) | async-done | bytes 1081376 | tf_op jit(solution)/shard_map/all_to_all | solution.py:43
  165.1 5.0 %all-to-all-start.5 = ((bf16[4,960,256]{2,1,0:T(8,128)(2,1)}), bf16[4,960,256]{2,1,0:T(8,128)(2,1)S(1)}, u32[]{:S(2)}, u32[]{:S(2)}) async-start(bf16[4,960,256]{2,1,0:T(8,128)(2,1)} %bitcast.34), calls=%async_computation.5 | async-start | bytes 3932160 | tf_op jit(solution)/shard_map/all_to_all | solution.py:43
  170.1 1.4 constant_dynamic-slice_fusion.m_ref
  171.5 2.4 activate.1
  173.9 20.1 %all-to-all-done.5.d_ref = bf16[4,960,256]{2,1,0:T(8,128)(2,1)S(1)} async-done(((bf16[4,960,256]{2,1,0:T(8,128)(2,1)}), bf16[4,960,256]{2,1,0:T(8,128)(2,1)S(1)}, u32[]{:S(2)}, u32[]{:S(2)}) %all-to-all-start.5) | async-done | bytes 1966112 | tf_op jit(solution)/shard_map/all_to_all | solution.py:43
  194.1 21.2 %all_to_all.66.a_ref = bf16[8,256,128]{2,1,0:T(8,128)(2,1)} all-to-all(bf16[8,256,128]{2,1,0:T(8,128)(2,1)} %activate.1), channel_id=1, replica_groups={{0,32,64,96,128,160,192,224},{8,40,72,104,136,168,200,232},{16,48,80,11..., dimensions={0} | all-to-all | bytes 1048576 | tf_op jit(solution)/shard_map/all_to_all | solution.py:43
  215.3 13.7 %combine.1 = bf16[1024,896]{1,0:T(8,128)(2,1)} custom-call(bf16[8,256,128]{2,1,0:T(8,128)(2,1)} %all_to_all.66.a_ref, bf16[1024,1024]{1,0:T(8,128)(2,1)} %bitcast.32, bf16[4,960,256]{2,1,0:T(8,128)(2,1)} %copy-done.2), custom_call_target="tpu_custom_call" | custom-call | tf_op jit(solution)/shard_map/combine/pallas_call | solution.py:266
  229.0 4.6 %all-to-all-start.6 = ((bf16[8,128,896]{2,1,0:T(8,128)(2,1)}), bf16[8,128,896]{2,1,0:T(8,128)(2,1)}, u32[]{:S(2)}, u32[]{:S(2)}) async-start(bf16[8,128,896]{2,1,0:T(8,128)(2,1)} %bitcast.36), calls=%async_computation.6 | async-start | bytes 3670016 | tf_op jit(solution)/shard_map/all_to_all | solution.py:43
  233.7 3.0 fusion.27
  236.7 3.0 fusion.10
  240.7 17.2 %all-to-all-done.6 = bf16[8,128,896]{2,1,0:T(8,128)(2,1)} async-done(((bf16[8,128,896]{2,1,0:T(8,128)(2,1)}), bf16[8,128,896]{2,1,0:T(8,128)(2,1)}, u32[]{:S(2)}, u32[]{:S(2)}) %all-to-all-start.6) | async-done | bytes 1835040 | tf_op jit(solution)/shard_map/all_to_all | solution.py:43
  257.8 3.4 %all-to-all-start = ((bf16[4,64,512]{2,0,1:T(4,128)(2,1)}), bf16[4,64,512]{2,0,1:T(4,128)(2,1)S(1)}, u32[]{:S(2)}, u32[]{:S(2)}) async-start(bf16[4,64,512]{2,0,1:T(4,128)(2,1)} %copy.41), calls=%async_computation | async-start | bytes 524288 | tf_op jit(solution)/shard_map/all_to_all | solution.py:365
  261.2 2.5 reduce_sum.66
  263.7 4.9 %all-to-all-done = bf16[4,64,512]{2,0,1:T(4,128)(2,1)S(1)} async-done(((bf16[4,64,512]{2,0,1:T(4,128)(2,1)}), bf16[4,64,512]{2,0,1:T(4,128)(2,1)S(1)}, u32[]{:S(2)}, u32[]{:S(2)}) %all-to-all-start) | async-done | bytes 262176 | tf_op jit(solution)/shard_map/all_to_all | solution.py:365
  268.7 4.8 %all-to-all-start.7 = ((bf16[4,32,896]{2,1,0:T(8,128)(2,1)}), bf16[4,32,896]{2,1,0:T(8,128)(2,1)S(1)}, u32[]{:S(2)}, u32[]{:S(2)}) async-start(bf16[4,32,896]{2,1,0:T(8,128)(2,1)} %bitcast.11), calls=%async_computation.7 | async-start | bytes 458752 | tf_op jit(solution)/shard_map/all_to_all | solution.py:43
  273.7 2.0 gather_fusion.1
  275.7 2.8 all-to-all-done.7
  278.5 5.1 %all-to-all-start.8 = ((bf16[32,224,128]{2,1,0:T(8,128)(2,1)}), bf16[32,224,128]{2,1,0:T(8,128)(2,1)S(1)}, u32[]{:S(2)}, u32[]{:S(2)}) async-start(bf16[32,224,128]{2,1,0:T(8,128)(2,1)} %gather_fusion.1), calls=%async_computation.8 | async-start | bytes 3670016 | tf_op jit(solution)/shard_map/all_to_all | solution.py:356
  286.4 41.1 %all-to-all-done.8 = bf16[32,224,128]{2,1,0:T(8,128)(2,1)S(1)} async-done(((bf16[32,224,128]{2,1,0:T(8,128)(2,1)}), bf16[32,224,128]{2,1,0:T(8,128)(2,1)S(1)}, u32[]{:S(2)}, u32[]{:S(2)}) %all-to-all-start.8) | async-done | bytes 1835040 | tf_op jit(solution)/shard_map/all_to_all | solution.py:356
  328.1 1.2 copy.58
  (55 shorter events, 11.2 us)
Async XLA Ops:
  0.6 284.8 %copy-start = (bf16[8,512,128]{2,1,0:T(8,128)(2,1)S(1)}, bf16[8,512,128]{2,1,0:T(8,128)(2,1)}, u32[]{:S(2)}) copy-start(bf16[8,512,128]{2,1,0:T(8,128)(2,1)} %param.16) | copy-start | bytes 3145732
  4.6 0.7 collective-permute-start
  5.3 4.8 %collective-permute-start.1 = (bf16[32,1024]{1,0:T(8,128)(2,1)S(1)}, bf16[32,1024]{1,0:T(8,128)(2,1)S(1)}, u32[]{:S(2)}, u32[]{:S(2)}) collective-permute-start(bf16[32,1024]{1,0:T(8,128)(2,1)S(1)} %collective-permute-done), channel_id=1, source_target_pairs={{0,8},{8,16},{16,24},{24,0},{32,40},{40,48},{48,56},{56,32},{64,72... | collective-permute-start | bytes 196616 | tf_op jit(solution)/shard_map/ppermute | solution.py:307
  6.9 5.8 %collective-permute-start.2 = (bf16[32,1024]{1,0:T(8,128)(2,1)S(1)}, bf16[32,1024]{1,0:T(8,128)(2,1)S(1)}, u32[]{:S(2)}, u32[]{:S(2)}) collective-permute-start(bf16[32,1024]{1,0:T(8,128)(2,1)S(1)} %collective-permute-done), channel_id=1, source_target_pairs={{0,16},{8,24},{16,0},{24,8},{32,48},{40,56},{48,32},{56,40},{64,80... | collective-permute-start | bytes 196616 | tf_op jit(solution)/shard_map/ppermute | solution.py:307
  9.7 4.3 %collective-permute-start.3 = (bf16[32,1024]{1,0:T(8,128)(2,1)S(1)}, bf16[32,1024]{1,0:T(8,128)(2,1)S(1)}, u32[]{:S(2)}, u32[]{:S(2)}) collective-permute-start(bf16[32,1024]{1,0:T(8,128)(2,1)S(1)} %collective-permute-done), channel_id=1, source_target_pairs={{0,24},{8,0},{16,8},{24,16},{32,56},{40,32},{48,40},{56,48},{64,88... | collective-permute-start | bytes 196616 | tf_op jit(solution)/shard_map/ppermute | solution.py:307
  16.1 42.5 %all-to-all-start.1 = ((bf16[8,128,1024]{2,1,0:T(8,128)(2,1)}), bf16[8,128,1024]{2,1,0:T(8,128)(2,1)S(1)}, u32[]{:S(2)}, u32[]{:S(2)}) async-start(bf16[8,128,1024]{2,1,0:T(8,128)(2,1)} %broadcast_in_dim.70), calls=%async_computation.1 | async-start | bytes 4194304 | tf_op jit(solution)/shard_map/all_to_all | solution.py:43
  58.6 51.5 %copy-start.1 = (bf16[8,128,1024]{2,1,0:T(8,128)(2,1)}, bf16[8,128,1024]{2,1,0:T(8,128)(2,1)S(1)}, u32[]{:S(2)}) copy-start(bf16[8,128,1024]{2,1,0:T(8,128)(2,1)S(1)} %all-to-all-done.1) | copy-start | bytes 6291460
  128.2 36.0 %all-to-all-start.3 = ((bf16[8,528,128]{2,1,0:T(8,128)(2,1)}), bf16[8,528,128]{2,1,0:T(8,128)(2,1)S(1)}, u32[]{:S(2)}, u32[]{:S(2)}) async-start(bf16[8,528,128]{2,1,0:T(8,128)(2,1)} %project.1), calls=%async_computation.3 | async-start | bytes 2162688 | tf_op jit(solution)/shard_map/all_to_all | solution.py:43
  164.1 1.0 copy-start.4
  165.1 29.0 %all-to-all-start.5 = ((bf16[4,960,256]{2,1,0:T(8,128)(2,1)}), bf16[4,960,256]{2,1,0:T(8,128)(2,1)S(1)}, u32[]{:S(2)}, u32[]{:S(2)}) async-start(bf16[4,960,256]{2,1,0:T(8,128)(2,1)} %bitcast.34), calls=%async_computation.5 | async-start | bytes 3932160 | tf_op jit(solution)/shard_map/all_to_all | solution.py:43
  194.1 21.2 %copy-start.2 = (bf16[4,960,256]{2,1,0:T(8,128)(2,1)}, bf16[4,960,256]{2,1,0:T(8,128)(2,1)S(1)}, u32[]{:S(2)}) copy-start(bf16[4,960,256]{2,1,0:T(8,128)(2,1)S(1)} %all-to-all-done.5.d_ref) | copy-start | bytes 5898244
  229.0 4.7 %copy-start.6 = (s32[4]{0:T(128)S(1)}, s32[4]{0:T(128)}, u32[]{:S(2)}) copy-start(s32[4]{0:T(128)} %param.15) | copy-start | bytes 52
  229.0 4.7 %copy-start.8 = (bf16[4,64,576]{2,1,0:T(8,128)(2,1)S(1)}, bf16[4,64,576]{2,1,0:T(8,128)(2,1)}, u32[]{:S(2)}) copy-start(bf16[4,64,576]{2,1,0:T(8,128)(2,1)} %param.13) | copy-start | bytes 884740
  229.0 28.8 %all-to-all-start.6 = ((bf16[8,128,896]{2,1,0:T(8,128)(2,1)}), bf16[8,128,896]{2,1,0:T(8,128)(2,1)}, u32[]{:S(2)}, u32[]{:S(2)}) async-start(bf16[8,128,896]{2,1,0:T(8,128)(2,1)} %bitcast.36), calls=%async_computation.6 | async-start | bytes 3670016 | tf_op jit(solution)/shard_map/all_to_all | solution.py:43
  239.7 33.8 %copy-start.7 = (s32[30]{0:T(128)S(1)}, s32[30]{0:T(128)}, u32[]{:S(2)}) copy-start(s32[30]{0:T(128)} %param.22) | copy-start | bytes 364
  239.7 33.8 %copy-start.9 = (s32[32]{0:T(128)S(1)}, s32[32]{0:T(128)}, u32[]{:S(2)}) copy-start(s32[32]{0:T(128)} %param.21) | copy-start | bytes 388
  239.7 34.0 %copy-start.3 = (bf16[30,224,128]{2,1,0:T(8,128)(2,1)S(1)}, bf16[30,224,128]{2,1,0:T(8,128)(2,1)}, u32[]{:S(2)}) copy-start(bf16[30,224,128]{2,1,0:T(8,128)(2,1)} %g_ref.1) | copy-start | bytes 5160964
  257.8 10.8 %all-to-all-start = ((bf16[4,64,512]{2,0,1:T(4,128)(2,1)}), bf16[4,64,512]{2,0,1:T(4,128)(2,1)S(1)}, u32[]{:S(2)}, u32[]{:S(2)}) async-start(bf16[4,64,512]{2,0,1:T(4,128)(2,1)} %copy.41), calls=%async_computation | async-start | bytes 524288 | tf_op jit(solution)/shard_map/all_to_all | solution.py:365
  268.7 9.9 %all-to-all-start.7 = ((bf16[4,32,896]{2,1,0:T(8,128)(2,1)}), bf16[4,32,896]{2,1,0:T(8,128)(2,1)S(1)}, u32[]{:S(2)}, u32[]{:S(2)}) async-start(bf16[4,32,896]{2,1,0:T(8,128)(2,1)} %bitcast.11), calls=%async_computation.7 | async-start | bytes 458752 | tf_op jit(solution)/shard_map/all_to_all | solution.py:43
  278.5 5.1 %copy-start.5 = (bf16[4,32,896]{2,1,0:T(8,128)(2,1)}, bf16[4,32,896]{2,1,0:T(8,128)(2,1)S(1)}, u32[]{:S(2)}) copy-start(bf16[4,32,896]{2,1,0:T(8,128)(2,1)S(1)} %all-to-all-done.7) | copy-start | bytes 688132
  278.5 49.0 %all-to-all-start.8 = ((bf16[32,224,128]{2,1,0:T(8,128)(2,1)}), bf16[32,224,128]{2,1,0:T(8,128)(2,1)S(1)}, u32[]{:S(2)}, u32[]{:S(2)}) async-start(bf16[32,224,128]{2,1,0:T(8,128)(2,1)} %gather_fusion.1), calls=%async_computation.8 | async-start | bytes 3670016 | tf_op jit(solution)/shard_map/all_to_all | solution.py:356
  284.8 42.7 %collective-permute-start.4 = (bf16[32,896]{1,0:T(8,128)(2,1)S(1)}, bf16[32,896]{1,0:T(8,128)(2,1)S(1)}, u32[]{:S(2)}, u32[]{:S(2)}) collective-permute-start(bf16[32,896]{1,0:T(8,128)(2,1)S(1)} %reduce_sum.67), channel_id=1, source_target_pairs={{0,0},{1,32},{2,64},{3,96},{4,128},{5,160},{6,192},{7,224},{8,8},{... | collective-permute-start | bytes 172040 | tf_op jit(solution)/shard_map/ppermute | solution.py:39

commit v2 on v1

--- a/solution.py
+++ b/solution.py
@@ -5,12 +5,13 @@
 from jax.experimental.pallas import tpu as pltpu
 from jax.sharding import PartitionSpec as P
 
+
 KVL = 512
 SCORE_SCALE = 192.0 ** (-0.5)
 ROUTE_SCALE = 2.5
 NORM_EPSILON = 1e-06
 
-NZ, NX, NT = 8, 4, 8
+NZ, NX, NT, NY = 8, 4, 8, 4
 RB = 32
 ZR = NX * RB
 ROWS = NZ * ZR
@@ -39,10 +40,24 @@
     return lax.ppermute(value, ("expert", "tensor"), SWAP)
 
 
-def exchange(value, axis, groups=None):
+def exchange(value, groups):
     return lax.all_to_all(
-        value, axis, split_axis=0, concat_axis=0, tiled=True, axis_index_groups=groups
-    )
+        value, "expert", split_axis=0, concat_axis=0, tiled=True, axis_index_groups=groups
+    )
+
+
+def shift_x(value, step):
+    pairs = [(z * NX + x, z * NX + (x + step) % NX) for z in range(NZ) for x in range(NX)]
+    return lax.ppermute(value, "expert", pairs)
+
+
+def shift_y(value, step):
+    pairs = [(y * 2 + c, (y + step) % NY * 2 + c) for y in range(NY) for c in range(2)]
+    return lax.ppermute(value, "tensor", pairs)
+
+
+def other_core(value):
+    return lax.ppermute(value, "tensor", [(t, t ^ 1) for t in range(NT)])
 
 
 def attend(query_latent, kv_cache, cache_len):
@@ -102,6 +117,7 @@
         in_specs=[spec, spec],
         out_specs=pl.BlockSpec((NX, STEP_E, 2 * FX, GL), lambda i: (0, i, 0, 0)),
         out_shape=jax.ShapeDtypeStruct((NX, NE, 2 * FX, GL), BF),
+        compiler_params=pltpu.CompilerParams(vmem_limit_bytes=16 << 20),
         name="turn_gate_up",
     )(gate, up)
 
@@ -113,6 +129,7 @@
         in_specs=[pl.BlockSpec((STEP_E, SLICE, FT), lambda i: (i, 0, 0))],
         out_specs=pl.BlockSpec((NX, STEP_E, FX, GL), lambda i: (0, i, 0, 0)),
         out_shape=jax.ShapeDtypeStruct((NX, NE, FX, GL), BF),
+        compiler_params=pltpu.CompilerParams(vmem_limit_bytes=16 << 20),
         name="turn_down",
     )(down)
 
@@ -123,8 +140,9 @@
 PB = PR + 16
 
 
-def project_body(x_ref, w_ref, p_ref, id_ref, y_ref):
-    meta = x_ref[:, 128:256]
+def project_body(z_ref, *refs):
+    x_refs, (w_ref, p_ref, id_ref, y_ref) = refs[:NZ], refs[NZ:]
+    meta = jnp.concatenate([x[:, 128:256] for x in x_refs], axis=0)
     col = iota((128, TOP * 128), 1)
     pick = (iota((128, TOP * 128), 0) - META == col // 128).astype(F32).astype(BF)
     spread = jnp.dot(meta, pick, preferred_element_type=F32)
@@ -135,7 +153,7 @@
         total = None
         for k in range(NX):
             part = lax.dot_general(
-                x_ref[:, k * GL : (k + 1) * GL],
+                jnp.concatenate([x[:, k * GL : (k + 1) * GL] for x in x_refs], axis=0),
                 w_ref[k, start : start + size, :],
                 (((1,), (1,)), ((), ())),
                 preferred_element_type=F32,
@@ -146,7 +164,7 @@
 
     def body(s, carry):
         r = pl.multiple_of(s * 16, 16)
-        z = s // 8
+        z = z_ref[s // 8]
         rr = pl.multiple_of((s % 8) * 16, 16)
         ids = [id_ref[pl.ds(r, 16), j * 128 : (j + 1) * 128] for j in range(TOP)]
         kept = [jnp.zeros((16, 128), BF) for _ in range(TOP)]
@@ -163,21 +181,27 @@
         return carry
 
     lax.fori_loop(0, ROWS // 16, body, 0)
-    for z in range(NZ):
-        turned = jnp.transpose(x_ref[z * ZR : (z + 1) * ZR, 128:256].astype(F32))
-        p_ref[z, PR:PB, :] = turned[112:128].astype(BF)
-
-
-def project(rows, weights):
+    for n in range(NZ):
+        turned = jnp.transpose(x_refs[n][:, 128:256].astype(F32))
+        p_ref[z_ref[n], PR:PB, :] = turned[112:128].astype(BF)
+
+
+SMEM = pl.BlockSpec(memory_space=pltpu.SMEM)
+VMEM = pl.BlockSpec(memory_space=pltpu.VMEM)
+
+
+def project(blocks, rows, weights):
     return pl.pallas_call(
         project_body,
+        in_specs=[SMEM] + [VMEM] * (NZ + 1),
         out_shape=jax.ShapeDtypeStruct((NZ, PB, 128), BF),
         scratch_shapes=[
             pltpu.VMEM((ROWS, TOP * 128), BF),
             pltpu.VMEM((ROWS, NE * 2 * FX), BF),
         ],
+        compiler_params=pltpu.CompilerParams(vmem_limit_bytes=32 << 20),
         name="project",
-    )(rows, weights)
+    )(blocks, *rows, weights)
 
 
 def activate_body(p_ref, m_ref, o_ref):
@@ -217,12 +241,17 @@
     return pl.pallas_call(
         activate_body,
         out_shape=jax.ShapeDtypeStruct((NZ, 2 * ZR, 128), BF),
+        compiler_params=pltpu.CompilerParams(vmem_limit_bytes=12 << 20),
         name="activate",
     )(parts, meta)
 
 
-def combine_body(a_ref, x_ref, d_ref, o_ref, id_ref, wide_ref):
-    meta = x_ref[:, 128:256]
+def combine_body(z_ref, a_ref, *refs):
+    x_refs, d_refs = refs[:NZ], refs[NZ : NZ + NX]
+    near_ref, far_ref, id_ref, wide_ref, d_ref = refs[NZ + NX :]
+    for s in range(NX):
+        d_ref[(z_ref[NZ] + NX - s) % NX] = d_refs[s][...]
+    meta = jnp.concatenate([x[:, 128:256] for x in x_refs], axis=0)
     row = iota((128, TOP * 128), 0) - META
     col = iota((128, TOP * 128), 1)
     q = col // 512
@@ -235,7 +264,7 @@
 
     def body(s, carry):
         r = pl.multiple_of(s * 16, 16)
-        z = s // 8
+        z = z_ref[s // 8]
         rr = pl.multiple_of((s % 8) * 16, 16)
         ids = [id_ref[pl.ds(r, 16), n * 128 : (n + 1) * 128] for n in range(TOP)]
         turned = []
@@ -259,19 +288,25 @@
             (((1,), (0,)), ((), ())),
             preferred_element_type=F32,
         )
-        o_ref[:, x * SLICE : (x + 1) * SLICE] = out[:, :SLICE].astype(BF)
-
-
-def combine(acts, rows, down):
+        out = out[:, :SLICE].astype(BF)
+        near_ref[:, x * SLICE : (x + 1) * SLICE] = out[: ROWS // 2]
+        far_ref[:, x * SLICE : (x + 1) * SLICE] = out[ROWS // 2 :]
+
+
+def combine(blocks, acts, rows, down):
     return pl.pallas_call(
         combine_body,
-        out_shape=jax.ShapeDtypeStruct((ROWS, WIDE), BF),
+        in_specs=[SMEM] + [VMEM] * (NZ + 1 + NX),
+        out_specs=[VMEM] * 2,
+        out_shape=[jax.ShapeDtypeStruct((ROWS // 2, WIDE), BF)] * 2,
         scratch_shapes=[
             pltpu.VMEM((ROWS, TOP * 128), BF),
             pltpu.VMEM((ROWS, 1024), BF),
+            pltpu.VMEM((NX, NE * FX, GL), BF),
         ],
+        compiler_params=pltpu.CompilerParams(vmem_limit_bytes=28 << 20),
         name="combine",
-    )(acts, rows, down)
+    )(blocks, acts, *rows, *down)
 
 
 def pack_rows(hidden_in, norm_gain, expert_ids, route_weight, updated_list):
@@ -303,25 +338,49 @@
 
 def gather_rows(packed):
     moved = swap_zt(packed)
-    copies = [moved] + [
-        lax.ppermute(
-            moved,
-            "expert",
-            [(z * NX + x, z * NX + (x + s) % NX) for z in range(NZ) for x in range(NX)],
-        )
-        for s in range(1, NX)
+    ring = jnp.concatenate([moved] + [shift_x(moved, s) for s in range(1, NX)], axis=0)
+    mine = [ring] + [shift_y(ring, s) for s in range(1, NY)]
+    return mine + [other_core(block) for block in mine]
+
+
+def block_places():
+    t = lax.axis_index("tensor")
+    y, c = t // 2, t % 2
+    s = jnp.arange(NY, dtype=jnp.int32)
+    turn = (y - s) % NY * 2
+    blocks = jnp.concatenate([turn + c, turn + 1 - c]).astype(jnp.int32)
+    zs = jnp.arange(NZ, dtype=jnp.int32)
+    places = (y - zs // 2) % NY + NY * (zs % 2 != c).astype(jnp.int32)
+    return blocks, places.astype(jnp.int32)
+
+
+def swap_down(down):
+    own = lax.axis_index("expert") % NX
+    mine = [
+        lax.dynamic_index_in_dim(down, (own + s) % NX, 0, keepdims=False) for s in range(NX)
     ]
-    own = lax.axis_index("expert") % NX
-    stacked = jnp.concatenate(copies, axis=0)
-    order = (own - jnp.arange(NX, dtype=jnp.int32)) % NX
-    ring = jnp.take(
-        stacked.reshape(NX, RB, stacked.shape[1]), order, axis=0, mode="clip"
-    ).reshape(ZR, stacked.shape[1])
-    spread = exchange(jnp.broadcast_to(ring[None], (NT,) + ring.shape), "tensor")
-    return spread.reshape(ROWS, spread.shape[2])
-
-
-def per_device(
+    return mine[:1] + [shift_x(mine[s], s) for s in range(1, NX)]
+
+
+def add(values):
+    total = values[0].astype(F32)
+    for value in values[1:]:
+        total = total + value.astype(F32)
+    return total.astype(BF)
+
+
+def gather_out(near, far):
+    size = near.shape[0] // NY
+    blocks = [
+        add([near[s * size : (s + 1) * size], far[s * size : (s + 1) * size]]) for s in range(NY)
+    ]
+    came = [blocks[0]] + [shift_y(blocks[s], NY - s) for s in range(1, NY)]
+    pieces = [add([b[s * RB : (s + 1) * RB] for b in came]) for s in range(NX)]
+    came = [pieces[0]] + [shift_x(pieces[s], NX - s) for s in range(1, NX)]
+    return swap_zt(add(came))
+
+
+def device_body(
     query_latent,
     kv_cache,
     cache_len,
@@ -337,15 +396,17 @@
     learner_down,
 ):
     turned = turn_gate_up(learner_gate, learner_up)
-    held = exchange(turned.reshape(NX, NE * 2 * FX, GL), "expert", X_GROUPS)
+    held = exchange(turned.reshape(NX, NE * 2 * FX, GL), X_GROUPS)
     rows = gather_rows(pack_rows(hidden_in, norm_gain, expert_ids, route_weight, updated_list))
-    held_down = exchange(
-        turn_down(learner_down).reshape(NX, NE * FX, GL), "expert", X_GROUPS
-    )
-    parts = exchange(project(rows, held), "expert", Z_GROUPS)
+    blocks, places = block_places()
+    down = turn_down(learner_down).reshape(NX, NE * FX, GL)
+    held_down = swap_down(down)
+    parts = exchange(project(blocks, rows, held), Z_GROUPS)
     z = lax.axis_index("expert") // NX
-    meta = lax.dynamic_slice(rows, (z * ZR, 128), (ZR, 128))
-    acts = exchange(activate(parts, meta), "expert", Z_GROUPS)
+    place = places[z]
+    metas = jnp.stack([block[:, 128:256] for block in rows])
+    meta = lax.dynamic_index_in_dim(metas, place, 0, keepdims=False)
+    acts = exchange(activate(parts, meta), Z_GROUPS)
 
     entry_range = jnp.arange(NE, dtype=jnp.int32)
     learner_entry = jnp.sum(
@@ -355,11 +416,14 @@
     chosen = jnp.take(learner_gate, learner_entry, axis=0, mode="clip")
     slot_gate = lax.all_to_all(chosen, "expert", split_axis=0, concat_axis=1, tiled=True)
 
-    partial = combine(acts, rows, held_down)
-    shared = exchange(partial.reshape(NT, ZR, WIDE), "tensor")
-    summed = jnp.sum(shared.astype(F32), axis=0).astype(BF)
-    crossed = exchange(summed.reshape(NX, RB, WIDE), "expert", X_GROUPS)
-    moe_out = swap_zt(jnp.sum(crossed.astype(F32), axis=0).astype(BF))
+    near, far = combine(
+        jnp.concatenate([blocks, lax.axis_index("expert").astype(jnp.int32)[None] % NX]),
+        acts,
+        rows,
+        held_down,
+    )
+    far = other_core(far)
+    moe_out = gather_out(near, far)
 
     latent = attend(query_latent, kv_cache, cache_len)
     head_rows = lax.all_to_all(latent, "tensor", split_axis=1, concat_axis=0, tiled=True)
@@ -388,5 +452,5 @@
     )
     out_specs = (P("expert", "tensor"), P("expert", "tensor"), P("expert", None, "tensor"))
     return jax.shard_map(
-        per_device, mesh=mesh, in_specs=in_specs, out_specs=out_specs, check_vma=False
-    )
+        device_body, mesh=mesh, in_specs=in_specs, out_specs=out_specs, check_vma=False
+    )

time: 332 us -> 272 us (0.82)
  the two profiles are of different devices: /device:TPU:2 before, /device:TPU:88 now
where the time goes in v2:
time: 272 us; the launch traced here: 271 us
  waiting for transfers between devices  132 us (49%)
  starting transfers between devices  67.3 us (25%)
  Pallas kernels  33.2 us (12%)
  local copies, waits for them, and re-layouts  26.1 us (10%)
  matrix products  7.02 us (3%)
  between operations  3.43 us (1%)
    ppermute x9, waiting for transfers between devices, shift_x(): return lax.ppermute(value, 'expert', pairs)  70 us
    all_to_all x3, waiting for transfers between devices, exchange(): lax.all_to_all(value, 'expert', split_axis=0, concat_axis=0, tiled=True,...  27.1 us
    ppermute x6, waiting for transfers between devices, shift_y(): return lax.ppermute(value, 'tensor', pairs)  21.5 us
    all_to_all x3, starting transfers between devices, exchange(): lax.all_to_all(value, 'expert', split_axis=0, concat_axis=0, tiled=True,...  19.3 us
    unnamed x91, local copies, waits for them, and re-layouts  19 us
    pallas_call x1, Pallas kernels, project(): pl.pallas_call(project_body, in_specs=[SMEM] + [VMEM] * (NZ + 1), out_sha...  17.7 us
    ppermute x9, starting transfers between devices, shift_x(): return lax.ppermute(value, 'expert', pairs)  15.1 us
    ppermute x2, starting transfers between devices, swap_zt(): return lax.ppermute(value, ('expert', 'tensor'), SWAP)  13.4 us
  transfers between devices with their start and end apart: 27, of which 17 were waited for; matrix products, arithmetic and copies ran while one was open for 8% of the time, Pallas kernels for 5%

profile of v2, /device:TPU:88, one launch (start us, length us, event | category | flops | bytes accessed | tf_op | source)
XLA Modules:
  0.0 270.6 jit_solution(2058765313783770273)
XLA Ops:
  5.4 1.9 copy-done.1
  7.4 5.0 %all-to-all-start.1 = ((bf16[4,1920,256]{2,1,0:T(8,128)(2,1)}), bf16[4,1920,256]{2,1,0:T(8,128)(2,1)}, u32[]{:S(2)}, u32[]{:S(2)}) async-start(bf16[4,1920,256]{2,1,0:T(8,128)(2,1)} %bitcast.66), calls=%async_computation.1 | async-start | bytes 7864320 | tf_op jit(solution)/shard_map/all_to_all | solution.py:44
  13.3 8.0 %collective-permute-start = (bf16[32,1024]{1,0:T(8,128)(2,1)S(1)}, bf16[32,1024]{1,0:T(8,128)(2,1)S(1)}, u32[]{:S(2)}, u32[]{:S(2)}) collective-permute-start(bf16[32,1024]{1,0:T(8,128)(2,1)S(1)} %concatenate.18), channel_id=1, source_target_pairs={{0,0},{1,32},{2,64},{3,96},{4,128},{5,160},{6,192},{7,224},{8,8},{... | collective-permute-start | bytes 196616 | tf_op jit(solution)/shard_map/ppermute | solution.py:40
  21.4 4.4 %collective-permute-done = bf16[32,1024]{1,0:T(8,128)(2,1)S(1)} collective-permute-done((bf16[32,1024]{1,0:T(8,128)(2,1)S(1)}, bf16[32,1024]{1,0:T(8,128)(2,1)S(1)}, u32[]{:S(2)}, u32[]{:S(2)}) %collective-permute-start) | collective-permute-done | bytes 65568 | tf_op jit(solution)/shard_map/ppermute | solution.py:40
  25.8 2.0 collective-permute-start.1
  27.8 2.7 collective-permute-start.2
  31.9 28.6 %collective-permute-done.1 = bf16[32,1024]{1,0:T(8,128)(2,1)S(1)} collective-permute-done((bf16[32,1024]{1,0:T(8,128)(2,1)S(1)}, bf16[32,1024]{1,0:T(8,128)(2,1)S(1)}, u32[]{:S(2)}, u32[]{:S(2)}) %collective-permute-start.1) | collective-permute-done | bytes 65568 | tf_op jit(solution)/shard_map/ppermute | solution.py:51
  61.8 2.6 collective-permute-start.5
  66.6 4.2 %collective-permute-done.4.refs_1_ = bf16[128,1024]{1,0:T(8,128)(2,1)S(1)} collective-permute-done((bf16[128,1024]{1,0:T(8,128)(2,1)S(1)}, bf16[128,1024]{1,0:T(8,128)(2,1)S(1)}, u32[]{:S(2)}, u32[]{:S(2)}) %collective-permute-start.4) | collective-permute-done | bytes 262176 | tf_op jit(solution)/shard_map/ppermute | solution.py:56
  72.5 3.2 %collective-permute-done.6.refs_3_ = bf16[128,1024]{1,0:T(8,128)(2,1)S(1)} collective-permute-done((bf16[128,1024]{1,0:T(8,128)(2,1)S(1)}, bf16[128,1024]{1,0:T(8,128)(2,1)S(1)}, u32[]{:S(2)}, u32[]{:S(2)}) %collective-permute-start.6) | collective-permute-done | bytes 262176 | tf_op jit(solution)/shard_map/ppermute | solution.py:56
  75.7 3.8 %fusion.37 = (f32[4,64]{1,0:T(4,128)S(1)}, bf16[4,64,768]{2,1,0:T(8,128)(2,1)}) fusion(pred[4,768]{1,0:T(4,128)(4,1)S(1)} %iota_compare_fusion, bf16[4,64,576]{2,1,0:T(8,128)(2,1)S(1)} %copy-done.36, bf16[4,768,576]{1,2,0:T(8,128)(2,1)} %param.14), kind=kOutput, calls=%fused_computation.94 | convolution fusion | flops 227672832 | bytes 4231168 | tf_op jit(solution)/shard_map/sub | solution.py:73
  79.6 17.7 %project.1 = bf16[8,528,128]{2,1,0:T(8,128)(2,1)} custom-call(s32[8]{0:T(128)S(1)} %pad_add_fusion.1.z_ref, bf16[128,1024]{1,0:T(8,128)(2,1)S(1)} %constant_dynamic-update-slice_fusion.refs_0_, bf16[128,1024]{1,0:T(8,128)(2,1)S(1)} %collective-permute-done.4.refs_1_, bf16[128,1024]{1,0:T(8,128)(2,1)S(1)} %collective-permute-done.5.refs_2_, ...), custom_call_target="tpu_custom_call" | custom-call | tf_op jit(solution)/shard_map/project/pallas_call | solution.py:194
  97.3 8.3 %all-to-all-start.2 = ((bf16[8,528,128]{2,1,0:T(8,128)(2,1)}), bf16[8,528,128]{2,1,0:T(8,128)(2,1)}, u32[]{:S(2)}, u32[]{:S(2)}) async-start(bf16[8,528,128]{2,1,0:T(8,128)(2,1)} %project.1), calls=%async_computation.2 | async-start | bytes 2162688 | tf_op jit(solution)/shard_map/all_to_all | solution.py:44
  105.6 3.0 %fusion.10 = bf16[4,64,512]{2,1,0:T(8,128)(2,1)S(1)} fusion(bf16[4,768,576]{1,2,0:T(8,128)(2,1)} %param.14, bf16[4,64,768]{2,1,0:T(8,128)(2,1)S(1)} %copy-done.38, f32[4,64]{1,0:T(4,128)S(1)} %get-tuple-element.28), kind=kOutput, calls=%fused_computation.10 | convolution fusion | flops 201588736 | bytes 3802112 | tf_op jit(solution)/shard_map/rhp,rpc->rhc/dot_general | solution.py:75
  117.6 15.6 %all-to-all-done.2.p_ref = bf16[8,528,128]{2,1,0:T(8,128)(2,1)} async-done(((bf16[8,528,128]{2,1,0:T(8,128)(2,1)}), bf16[8,528,128]{2,1,0:T(8,128)(2,1)}, u32[]{:S(2)}, u32[]{:S(2)}) %all-to-all-start.2) | async-done | bytes 1081376 | tf_op jit(solution)/shard_map/all_to_all | solution.py:44
  133.2 4.9 %all-to-all-start = ((bf16[4,64,512]{2,0,1:T(4,128)(2,1)}), bf16[4,64,512]{2,0,1:T(4,128)(2,1)S(1)}, u32[]{:S(2)}, u32[]{:S(2)}) async-start(bf16[4,64,512]{2,0,1:T(4,128)(2,1)} %copy.58), calls=%async_computation | async-start | bytes 524288 | tf_op jit(solution)/shard_map/all_to_all | solution.py:429
  144.3 6.0 %all-to-all-start.3 = ((bf16[8,256,128]{2,1,0:T(8,128)(2,1)}), bf16[8,256,128]{2,1,0:T(8,128)(2,1)S(1)}, u32[]{:S(2)}, u32[]{:S(2)}) async-start(bf16[8,256,128]{2,1,0:T(8,128)(2,1)} %copy-done.4), calls=%async_computation.3 | async-start | bytes 1048576 | tf_op jit(solution)/shard_map/all_to_all | solution.py:44
  150.5 2.0 gather_fusion
  152.5 11.5 %all-to-all-done.3.a_ref = bf16[8,256,128]{2,1,0:T(8,128)(2,1)S(1)} async-done(((bf16[8,256,128]{2,1,0:T(8,128)(2,1)}), bf16[8,256,128]{2,1,0:T(8,128)(2,1)S(1)}, u32[]{:S(2)}, u32[]{:S(2)}) %all-to-all-start.3) | async-done | bytes 524320 | tf_op jit(solution)/shard_map/all_to_all | solution.py:44
  164.0 8.1 %all-to-all-start.4 = ((bf16[32,224,128]{2,1,0:T(8,128)(2,1)}), bf16[32,224,128]{2,1,0:T(8,128)(2,1)}, u32[]{:S(2)}, u32[]{:S(2)}) async-start(bf16[32,224,128]{2,1,0:T(8,128)(2,1)} %gather_fusion), calls=%async_computation.4 | async-start | bytes 3670016 | tf_op jit(solution)/shard_map/all_to_all | solution.py:417
  176.6 2.7 collective-permute-start.12
  180.8 26.2 %collective-permute-done.11.refs_9_ = bf16[960,256]{1,0:T(8,128)(2,1)S(1)} collective-permute-done((bf16[960,256]{1,0:T(8,128)(2,1)S(1)}, bf16[960,256]{1,0:T(8,128)(2,1)S(1)}, u32[]{:S(2)}, u32[]{:S(2)}) %collective-permute-start.11) | collective-permute-done | bytes 491552 | tf_op jit(solution)/shard_map/ppermute | solution.py:51
  207.0 10.8 %collective-permute-done.12.refs_10_ = bf16[960,256]{1,0:T(8,128)(2,1)S(1)} collective-permute-done((bf16[960,256]{1,0:T(8,128)(2,1)S(1)}, bf16[960,256]{1,0:T(8,128)(2,1)S(1)}, u32[]{:S(2)}, u32[]{:S(2)}) %collective-permute-start.12) | collective-permute-done | bytes 491552 | tf_op jit(solution)/shard_map/ppermute | solution.py:51
  217.9 11.0 %combine.1 = (bf16[512,896]{1,0:T(8,128)(2,1)S(1)}, bf16[512,896]{1,0:T(8,128)(2,1)S(1)}) custom-call(s32[9]{0:T(128)S(1)} %pad_add_fusion.z_ref, bf16[8,256,128]{2,1,0:T(8,128)(2,1)S(1)} %all-to-all-done.3.a_ref, bf16[128,1024]{1,0:T(8,128)(2,1)S(1)} %copy-done.8, bf16[128,1024]{1,0:T(8,128)(2,1)S(1)} %copy-done.10, bf16[128,1024]{1,0:T(8,128)(2,1)S(1)} %copy-done.12, ...), custom_call_target="tpu_custom_call" | custom-call | tf_op jit(solution)/shard_map/combine/pallas_call | solution.py:297
  229.0 2.5 collective-permute-done.14
  231.7 2.1 collective-permute-start.17
  235.3 8.7 %collective-permute-done.17 = bf16[128,896]{1,0:T(8,128)(2,1)S(1)} collective-permute-done((bf16[128,896]{1,0:T(8,128)(2,1)S(1)}, bf16[128,896]{1,0:T(8,128)(2,1)S(1)}, u32[]{:S(2)}, u32[]{:S(2)}) %collective-permute-start.17) | collective-permute-done | bytes 229408 | tf_op jit(solution)/shard_map/ppermute | solution.py:56
  244.0 3.7 %collective-permute-done.15 = bf16[128,896]{1,0:T(8,128)(2,1)S(1)} collective-permute-done((bf16[128,896]{1,0:T(8,128)(2,1)S(1)}, bf16[128,896]{1,0:T(8,128)(2,1)S(1)}, u32[]{:S(2)}, u32[]{:S(2)}) %collective-permute-start.15) | collective-permute-done | bytes 229408 | tf_op jit(solution)/shard_map/ppermute | solution.py:56
  251.3 2.9 %collective-permute-done.20 = bf16[32,896]{1,0:T(8,128)(2,1)S(1)} collective-permute-done((bf16[32,896]{1,0:T(8,128)(2,1)S(1)}, bf16[32,896]{1,0:T(8,128)(2,1)S(1)}, u32[]{:S(2)}, u32[]{:S(2)}) %collective-permute-start.20) | collective-permute-done | bytes 57376 | tf_op jit(solution)/shard_map/ppermute | solution.py:51
  254.8 5.4 %collective-permute-start.21 = (bf16[32,896]{1,0:T(8,128)(2,1)S(1)}, bf16[32,896]{1,0:T(8,128)(2,1)S(1)}, u32[]{:S(2)}, u32[]{:S(2)}) collective-permute-start(bf16[32,896]{1,0:T(8,128)(2,1)S(1)} %add_convert_fusion.4), channel_id=1, source_target_pairs={{0,0},{1,32},{2,64},{3,96},{4,128},{5,160},{6,192},{7,224},{8,8},{... | collective-permute-start | bytes 172040 | tf_op jit(solution)/shard_map/ppermute | solution.py:40
  261.2 6.0 %collective-permute-done.21 = bf16[32,896]{1,0:T(8,128)(2,1)S(1)} collective-permute-done((bf16[32,896]{1,0:T(8,128)(2,1)S(1)}, bf16[32,896]{1,0:T(8,128)(2,1)S(1)}, u32[]{:S(2)}, u32[]{:S(2)}) %collective-permute-start.21) | collective-permute-done | bytes 57376 | tf_op jit(solution)/shard_map/ppermute | solution.py:40
  267.8 2.8 %copy.88 = bf16[1,7168,128]{2,1,0:T(8,128)(2,1)} copy(bf16[1,7168,128]{2,1,0:T(8,128)(2,1)} %bitcast.21) | data formatting | bytes 3670016
  (155 shorter events, 39.1 us)
Async XLA Ops:
  0.6 259.6 %copy-start = (bf16[8,512,128]{2,1,0:T(8,128)(2,1)S(1)}, bf16[8,512,128]{2,1,0:T(8,128)(2,1)}, u32[]{:S(2)}) copy-start(bf16[8,512,128]{2,1,0:T(8,128)(2,1)} %param.16) | copy-start | bytes 3145732
  7.4 59.1 %copy-start.33 = (s32[4]{0:T(128)S(1)}, s32[4]{0:T(128)}, u32[]{:S(2)}) copy-start(s32[4]{0:T(128)} %param.15) | copy-start | bytes 52
  7.4 68.3 %copy-start.36 = (bf16[4,64,576]{2,1,0:T(8,128)(2,1)S(1)}, bf16[4,64,576]{2,1,0:T(8,128)(2,1)}, u32[]{:S(2)}) copy-start(bf16[4,64,576]{2,1,0:T(8,128)(2,1)} %param.13) | copy-start | bytes 884740
  7.4 72.2 %all-to-all-start.1 = ((bf16[4,1920,256]{2,1,0:T(8,128)(2,1)}), bf16[4,1920,256]{2,1,0:T(8,128)(2,1)}, u32[]{:S(2)}, u32[]{:S(2)}) async-start(bf16[4,1920,256]{2,1,0:T(8,128)(2,1)} %bitcast.66), calls=%async_computation.1 | async-start | bytes 7864320 | tf_op jit(solution)/shard_map/all_to_all | solution.py:44
  13.3 12.5 %collective-permute-start = (bf16[32,1024]{1,0:T(8,128)(2,1)S(1)}, bf16[32,1024]{1,0:T(8,128)(2,1)S(1)}, u32[]{:S(2)}, u32[]{:S(2)}) collective-permute-start(bf16[32,1024]{1,0:T(8,128)(2,1)S(1)} %concatenate.18), channel_id=1, source_target_pairs={{0,0},{1,32},{2,64},{3,96},{4,128},{5,160},{6,192},{7,224},{8,8},{... | collective-permute-start | bytes 196616 | tf_op jit(solution)/shard_map/ppermute | solution.py:40
  21.3 45.1 %copy-start.29 = (s32[4]{0:T(128)}, s32[4]{0:T(128)S(1)}, u32[]{:S(2)}) copy-start(s32[4]{0:T(128)S(1)} %get-tuple-element.30) | copy-start | bytes 52
  25.8 34.7 %collective-permute-start.1 = (bf16[32,1024]{1,0:T(8,128)(2,1)S(1)}, bf16[32,1024]{1,0:T(8,128)(2,1)S(1)}, u32[]{:S(2)}, u32[]{:S(2)}) collective-permute-start(bf16[32,1024]{1,0:T(8,128)(2,1)S(1)} %collective-permute-done), channel_id=1, source_target_pairs={{0,8},{8,16},{16,24},{24,0},{32,40},{40,48},{48,56},{56,32},{64,72... | collective-permute-start | bytes 196616 | tf_op jit(solution)/shard_map/ppermute | solution.py:51
  27.8 33.7 %collective-permute-start.2 = (bf16[32,1024]{1,0:T(8,128)(2,1)S(1)}, bf16[32,1024]{1,0:T(8,128)(2,1)S(1)}, u32[]{:S(2)}, u32[]{:S(2)}) collective-permute-start(bf16[32,1024]{1,0:T(8,128)(2,1)S(1)} %collective-permute-done), channel_id=1, source_target_pairs={{0,16},{8,24},{16,0},{24,8},{32,48},{40,56},{48,32},{56,40},{64,80... | collective-permute-start | bytes 196616 | tf_op jit(solution)/shard_map/ppermute | solution.py:51
  30.4 31.1 %collective-permute-start.3 = (bf16[32,1024]{1,0:T(8,128)(2,1)S(1)}, bf16[32,1024]{1,0:T(8,128)(2,1)S(1)}, u32[]{:S(2)}, u32[]{:S(2)}) collective-permute-start(bf16[32,1024]{1,0:T(8,128)(2,1)S(1)} %collective-permute-done), channel_id=1, source_target_pairs={{0,24},{8,0},{16,8},{24,16},{32,56},{40,32},{48,40},{56,48},{64,88... | collective-permute-start | bytes 196616 | tf_op jit(solution)/shard_map/ppermute | solution.py:51
  61.5 48.7 %copy-start.7 = (bf16[128,1024]{1,0:T(8,128)(2,1)}, bf16[128,1024]{1,0:T(8,128)(2,1)S(1)}, u32[]{:S(2)}) copy-start(bf16[128,1024]{1,0:T(8,128)(2,1)S(1)} %constant_dynamic-update-slice_fusion.refs_0_) | copy-start | bytes 786436
  61.5 9.3 %collective-permute-start.4 = (bf16[128,1024]{1,0:T(8,128)(2,1)S(1)}, bf16[128,1024]{1,0:T(8,128)(2,1)S(1)}, u32[]{:S(2)}, u32[]{:S(2)}) collective-permute-start(bf16[128,1024]{1,0:T(8,128)(2,1)S(1)} %constant_dynamic-update-slice_fusion.refs_0_), channel_id=1, source_target_pairs={{0,2},{1,3},{2,4},{3,5},{4,6},{5,7},{6,0},{7,1},{8,10},{9,11},{10,... | collective-permute-start | bytes 786440 | tf_op jit(solution)/shard_map/ppermute | solution.py:56
  61.8 10.7 %collective-permute-start.5 = (bf16[128,1024]{1,0:T(8,128)(2,1)S(1)}, bf16[128,1024]{1,0:T(8,128)(2,1)S(1)}, u32[]{:S(2)}, u32[]{:S(2)}) collective-permute-start(bf16[128,1024]{1,0:T(8,128)(2,1)S(1)} %constant_dynamic-update-slice_fusion.refs_0_), channel_id=1, source_target_pairs={{0,4},{1,5},{2,6},{3,7},{4,0},{5,1},{6,2},{7,3},{8,12},{9,13},{10,... | collective-permute-start | bytes 786440 | tf_op jit(solution)/shard_map/ppermute | solution.py:56
  64.4 11.3 %collective-permute-start.6 = (bf16[128,1024]{1,0:T(8,128)(2,1)S(1)}, bf16[128,1024]{1,0:T(8,128)(2,1)S(1)}, u32[]{:S(2)}, u32[]{:S(2)}) collective-permute-start(bf16[128,1024]{1,0:T(8,128)(2,1)S(1)} %constant_dynamic-update-slice_fusion.refs_0_), channel_id=1, source_target_pairs={{0,6},{1,7},{2,0},{3,1},{4,2},{5,3},{6,4},{7,5},{8,14},{9,15},{10,... | collective-permute-start | bytes 786440 | tf_op jit(solution)/shard_map/ppermute | solution.py:56
  66.5 13.0 %collective-permute-start.7 = (bf16[128,1024]{1,0:T(8,128)(2,1)S(1)}, bf16[128,1024]{1,0:T(8,128)(2,1)S(1)}, u32[]{:S(2)}, u32[]{:S(2)}) collective-permute-start(bf16[128,1024]{1,0:T(8,128)(2,1)S(1)} %constant_dynamic-update-slice_fusion.refs_0_), channel_id=1, source_target_pairs={{0,1},{1,0},{2,3},{3,2},{4,5},{5,4},{6,7},{7,6},{8,9},{9,8},{10,11... | collective-permute-start | bytes 786440 | tf_op jit(solution)/shard_map/ppermute | solution.py:60
  70.8 8.8 %collective-permute-start.8 = (bf16[128,1024]{1,0:T(8,128)(2,1)S(1)}, bf16[128,1024]{1,0:T(8,128)(2,1)S(1)}, u32[]{:S(2)}, u32[]{:S(2)}) collective-permute-start(bf16[128,1024]{1,0:T(8,128)(2,1)S(1)} %collective-permute-done.4.refs_1_), channel_id=1, source_target_pairs={{0,1},{1,0},{2,3},{3,2},{4,5},{5,4},{6,7},{7,6},{8,9},{9,8},{10,11... | collective-permute-start | bytes 786440 | tf_op jit(solution)/shard_map/ppermute | solution.py:60
  72.5 7.0 %collective-permute-start.9 = (bf16[128,1024]{1,0:T(8,128)(2,1)S(1)}, bf16[128,1024]{1,0:T(8,128)(2,1)S(1)}, u32[]{:S(2)}, u32[]{:S(2)}) collective-permute-start(bf16[128,1024]{1,0:T(8,128)(2,1)S(1)} %collective-permute-done.5.refs_2_), channel_id=1, source_target_pairs={{0,1},{1,0},{2,3},{3,2},{4,5},{5,4},{6,7},{7,6},{8,9},{9,8},{10,11... | collective-permute-start | bytes 786440 | tf_op jit(solution)/shard_map/ppermute | solution.py:60
  75.7 3.9 %collective-permute-start.10 = (bf16[128,1024]{1,0:T(8,128)(2,1)S(1)}, bf16[128,1024]{1,0:T(8,128)(2,1)S(1)}, u32[]{:S(2)}, u32[]{:S(2)}) collective-permute-start(bf16[128,1024]{1,0:T(8,128)(2,1)S(1)} %collective-permute-done.6.refs_3_), channel_id=1, source_target_pairs={{0,1},{1,0},{2,3},{3,2},{4,5},{5,4},{6,7},{7,6},{8,9},{9,8},{10,11... | collective-permute-start | bytes 786440 | tf_op jit(solution)/shard_map/ppermute | solution.py:60
  97.3 35.9 %all-to-all-start.2 = ((bf16[8,528,128]{2,1,0:T(8,128)(2,1)}), bf16[8,528,128]{2,1,0:T(8,128)(2,1)}, u32[]{:S(2)}, u32[]{:S(2)}) async-start(bf16[8,528,128]{2,1,0:T(8,128)(2,1)} %project.1), calls=%async_computation.2 | async-start | bytes 2162688 | tf_op jit(solution)/shard_map/all_to_all | solution.py:44
  133.2 10.4 %all-to-all-start = ((bf16[4,64,512]{2,0,1:T(4,128)(2,1)}), bf16[4,64,512]{2,0,1:T(4,128)(2,1)S(1)}, u32[]{:S(2)}, u32[]{:S(2)}) async-start(bf16[4,64,512]{2,0,1:T(4,128)(2,1)} %copy.58), calls=%async_computation | async-start | bytes 524288 | tf_op jit(solution)/shard_map/all_to_all | solution.py:429
  144.3 19.7 %all-to-all-start.3 = ((bf16[8,256,128]{2,1,0:T(8,128)(2,1)}), bf16[8,256,128]{2,1,0:T(8,128)(2,1)S(1)}, u32[]{:S(2)}, u32[]{:S(2)}) async-start(bf16[8,256,128]{2,1,0:T(8,128)(2,1)} %copy-done.4), calls=%async_computation.3 | async-start | bytes 1048576 | tf_op jit(solution)/shard_map/all_to_all | solution.py:44
  164.0 97.1 %all-to-all-start.4 = ((bf16[32,224,128]{2,1,0:T(8,128)(2,1)}), bf16[32,224,128]{2,1,0:T(8,128)(2,1)}, u32[]{:S(2)}, u32[]{:S(2)}) async-start(bf16[32,224,128]{2,1,0:T(8,128)(2,1)} %gather_fusion), calls=%async_computation.4 | async-start | bytes 3670016 | tf_op jit(solution)/shard_map/all_to_all | solution.py:417
  175.1 31.9 %collective-permute-start.11 = (bf16[960,256]{1,0:T(8,128)(2,1)S(1)}, bf16[960,256]{1,0:T(8,128)(2,1)S(1)}, u32[]{:S(2)}, u32[]{:S(2)}) collective-permute-start(bf16[960,256]{1,0:T(8,128)(2,1)S(1)} %get-tuple-element.9), channel_id=1, source_target_pairs={{0,8},{8,16},{16,24},{24,0},{32,40},{40,48},{48,56},{56,32},{64,72... | collective-permute-start | bytes 1474568 | tf_op jit(solution)/shard_map/ppermute | solution.py:51
  176.6 41.2 %collective-permute-start.12 = (bf16[960,256]{1,0:T(8,128)(2,1)S(1)}, bf16[960,256]{1,0:T(8,128)(2,1)S(1)}, u32[]{:S(2)}, u32[]{:S(2)}) collective-permute-start(bf16[960,256]{1,0:T(8,128)(2,1)S(1)} %get-tuple-element.8), channel_id=1, source_target_pairs={{0,16},{8,24},{16,0},{24,8},{32,48},{40,56},{48,32},{56,40},{64,80... | collective-permute-start | bytes 1474568 | tf_op jit(solution)/shard_map/ppermute | solution.py:51
  179.3 38.5 %collective-permute-start.13 = (bf16[960,256]{1,0:T(8,128)(2,1)S(1)}, bf16[960,256]{1,0:T(8,128)(2,1)S(1)}, u32[]{:S(2)}, u32[]{:S(2)}) collective-permute-start(bf16[960,256]{1,0:T(8,128)(2,1)S(1)} %get-tuple-element.7), channel_id=1, source_target_pairs={{0,24},{8,0},{16,8},{24,16},{32,56},{40,32},{48,40},{56,48},{64,88... | collective-permute-start | bytes 1474568 | tf_op jit(solution)/shard_map/ppermute | solution.py:51
  228.9 2.6 collective-permute-start.14
  231.7 12.3 %collective-permute-start.17 = (bf16[128,896]{1,0:T(8,128)(2,1)S(1)}, bf16[128,896]{1,0:T(8,128)(2,1)S(1)}, u32[]{:S(2)}, u32[]{:S(2)}) collective-permute-start(bf16[128,896]{1,0:T(8,128)(2,1)S(1)} %get-tuple-element.12), channel_id=1, source_target_pairs={{0,2},{1,3},{2,4},{3,5},{4,6},{5,7},{6,0},{7,1},{8,10},{9,11},{10,... | collective-permute-start | bytes 688136 | tf_op jit(solution)/shard_map/ppermute | solution.py:56
  233.9 10.1 %collective-permute-start.16 = (bf16[128,896]{1,0:T(8,128)(2,1)S(1)}, bf16[128,896]{1,0:T(8,128)(2,1)S(1)}, u32[]{:S(2)}, u32[]{:S(2)}) collective-permute-start(bf16[128,896]{1,0:T(8,128)(2,1)S(1)} %get-tuple-element.13), channel_id=1, source_target_pairs={{0,4},{1,5},{2,6},{3,7},{4,0},{5,1},{6,2},{7,3},{8,12},{9,13},{10,... | collective-permute-start | bytes 688136 | tf_op jit(solution)/shard_map/ppermute | solution.py:56
  234.5 13.2 %collective-permute-start.15 = (bf16[128,896]{1,0:T(8,128)(2,1)S(1)}, bf16[128,896]{1,0:T(8,128)(2,1)S(1)}, u32[]{:S(2)}, u32[]{:S(2)}) collective-permute-start(bf16[128,896]{1,0:T(8,128)(2,1)S(1)} %get-tuple-element.14), channel_id=1, source_target_pairs={{0,6},{1,7},{2,0},{3,1},{4,2},{5,3},{6,4},{7,5},{8,14},{9,15},{10,... | collective-permute-start | bytes 688136 | tf_op jit(solution)/shard_map/ppermute | solution.py:56
  247.8 6.4 %collective-permute-start.20 = (bf16[32,896]{1,0:T(8,128)(2,1)S(1)}, bf16[32,896]{1,0:T(8,128)(2,1)S(1)}, u32[]{:S(2)}, u32[]{:S(2)}) collective-permute-start(bf16[32,896]{1,0:T(8,128)(2,1)S(1)} %get-tuple-element.16), channel_id=1, source_target_pairs={{0,8},{8,16},{16,24},{24,0},{32,40},{40,48},{48,56},{56,32},{64,72... | collective-permute-start | bytes 172040 | tf_op jit(solution)/shard_map/ppermute | solution.py:51
  247.9 6.3 %collective-permute-start.19 = (bf16[32,896]{1,0:T(8,128)(2,1)S(1)}, bf16[32,896]{1,0:T(8,128)(2,1)S(1)}, u32[]{:S(2)}, u32[]{:S(2)}) collective-permute-start(bf16[32,896]{1,0:T(8,128)(2,1)S(1)} %get-tuple-element.17), channel_id=1, source_target_pairs={{0,16},{8,24},{16,0},{24,8},{32,48},{40,56},{48,32},{56,40},{64,80... | collective-permute-start | bytes 172040 | tf_op jit(solution)/shard_map/ppermute | solution.py:51
  249.5 5.2 %collective-permute-start.18 = (bf16[32,896]{1,0:T(8,128)(2,1)S(1)}, bf16[32,896]{1,0:T(8,128)(2,1)S(1)}, u32[]{:S(2)}, u32[]{:S(2)}) collective-permute-start(bf16[32,896]{1,0:T(8,128)(2,1)S(1)} %get-tuple-element.15), channel_id=1, source_target_pairs={{0,24},{8,0},{16,8},{24,16},{32,56},{40,32},{48,40},{56,48},{64,88... | collective-permute-start | bytes 172040 | tf_op jit(solution)/shard_map/ppermute | solution.py:51
  254.8 12.4 %collective-permute-start.21 = (bf16[32,896]{1,0:T(8,128)(2,1)S(1)}, bf16[32,896]{1,0:T(8,128)(2,1)S(1)}, u32[]{:S(2)}, u32[]{:S(2)}) collective-permute-start(bf16[32,896]{1,0:T(8,128)(2,1)S(1)} %add_convert_fusion.4), channel_id=1, source_target_pairs={{0,0},{1,32},{2,64},{3,96},{4,128},{5,160},{6,192},{7,224},{8,8},{... | collective-permute-start | bytes 172040 | tf_op jit(solution)/shard_map/ppermute | solution.py:40
  (34 other events, 736.5 us)

commit v3 on v2

--- a/solution.py
+++ b/solution.py
@@ -24,7 +24,6 @@
 TOP = 8
 DIM = 7168
 
-X_GROUPS = [[z * NX + x for x in range(NX)] for z in range(NZ)]
 Z_GROUPS = [[z * NX + x for z in range(NZ)] for x in range(NX)]
 SWAP = [
     ((z * NX + x) * NT + t, (t * NX + x) * NT + z)
@@ -90,48 +89,80 @@
     return jnp.concatenate([turned, jnp.zeros((FT, GL - SLICE), F32)], axis=1).astype(BF)
 
 
-def gate_up_body(g_ref, u_ref, o_ref):
-    for e in range(g_ref.shape[0]):
-        g = flip(g_ref[e])
-        u = flip(u_ref[e])
-        for x in range(NX):
-            o_ref[x, e, 0:FX, :] = g[x * FX : (x + 1) * FX]
-            o_ref[x, e, FX : 2 * FX, :] = u[x * FX : (x + 1) * FX]
-
-
-def down_body(d_ref, o_ref):
-    for e in range(d_ref.shape[0]):
-        d = flip(d_ref[e])
-        for x in range(NX):
-            o_ref[x, e] = d[x * FX : (x + 1) * FX]
-
-
-STEP_E = 5
-
-
-def turn_gate_up(gate, up):
-    spec = pl.BlockSpec((STEP_E, SLICE, FT), lambda i: (i, 0, 0))
+SMEM = pl.BlockSpec(memory_space=pltpu.SMEM)
+VMEM = pl.BlockSpec(memory_space=pltpu.VMEM)
+HEAD = 16
+
+
+def gate_up_body(own_ref, g_ref, u_ref, *refs):
+    outs, (turn_ref,) = refs[:5], refs[5:]
+    own = own_ref[0]
+
+    def turn(e, carry):
+        turn_ref[0, e] = flip(g_ref[e])
+        turn_ref[1, e] = flip(u_ref[e])
+        return carry
+
+    lax.fori_loop(0, NE, turn, 0, unroll=5)
+    for s in range(NX):
+        at = pl.multiple_of((own + s) % NX * FX, FX)
+        spans = [(outs[s], 0, NE)]
+        if s == 2:
+            spans = [(outs[2], 0, HEAD), (outs[4], HEAD, NE)]
+        for out, low, high in spans:
+
+            def copy(e, carry, out=out, low=low, at=at):
+                row = pl.multiple_of((e - low) * 2 * FX, 2 * FX)
+                out[pl.ds(row, FX)] = turn_ref[0, e, pl.ds(at, FX), :]
+                out[pl.ds(row + FX, FX)] = turn_ref[1, e, pl.ds(at, FX), :]
+                return carry
+
+            lax.fori_loop(low, high, copy, 0, unroll=2)
+
+
+def down_body(own_ref, d_ref, *refs):
+    outs, (turn_ref,) = refs[:NX], refs[NX:]
+    own = own_ref[0]
+
+    def turn(e, carry):
+        turn_ref[e] = flip(d_ref[e])
+        return carry
+
+    lax.fori_loop(0, NE, turn, 0, unroll=5)
+    for s in range(NX):
+        at = pl.multiple_of((own + s) % NX * FX, FX)
+
+        def copy(e, carry, out=outs[s], at=at):
+            row = pl.multiple_of(e * FX, FX)
+            out[pl.ds(row, FX)] = turn_ref[e, pl.ds(at, FX), :]
+            return carry
+
+        lax.fori_loop(0, NE, copy, 0, unroll=3)
+
+
+def turn_gate_up(own, gate, up):
+    sizes = [NE, NE, HEAD, NE, NE - HEAD]
     return pl.pallas_call(
         gate_up_body,
-        grid=(NE // STEP_E,),
-        in_specs=[spec, spec],
-        out_specs=pl.BlockSpec((NX, STEP_E, 2 * FX, GL), lambda i: (0, i, 0, 0)),
-        out_shape=jax.ShapeDtypeStruct((NX, NE, 2 * FX, GL), BF),
-        compiler_params=pltpu.CompilerParams(vmem_limit_bytes=16 << 20),
+        in_specs=[SMEM, VMEM, VMEM],
+        out_specs=[VMEM] * 5,
+        out_shape=[jax.ShapeDtypeStruct((n * 2 * FX, GL), BF) for n in sizes],
+        scratch_shapes=[pltpu.VMEM((2, NE, FT, GL), BF)],
+        compiler_params=pltpu.CompilerParams(vmem_limit_bytes=20 << 20),
         name="turn_gate_up",
-    )(gate, up)
-
-
-def turn_down(down):
+    )(own, gate, up)
+
+
+def turn_down(own, down):
     return pl.pallas_call(
         down_body,
-        grid=(NE // STEP_E,),
-        in_specs=[pl.BlockSpec((STEP_E, SLICE, FT), lambda i: (i, 0, 0))],
-        out_specs=pl.BlockSpec((NX, STEP_E, FX, GL), lambda i: (0, i, 0, 0)),
-        out_shape=jax.ShapeDtypeStruct((NX, NE, FX, GL), BF),
-        compiler_params=pltpu.CompilerParams(vmem_limit_bytes=16 << 20),
+        in_specs=[SMEM, VMEM],
+        out_specs=[VMEM] * NX,
+        out_shape=[jax.ShapeDtypeStruct((NE * FX, GL), BF)] * NX,
+        scratch_shapes=[pltpu.VMEM((NE, FT, GL), BF)],
+        compiler_params=pltpu.CompilerParams(vmem_limit_bytes=14 << 20),
         name="turn_down",
-    )(down)
+    )(own, down)
 
 
 META = 96
@@ -141,20 +172,28 @@
 
 
 def project_body(z_ref, *refs):
-    x_refs, (w_ref, p_ref, id_ref, y_ref) = refs[:NZ], refs[NZ:]
+    x_refs, w_refs = refs[:NZ], refs[NZ : NZ + 5]
+    p_ref, id_ref, y_ref = refs[NZ + 5 :]
     meta = jnp.concatenate([x[:, 128:256] for x in x_refs], axis=0)
     col = iota((128, TOP * 128), 1)
     pick = (iota((128, TOP * 128), 0) - META == col // 128).astype(F32).astype(BF)
     spread = jnp.dot(meta, pick, preferred_element_type=F32)
     half = (iota((1, TOP * 128), 1) % 128 // 64).astype(F32)
     id_ref[...] = (spread - half).astype(BF)
+    xs = []
+    for s in range(NX):
+        lane = pl.multiple_of((z_ref[NZ] + NX - s) % NX * GL, GL)
+        xs.append(jnp.concatenate([x[:, pl.ds(lane, GL)] for x in x_refs], axis=0))
     for start in range(0, NE * 2 * FX, 256):
         size = min(256, NE * 2 * FX - start)
         total = None
-        for k in range(NX):
+        for s in range(NX):
+            w_ref, row = w_refs[s], start
+            if s == 2 and start >= HEAD * 2 * FX:
+                w_ref, row = w_refs[4], start - HEAD * 2 * FX
             part = lax.dot_general(
-                jnp.concatenate([x[:, k * GL : (k + 1) * GL] for x in x_refs], axis=0),
-                w_ref[k, start : start + size, :],
+                xs[s],
+                w_ref[row : row + size, :],
                 (((1,), (1,)), ((), ())),
                 preferred_element_type=F32,
             )
@@ -186,14 +225,10 @@
         p_ref[z_ref[n], PR:PB, :] = turned[112:128].astype(BF)
 
 
-SMEM = pl.BlockSpec(memory_space=pltpu.SMEM)
-VMEM = pl.BlockSpec(memory_space=pltpu.VMEM)
-
-
 def project(blocks, rows, weights):
     return pl.pallas_call(
         project_body,
-        in_specs=[SMEM] + [VMEM] * (NZ + 1),
+        in_specs=[SMEM] + [VMEM] * (NZ + 5),
         out_shape=jax.ShapeDtypeStruct((NZ, PB, 128), BF),
         scratch_shapes=[
             pltpu.VMEM((ROWS, TOP * 128), BF),
@@ -201,7 +236,7 @@
         ],
         compiler_params=pltpu.CompilerParams(vmem_limit_bytes=32 << 20),
         name="project",
-    )(blocks, *rows, weights)
+    )(blocks, *rows, *weights)
 
 
 def activate_body(p_ref, m_ref, o_ref):
@@ -309,36 +344,44 @@
     )(blocks, acts, *rows, *down)
 
 
+def pack_body(h_ref, n_ref, e_ref, r_ref, l_ref, o_ref):
+    widened = h_ref[...].astype(F32)
+    scaled = (widened * n_ref[...].astype(F32)).astype(BF)
+    squares = jnp.sum(widened * widened, axis=1, keepdims=True)
+    high = squares.astype(BF).astype(F32)
+    place = iota((RB, NE), 1)
+    entries = [
+        jnp.sum(
+            jnp.where(l_ref[...] == e_ref[:, j : j + 1], place, 0), axis=1, keepdims=True
+        ).astype(F32)
+        for j in range(TOP)
+    ]
+    weight = r_ref[...]
+    meta = entries + [
+        (weight >> 6).astype(F32),
+        (weight & 63).astype(F32),
+        high,
+        squares - high,
+        jnp.zeros((RB, GL - SLICE - 26), F32),
+    ]
+    o_ref[...] = jnp.zeros((RB, NX * GL), BF)
+    for k in range(NX):
+        o_ref[:, k * GL : k * GL + SLICE] = scaled[:, k * SLICE : (k + 1) * SLICE]
+    o_ref[:, SLICE:GL] = jnp.concatenate(meta, axis=1).astype(BF)
+
+
 def pack_rows(hidden_in, norm_gain, expert_ids, route_weight, updated_list):
-    named = updated_list[None, None, :] == expert_ids[:, :, None]
-    entries = jnp.sum(
-        jnp.where(named, jnp.arange(NE, dtype=jnp.int32)[None, None, :], 0), axis=2
-    )
-    widened = hidden_in.astype(F32)
-    scaled = (widened * norm_gain.astype(F32)[None, :]).astype(BF)
-    squares = jnp.sum(widened * widened, axis=1, keepdims=True)
-    high = lax.reduce_precision(squares, 8, 7)
-    meta = jnp.concatenate(
-        [
-            entries.astype(F32),
-            (route_weight // 64).astype(F32),
-            (route_weight % 64).astype(F32),
-            high,
-            squares - high,
-            jnp.zeros((RB, GL - SLICE - 26), F32),
-        ],
-        axis=1,
-    ).astype(BF)
-    pad = jnp.zeros((RB, GL - SLICE), BF)
-    pieces = []
-    for k in range(NX):
-        pieces += [scaled[:, k * SLICE : (k + 1) * SLICE], meta if k == 0 else pad]
-    return jnp.concatenate(pieces, axis=1)
+    return pl.pallas_call(
+        pack_body,
+        out_shape=jax.ShapeDtypeStruct((RB, NX * GL), BF),
+        compiler_params=pltpu.CompilerParams(vmem_limit_bytes=4 << 20),
+        name="pack_rows",
+    )(hidden_in, norm_gain[None, :], expert_ids, route_weight, updated_list[None, :])
 
 
 def gather_rows(packed):
-    moved = swap_zt(packed)
-    ring = jnp.concatenate([moved] + [shift_x(moved, s) for s in range(1, NX)], axis=0)
+    came = [shift_x(packed, s) for s in range(1, NX)]
+    ring = swap_zt(jnp.concatenate([packed] + came, axis=0))
     mine = [ring] + [shift_y(ring, s) for s in range(1, NY)]
     return mine + [other_core(block) for block in mine]
 
@@ -354,12 +397,57 @@
     return blocks, places.astype(jnp.int32)
 
 
-def swap_down(down):
-    own = lax.axis_index("expert") % NX
-    mine = [
-        lax.dynamic_index_in_dim(down, (own + s) % NX, 0, keepdims=False) for s in range(NX)
+def move_gate_up(pieces):
+    ahead = shift_x(pieces[2], 1)
+    behind = shift_x(pieces[4], NX - 1)
+    came = [pieces[0], shift_x(pieces[1], 1), shift_x(pieces[3], NX - 1)]
+    ahead = shift_x(ahead, 1)
+    behind = shift_x(behind, NX - 1)
+    return [came[0], came[1], ahead, came[2], behind]
+
+
+def move_down(pieces):
+    return [pieces[0]] + [shift_x(pieces[s], s) for s in range(1, NX)]
+
+
+def place_body(own_ref, *refs):
+    pieces, (out_ref, sems) = refs[:NX], refs[NX:]
+    copies = [
+        pltpu.make_async_copy(
+            pieces[s], out_ref.at[:, (own_ref[0] + NX - s) % NX], sems.at[s]
+        )
+        for s in range(NX)
     ]
-    return mine[:1] + [shift_x(mine[s], s) for s in range(1, NX)]
+    for copy in copies:
+        copy.start()
+    for copy in copies:
+        copy.wait()
+
+
+def move_gate(chosen, own):
+    came = lax.all_to_all(
+        chosen.reshape(NZ, NX, SLICE, FT),
+        "expert",
+        split_axis=0,
+        concat_axis=0,
+        tiled=True,
+        axis_index_groups=Z_GROUPS,
+    )
+    x = own[0]
+    pieces = [
+        lax.dynamic_index_in_dim(came, (x + s) % NX, 1, keepdims=False) for s in range(NX)
+    ]
+    pieces = [pieces[0]] + [shift_x(pieces[s], s) for s in range(1, NX)]
+    anywhere = pl.BlockSpec(memory_space=pl.ANY)
+    return pl.pallas_call(
+        place_body,
+        in_specs=[SMEM] + [anywhere] * NX,
+        out_specs=anywhere,
+        out_shape=jax.ShapeDtypeStruct((NZ, NX, SLICE, FT), BF),
+        scratch_shapes=[pltpu.SemaphoreType.DMA((NX,))],
+        compiler_params=pltpu.CompilerParams(vmem_limit_bytes=1 << 20),
+        name="place_gate",
+    )(own, *pieces).reshape(1, DIM, FT)
 
 
 def add(values):
@@ -395,33 +483,26 @@
     learner_up,
     learner_down,
 ):
-    turned = turn_gate_up(learner_gate, learner_up)
-    held = exchange(turned.reshape(NX, NE * 2 * FX, GL), X_GROUPS)
+    own = (lax.axis_index("expert") % NX).astype(jnp.int32)[None]
+    held = move_gate_up(turn_gate_up(own, learner_gate, learner_up))
     rows = gather_rows(pack_rows(hidden_in, norm_gain, expert_ids, route_weight, updated_list))
     blocks, places = block_places()
-    down = turn_down(learner_down).reshape(NX, NE * FX, GL)
-    held_down = swap_down(down)
-    parts = exchange(project(blocks, rows, held), Z_GROUPS)
-    z = lax.axis_index("expert") // NX
-    place = places[z]
-    metas = jnp.stack([block[:, 128:256] for block in rows])
-    meta = lax.dynamic_index_in_dim(metas, place, 0, keepdims=False)
-    acts = exchange(activate(parts, meta), Z_GROUPS)
+    blocks = jnp.concatenate([blocks, own])
 
     entry_range = jnp.arange(NE, dtype=jnp.int32)
     learner_entry = jnp.sum(
         entry_range[None, :] * (updated_list[None, :] == placement_plan[:, None]).astype(jnp.int32),
         axis=1,
     )
-    chosen = jnp.take(learner_gate, learner_entry, axis=0, mode="clip")
-    slot_gate = lax.all_to_all(chosen, "expert", split_axis=0, concat_axis=1, tiled=True)
-
-    near, far = combine(
-        jnp.concatenate([blocks, lax.axis_index("expert").astype(jnp.int32)[None] % NX]),
-        acts,
-        rows,
-        held_down,
-    )
+    slot_gate = move_gate(jnp.take(learner_gate, learner_entry, axis=0, mode="clip"), own)
+
+    held_down = move_down(turn_down(own, learner_down))
+    parts = exchange(project(blocks, rows, held), Z_GROUPS)
+    z = lax.axis_index("expert") // NX
+    metas = jnp.stack([block[:, 128:256] for block in rows])
+    meta = lax.dynamic_index_in_dim(metas, places[z], 0, keepdims=False)
+    acts = exchange(activate(parts, meta), Z_GROUPS)
+    near, far = combine(blocks, acts, rows, held_down)
     far = other_core(far)
     moe_out = gather_out(near, far)
 

time: 272 us -> 262 us (0.963)
  the two profiles are of different devices: /device:TPU:88 before, /device:TPU:2 now
where the time goes in v3:
time: 262 us; the launch traced here: 260 us
  waiting for transfers between devices  108 us (41%)
  starting transfers between devices  74.4 us (28%)
  Pallas kernels  37.5 us (14%)
  local copies, waits for them, and re-layouts  24.9 us (10%)
  matrix products  6.92 us (3%)
  other arithmetic  5.77 us (2%)
  between operations  3.02 us (1%)
    ppermute x18, waiting for transfers between devices, shift_x(): return lax.ppermute(value, 'expert', pairs)  56.3 us
    all_to_all x2, waiting for transfers between devices, exchange(): lax.all_to_all(value, 'expert', split_axis=0, concat_axis=0, tiled=True,...  38.6 us
    ppermute x6, starting transfers between devices, shift_y(): return lax.ppermute(value, 'tensor', pairs)  33.6 us
    ppermute x18, starting transfers between devices, shift_x(): return lax.ppermute(value, 'expert', pairs)  23.2 us
    pallas_call x1, Pallas kernels, project(): pl.pallas_call(project_body, in_specs=[SMEM] + [VMEM] * (NZ + 5), out_sha...  17 us
    unnamed x78, local copies, waits for them, and re-layouts  15.7 us
    ppermute x6, waiting for transfers between devices, shift_y(): return lax.ppermute(value, 'tensor', pairs)  12.3 us
    pallas_call x1, Pallas kernels, combine(): pl.pallas_call(combine_body, in_specs=[SMEM] + [VMEM] * (NZ + 1 + NX), ou...  12 us
  transfers between devices with their start and end apart: 35, of which 14 were waited for; matrix products, arithmetic and copies ran while one was open for 9% of the time, Pallas kernels for 7%

profile of v3, /device:TPU:2, one launch (start us, length us, event | category | flops | bytes accessed | tf_op | source)
XLA Modules:
  0.0 260.4 jit_solution(9140536886184287699)
XLA Ops:
  5.1 2.3 collective-permute-start.2
  8.1 1.8 collective-permute-start
  12.9 3.4 %turn_gate_up.1 = (bf16[1920,256]{1,0:T(8,128)(2,1)S(1)}, bf16[1920,256]{1,0:T(8,128)(2,1)}, bf16[1024,256]{1,0:T(8,128)(2,1)S(1)}, bf16[1920,256]{1,0:T(8,128)(2,1)}, bf16[896,256]{1,0:T(8,128)(2,1)S(1)}) custom-call(s32[1]{0:T(128)} %bitcast.3.own_ref, bf16[30,224,128]{2,1,0:T(8,128)(2,1)S(1)} %copy-done.1, bf16[30,224,128]{2,1,0:T(8,128)(2,1)S(1)} %copy-done.5), custom_call_target="tpu_custom_call" | custom-call | tf_op jit(solution)/shard_map/turn_gate_up/pallas_call | solution.py:145
  20.0 23.8 %collective-permute-start.4 = (bf16[128,1024]{1,0:T(8,128)(2,1)S(1)}, bf16[128,1024]{1,0:T(8,128)(2,1)S(1)}, u32[]{:S(2)}, u32[]{:S(2)}) collective-permute-start(bf16[128,1024]{1,0:T(8,128)(2,1)S(1)} %collective-permute-done.3.refs_0_), channel_id=1, source_target_pairs={{0,2},{1,3},{2,4},{3,5},{4,6},{5,7},{6,0},{7,1},{8,10},{9,11},{10,... | collective-permute-start | bytes 786440 | tf_op jit(solution)/shard_map/ppermute | solution.py:55
  43.9 3.7 %collective-permute-start.5 = (bf16[128,1024]{1,0:T(8,128)(2,1)S(1)}, bf16[128,1024]{1,0:T(8,128)(2,1)S(1)}, u32[]{:S(2)}, u32[]{:S(2)}) collective-permute-start(bf16[128,1024]{1,0:T(8,128)(2,1)S(1)} %collective-permute-done.3.refs_0_), channel_id=1, source_target_pairs={{0,4},{1,5},{2,6},{3,7},{4,0},{5,1},{6,2},{7,3},{8,12},{9,13},{10,... | collective-permute-start | bytes 786440 | tf_op jit(solution)/shard_map/ppermute | solution.py:55
  49.6 3.5 %collective-permute-done.4.refs_1_ = bf16[128,1024]{1,0:T(8,128)(2,1)S(1)} collective-permute-done((bf16[128,1024]{1,0:T(8,128)(2,1)S(1)}, bf16[128,1024]{1,0:T(8,128)(2,1)S(1)}, u32[]{:S(2)}, u32[]{:S(2)}) %collective-permute-start.4) | collective-permute-done | bytes 262176 | tf_op jit(solution)/shard_map/ppermute | solution.py:55
  53.1 6.8 %collective-permute-done.5.refs_2_ = bf16[128,1024]{1,0:T(8,128)(2,1)S(1)} collective-permute-done((bf16[128,1024]{1,0:T(8,128)(2,1)S(1)}, bf16[128,1024]{1,0:T(8,128)(2,1)S(1)}, u32[]{:S(2)}, u32[]{:S(2)}) %collective-permute-start.5) | collective-permute-done | bytes 262176 | tf_op jit(solution)/shard_map/ppermute | solution.py:55
  65.1 17.4 %collective-permute-done.16.refs_12_ = bf16[896,256]{1,0:T(8,128)(2,1)} collective-permute-done((bf16[896,256]{1,0:T(8,128)(2,1)}, bf16[896,256]{1,0:T(8,128)(2,1)}, u32[]{:S(2)}, u32[]{:S(2)}) %collective-permute-start.16) | collective-permute-done | bytes 458784 | tf_op jit(solution)/shard_map/ppermute | solution.py:50
  84.0 17.0 %project.1 = bf16[8,528,128]{2,1,0:T(8,128)(2,1)} custom-call(s32[9]{0:T(128)S(1)} %pad_add_fusion.z_ref, bf16[128,1024]{1,0:T(8,128)(2,1)S(1)} %collective-permute-done.3.refs_0_, bf16[128,1024]{1,0:T(8,128)(2,1)S(1)} %collective-permute-done.4.refs_1_, bf16[128,1024]{1,0:T(8,128)(2,1)S(1)} %collective-permute-done.5.refs_2_, ...), custom_call_target="tpu_custom_call" | custom-call | tf_op jit(solution)/shard_map/project/pallas_call | solution.py:229
  101.5 4.3 %all-to-all-start.1 = ((bf16[8,528,128]{2,1,0:T(8,128)(2,1)}), bf16[8,528,128]{2,1,0:T(8,128)(2,1)}, u32[]{:S(2)}, u32[]{:S(2)}) async-start(bf16[8,528,128]{2,1,0:T(8,128)(2,1)} %project.1), calls=%async_computation.1 | async-start | bytes 2162688 | tf_op jit(solution)/shard_map/all_to_all | solution.py:43
  110.5 24.4 %all-to-all-done.1.p_ref = bf16[8,528,128]{2,1,0:T(8,128)(2,1)} async-done(((bf16[8,528,128]{2,1,0:T(8,128)(2,1)}), bf16[8,528,128]{2,1,0:T(8,128)(2,1)}, u32[]{:S(2)}, u32[]{:S(2)}) %all-to-all-start.1) | async-done | bytes 1081376 | tf_op jit(solution)/shard_map/all_to_all | solution.py:43
  138.0 3.5 %all-to-all-start.2 = ((bf16[8,256,128]{2,1,0:T(8,128)(2,1)}), bf16[8,256,128]{2,1,0:T(8,128)(2,1)S(1)}, u32[]{:S(2)}, u32[]{:S(2)}) async-start(bf16[8,256,128]{2,1,0:T(8,128)(2,1)} %copy-done.3), calls=%async_computation.2 | async-start | bytes 1048576 | tf_op jit(solution)/shard_map/all_to_all | solution.py:43
  143.0 2.1 gather_fusion
  145.1 14.3 %all-to-all-done.2.a_ref = bf16[8,256,128]{2,1,0:T(8,128)(2,1)S(1)} async-done(((bf16[8,256,128]{2,1,0:T(8,128)(2,1)}), bf16[8,256,128]{2,1,0:T(8,128)(2,1)S(1)}, u32[]{:S(2)}, u32[]{:S(2)}) %all-to-all-start.2) | async-done | bytes 524320 | tf_op jit(solution)/shard_map/all_to_all | solution.py:43
  159.4 4.5 %all-to-all-start.3 = ((bf16[8,4,224,128]{3,2,1,0:T(8,128)(2,1)}), bf16[8,4,224,128]{3,2,1,0:T(8,128)(2,1)}, u32[]{:S(2)}, u32[]{:S(2)}) async-start(bf16[8,4,224,128]{3,2,1,0:T(8,128)(2,1)} %bitcast.65), calls=%async_computation.3 | async-start | bytes 3670016 | tf_op jit(solution)/shard_map/all_to_all | solution.py:428
  166.7 2.9 %collective-permute-start.18 = (bf16[960,256]{1,0:T(8,128)(2,1)S(1)}, bf16[960,256]{1,0:T(8,128)(2,1)S(1)}, u32[]{:S(2)}, u32[]{:S(2)}) collective-permute-start(bf16[960,256]{1,0:T(8,128)(2,1)S(1)} %get-tuple-element.21), channel_id=1, source_target_pairs={{0,16},{8,24},{16,0},{24,8},{32,48},{40,56},{48,32},{56,40},{64,80... | collective-permute-start | bytes 1474568 | tf_op jit(solution)/shard_map/ppermute | solution.py:50
  170.7 8.9 %collective-permute-done.17.refs_9_ = bf16[960,256]{1,0:T(8,128)(2,1)S(1)} collective-permute-done((bf16[960,256]{1,0:T(8,128)(2,1)S(1)}, bf16[960,256]{1,0:T(8,128)(2,1)S(1)}, u32[]{:S(2)}, u32[]{:S(2)}) %collective-permute-start.17) | collective-permute-done | bytes 491552 | tf_op jit(solution)/shard_map/ppermute | solution.py:50
  179.5 2.8 %collective-permute-done.18.refs_10_ = bf16[960,256]{1,0:T(8,128)(2,1)S(1)} collective-permute-done((bf16[960,256]{1,0:T(8,128)(2,1)S(1)}, bf16[960,256]{1,0:T(8,128)(2,1)S(1)}, u32[]{:S(2)}, u32[]{:S(2)}) %collective-permute-start.18) | collective-permute-done | bytes 491552 | tf_op jit(solution)/shard_map/ppermute | solution.py:50
  182.3 9.3 %collective-permute-done.19.refs_11_ = bf16[960,256]{1,0:T(8,128)(2,1)S(1)} collective-permute-done((bf16[960,256]{1,0:T(8,128)(2,1)S(1)}, bf16[960,256]{1,0:T(8,128)(2,1)S(1)}, u32[]{:S(2)}, u32[]{:S(2)}) %collective-permute-start.19) | collective-permute-done | bytes 491552 | tf_op jit(solution)/shard_map/ppermute | solution.py:50
  193.2 12.0 %combine.1 = (bf16[512,896]{1,0:T(8,128)(2,1)S(1)}, bf16[512,896]{1,0:T(8,128)(2,1)}) custom-call(s32[9]{0:T(128)S(1)} %copy-done.25, bf16[8,256,128]{2,1,0:T(8,128)(2,1)S(1)} %all-to-all-done.2.a_ref, bf16[128,1024]{1,0:T(8,128)(2,1)S(1)} %collective-permute-done.3.refs_0_, bf16[128,1024]{1,0:T(8,128)(2,1)S(1)} %copy-done.7, ...), custom_call_target="tpu_custom_call" | custom-call | tf_op jit(solution)/shard_map/combine/pallas_call | solution.py:332
  205.4 3.7 %fusion.28 = (f32[4,64]{1,0:T(4,128)S(1)}, bf16[4,64,768]{2,1,0:T(8,128)(2,1)}) fusion(pred[4,768]{1,0:T(4,128)(4,1)S(1)} %iota_compare_fusion, bf16[4,64,576]{2,1,0:T(8,128)(2,1)S(1)} %copy-done.32, bf16[4,768,576]{1,2,0:T(8,128)(2,1)} %param.14), kind=kOutput, calls=%fused_computation.70 | convolution fusion | flops 227672832 | bytes 4231168 | tf_op jit(solution)/shard_map/sub | solution.py:72
  209.1 2.3 add_convert_fusion.3
  211.4 4.4 %collective-permute-start.22 = (bf16[128,896]{1,0:T(8,128)(2,1)}, bf16[128,896]{1,0:T(8,128)(2,1)S(1)}, u32[]{:S(2)}, u32[]{:S(2)}) collective-permute-start(bf16[128,896]{1,0:T(8,128)(2,1)} %get-tuple-element.31), channel_id=1, source_target_pairs={{0,4},{1,5},{2,6},{3,7},{4,0},{5,1},{6,2},{7,3},{8,12},{9,13},{10,... | collective-permute-start | bytes 688136 | tf_op jit(solution)/shard_map/ppermute | solution.py:55
  217.6 3.0 %fusion.10 = bf16[4,64,512]{2,1,0:T(8,128)(2,1)S(1)} fusion(bf16[4,768,576]{1,2,0:T(8,128)(2,1)} %param.14, bf16[4,64,768]{2,1,0:T(8,128)(2,1)S(1)} %copy-done.33, f32[4,64]{1,0:T(4,128)S(1)} %get-tuple-element.36), kind=kOutput, calls=%fused_computation.10 | convolution fusion | flops 201588736 | bytes 3802112 | tf_op jit(solution)/shard_map/rhp,rpc->rhc/dot_general | solution.py:74
  221.5 3.4 %all-to-all-start = ((bf16[4,64,512]{2,0,1:T(4,128)(2,1)}), bf16[4,64,512]{2,0,1:T(4,128)(2,1)S(1)}, u32[]{:S(2)}, u32[]{:S(2)}) async-start(bf16[4,64,512]{2,0,1:T(4,128)(2,1)} %copy.34), calls=%async_computation | async-start | bytes 524288 | tf_op jit(solution)/shard_map/all_to_all | solution.py:510
  224.9 2.0 collective-permute-done.22
  228.3 2.9 %collective-permute-start.25 = (bf16[32,896]{1,0:T(8,128)(2,1)}, bf16[32,896]{1,0:T(8,128)(2,1)S(1)}, u32[]{:S(2)}, u32[]{:S(2)}) collective-permute-start(bf16[32,896]{1,0:T(8,128)(2,1)} %get-tuple-element.35), channel_id=1, source_target_pairs={{0,16},{8,24},{16,0},{24,8},{32,48},{40,56},{48,32},{56,40},{64,80... | collective-permute-start | bytes 172040 | tf_op jit(solution)/shard_map/ppermute | solution.py:50
  231.1 2.0 collective-permute-start.24
  233.2 2.5 dynamic-slice_bitcast_fusion
  235.8 2.1 collective-permute-start.29
  240.7 8.6 %collective-permute-done.28.refs_1_ = bf16[8,224,128]{2,1,0:T(8,128)(2,1)S(1)} collective-permute-done((bf16[8,224,128]{2,1,0:T(8,128)(2,1)}, bf16[8,224,128]{2,1,0:T(8,128)(2,1)S(1)}, u32[]{:S(2)}, u32[]{:S(2)}) %collective-permute-start.28) | collective-permute-done | bytes 458784 | tf_op jit(solution)/shard_map/ppermute | solution.py:50
  251.0 7.6 %collective-permute-done.30.refs_3_ = bf16[8,224,128]{2,1,0:T(8,128)(2,1)S(1)} collective-permute-done((bf16[8,224,128]{2,1,0:T(8,128)(2,1)}, bf16[8,224,128]{2,1,0:T(8,128)(2,1)S(1)}, u32[]{:S(2)}, u32[]{:S(2)}) %collective-permute-start.30) | collective-permute-done | bytes 458784 | tf_op jit(solution)/shard_map/ppermute | solution.py:50
  (146 shorter events, 44.4 us)
Async XLA Ops:
  5.1 14.2 %collective-permute-start.2 = (bf16[32,1024]{1,0:T(8,128)(2,1)S(1)}, bf16[32,1024]{1,0:T(8,128)(2,1)S(1)}, u32[]{:S(2)}, u32[]{:S(2)}) collective-permute-start(bf16[32,1024]{1,0:T(8,128)(2,1)S(1)} %pack_rows.1), channel_id=1, source_target_pairs={{0,24},{8,0},{16,8},{24,16},{32,56},{40,32},{48,40},{56,48},{64,88... | collective-permute-start | bytes 196616 | tf_op jit(solution)/shard_map/ppermute | solution.py:50
  7.4 11.9 %collective-permute-start.1 = (bf16[32,1024]{1,0:T(8,128)(2,1)S(1)}, bf16[32,1024]{1,0:T(8,128)(2,1)S(1)}, u32[]{:S(2)}, u32[]{:S(2)}) collective-permute-start(bf16[32,1024]{1,0:T(8,128)(2,1)S(1)} %pack_rows.1), channel_id=1, source_target_pairs={{0,16},{8,24},{16,0},{24,8},{32,48},{40,56},{48,32},{56,40},{64,80... | collective-permute-start | bytes 196616 | tf_op jit(solution)/shard_map/ppermute | solution.py:50
  8.1 11.2 %collective-permute-start = (bf16[32,1024]{1,0:T(8,128)(2,1)S(1)}, bf16[32,1024]{1,0:T(8,128)(2,1)S(1)}, u32[]{:S(2)}, u32[]{:S(2)}) collective-permute-start(bf16[32,1024]{1,0:T(8,128)(2,1)S(1)} %pack_rows.1), channel_id=1, source_target_pairs={{0,8},{8,16},{16,24},{24,0},{32,40},{40,48},{48,56},{56,32},{64,72... | collective-permute-start | bytes 196616 | tf_op jit(solution)/shard_map/ppermute | solution.py:50
  17.3 30.5 %collective-permute-start.15 = (bf16[896,256]{1,0:T(8,128)(2,1)S(1)}, bf16[896,256]{1,0:T(8,128)(2,1)}, u32[]{:S(2)}, u32[]{:S(2)}) collective-permute-start(bf16[896,256]{1,0:T(8,128)(2,1)S(1)} %get-tuple-element.18), channel_id=1, source_target_pairs={{0,24},{8,0},{16,8},{24,16},{32,56},{40,32},{48,40},{56,48},{64,88... | collective-permute-start | bytes 1376264 | tf_op jit(solution)/shard_map/ppermute | solution.py:50
  17.5 32.1 %collective-permute-start.12 = (bf16[1024,256]{1,0:T(8,128)(2,1)S(1)}, bf16[1024,256]{1,0:T(8,128)(2,1)}, u32[]{:S(2)}, u32[]{:S(2)}) collective-permute-start(bf16[1024,256]{1,0:T(8,128)(2,1)S(1)} %get-tuple-element.16), channel_id=1, source_target_pairs={{0,8},{8,16},{16,24},{24,0},{32,40},{40,48},{48,56},{56,32},{64,72... | collective-permute-start | bytes 1572872 | tf_op jit(solution)/shard_map/ppermute | solution.py:50
  20.0 33.1 %collective-permute-start.4 = (bf16[128,1024]{1,0:T(8,128)(2,1)S(1)}, bf16[128,1024]{1,0:T(8,128)(2,1)S(1)}, u32[]{:S(2)}, u32[]{:S(2)}) collective-permute-start(bf16[128,1024]{1,0:T(8,128)(2,1)S(1)} %collective-permute-done.3.refs_0_), channel_id=1, source_target_pairs={{0,2},{1,3},{2,4},{3,5},{4,6},{5,7},{6,0},{7,1},{8,10},{9,11},{10,... | collective-permute-start | bytes 786440 | tf_op jit(solution)/shard_map/ppermute | solution.py:55
  43.9 16.0 %collective-permute-start.5 = (bf16[128,1024]{1,0:T(8,128)(2,1)S(1)}, bf16[128,1024]{1,0:T(8,128)(2,1)S(1)}, u32[]{:S(2)}, u32[]{:S(2)}) collective-permute-start(bf16[128,1024]{1,0:T(8,128)(2,1)S(1)} %collective-permute-done.3.refs_0_), channel_id=1, source_target_pairs={{0,4},{1,5},{2,6},{3,7},{4,0},{5,1},{6,2},{7,3},{8,12},{9,13},{10,... | collective-permute-start | bytes 786440 | tf_op jit(solution)/shard_map/ppermute | solution.py:55
  47.5 35.0 %collective-permute-start.11 = (bf16[1920,256]{1,0:T(8,128)(2,1)}, bf16[1920,256]{1,0:T(8,128)(2,1)}, u32[]{:S(2)}, u32[]{:S(2)}) collective-permute-start(bf16[1920,256]{1,0:T(8,128)(2,1)} %get-tuple-element.15), channel_id=1, source_target_pairs={{0,8},{8,16},{16,24},{24,0},{32,40},{40,48},{48,56},{56,32},{64,72... | collective-permute-start | bytes 2949128 | tf_op jit(solution)/shard_map/ppermute | solution.py:50
  47.8 34.7 %collective-permute-start.14 = (bf16[1920,256]{1,0:T(8,128)(2,1)}, bf16[1920,256]{1,0:T(8,128)(2,1)}, u32[]{:S(2)}, u32[]{:S(2)}) collective-permute-start(bf16[1920,256]{1,0:T(8,128)(2,1)} %get-tuple-element.17), channel_id=1, source_target_pairs={{0,24},{8,0},{16,8},{24,16},{32,56},{40,32},{48,40},{56,48},{64,88... | collective-permute-start | bytes 2949128 | tf_op jit(solution)/shard_map/ppermute | solution.py:50
  49.6 10.3 %collective-permute-start.6 = (bf16[128,1024]{1,0:T(8,128)(2,1)S(1)}, bf16[128,1024]{1,0:T(8,128)(2,1)S(1)}, u32[]{:S(2)}, u32[]{:S(2)}) collective-permute-start(bf16[128,1024]{1,0:T(8,128)(2,1)S(1)} %collective-permute-done.3.refs_0_), channel_id=1, source_target_pairs={{0,6},{1,7},{2,0},{3,1},{4,2},{5,3},{6,4},{7,5},{8,14},{9,15},{10,... | collective-permute-start | bytes 786440 | tf_op jit(solution)/shard_map/ppermute | solution.py:55
  53.1 7.3 %collective-permute-start.7 = (bf16[128,1024]{1,0:T(8,128)(2,1)S(1)}, bf16[128,1024]{1,0:T(8,128)(2,1)S(1)}, u32[]{:S(2)}, u32[]{:S(2)}) collective-permute-start(bf16[128,1024]{1,0:T(8,128)(2,1)S(1)} %collective-permute-done.3.refs_0_), channel_id=1, source_target_pairs={{0,1},{1,0},{2,3},{3,2},{4,5},{5,4},{6,7},{7,6},{8,9},{9,8},{10,11... | collective-permute-start | bytes 786440 | tf_op jit(solution)/shard_map/ppermute | solution.py:59
  60.4 22.3 %collective-permute-start.13 = (bf16[1024,256]{1,0:T(8,128)(2,1)}, bf16[1024,256]{1,0:T(8,128)(2,1)}, u32[]{:S(2)}, u32[]{:S(2)}) collective-permute-start(bf16[1024,256]{1,0:T(8,128)(2,1)} %collective-permute-done.12), channel_id=1, source_target_pairs={{0,8},{8,16},{16,24},{24,0},{32,40},{40,48},{48,56},{56,32},{64,72... | collective-permute-start | bytes 1572872 | tf_op jit(solution)/shard_map/ppermute | solution.py:50
  61.4 21.1 %collective-permute-start.16 = (bf16[896,256]{1,0:T(8,128)(2,1)}, bf16[896,256]{1,0:T(8,128)(2,1)}, u32[]{:S(2)}, u32[]{:S(2)}) collective-permute-start(bf16[896,256]{1,0:T(8,128)(2,1)} %collective-permute-done.15), channel_id=1, source_target_pairs={{0,24},{8,0},{16,8},{24,16},{32,56},{40,32},{48,40},{56,48},{64,88... | collective-permute-start | bytes 1376264 | tf_op jit(solution)/shard_map/ppermute | solution.py:50
  62.5 2.7 %collective-permute-start.10 = (bf16[128,1024]{1,0:T(8,128)(2,1)S(1)}, bf16[128,1024]{1,0:T(8,128)(2,1)S(1)}, u32[]{:S(2)}, u32[]{:S(2)}) collective-permute-start(bf16[128,1024]{1,0:T(8,128)(2,1)S(1)} %collective-permute-done.6.refs_3_), channel_id=1, source_target_pairs={{0,1},{1,0},{2,3},{3,2},{4,5},{5,4},{6,7},{7,6},{8,9},{9,8},{10,11... | collective-permute-start | bytes 786440 | tf_op jit(solution)/shard_map/ppermute | solution.py:59
  101.5 33.3 %all-to-all-start.1 = ((bf16[8,528,128]{2,1,0:T(8,128)(2,1)}), bf16[8,528,128]{2,1,0:T(8,128)(2,1)}, u32[]{:S(2)}, u32[]{:S(2)}) async-start(bf16[8,528,128]{2,1,0:T(8,128)(2,1)} %project.1), calls=%async_computation.1 | async-start | bytes 2162688 | tf_op jit(solution)/shard_map/all_to_all | solution.py:43
  138.0 21.4 %all-to-all-start.2 = ((bf16[8,256,128]{2,1,0:T(8,128)(2,1)}), bf16[8,256,128]{2,1,0:T(8,128)(2,1)S(1)}, u32[]{:S(2)}, u32[]{:S(2)}) async-start(bf16[8,256,128]{2,1,0:T(8,128)(2,1)} %copy-done.3), calls=%async_computation.2 | async-start | bytes 1048576 | tf_op jit(solution)/shard_map/all_to_all | solution.py:43
  159.4 62.1 %all-to-all-start.3 = ((bf16[8,4,224,128]{3,2,1,0:T(8,128)(2,1)}), bf16[8,4,224,128]{3,2,1,0:T(8,128)(2,1)}, u32[]{:S(2)}, u32[]{:S(2)}) async-start(bf16[8,4,224,128]{3,2,1,0:T(8,128)(2,1)} %bitcast.65), calls=%async_computation.3 | async-start | bytes 3670016 | tf_op jit(solution)/shard_map/all_to_all | solution.py:428
  165.3 14.2 %collective-permute-start.17 = (bf16[960,256]{1,0:T(8,128)(2,1)S(1)}, bf16[960,256]{1,0:T(8,128)(2,1)S(1)}, u32[]{:S(2)}, u32[]{:S(2)}) collective-permute-start(bf16[960,256]{1,0:T(8,128)(2,1)S(1)} %get-tuple-element.20), channel_id=1, source_target_pairs={{0,8},{8,16},{16,24},{24,0},{32,40},{40,48},{48,56},{56,32},{64,72... | collective-permute-start | bytes 1474568 | tf_op jit(solution)/shard_map/ppermute | solution.py:50
  166.7 15.6 %collective-permute-start.18 = (bf16[960,256]{1,0:T(8,128)(2,1)S(1)}, bf16[960,256]{1,0:T(8,128)(2,1)S(1)}, u32[]{:S(2)}, u32[]{:S(2)}) collective-permute-start(bf16[960,256]{1,0:T(8,128)(2,1)S(1)} %get-tuple-element.21), channel_id=1, source_target_pairs={{0,16},{8,24},{16,0},{24,8},{32,48},{40,56},{48,32},{56,40},{64,80... | collective-permute-start | bytes 1474568 | tf_op jit(solution)/shard_map/ppermute | solution.py:50
  169.5 22.0 %collective-permute-start.19 = (bf16[960,256]{1,0:T(8,128)(2,1)S(1)}, bf16[960,256]{1,0:T(8,128)(2,1)S(1)}, u32[]{:S(2)}, u32[]{:S(2)}) collective-permute-start(bf16[960,256]{1,0:T(8,128)(2,1)S(1)} %get-tuple-element.22), channel_id=1, source_target_pairs={{0,24},{8,0},{16,8},{24,16},{32,56},{40,32},{48,40},{56,48},{64,88... | collective-permute-start | bytes 1474568 | tf_op jit(solution)/shard_map/ppermute | solution.py:50
  205.2 3.9 %collective-permute-start.20 = (bf16[512,896]{1,0:T(8,128)(2,1)}, bf16[512,896]{1,0:T(8,128)(2,1)}, u32[]{:S(2)}, u32[]{:S(2)}) collective-permute-start(bf16[512,896]{1,0:T(8,128)(2,1)} %get-tuple-element.24), channel_id=1, source_target_pairs={{0,1},{1,0},{2,3},{3,2},{4,5},{5,4},{6,7},{7,6},{8,9},{9,8},{10,11... | collective-permute-start | bytes 2752520 | tf_op jit(solution)/shard_map/ppermute | solution.py:59
  211.4 13.4 %collective-permute-start.23 = (bf16[128,896]{1,0:T(8,128)(2,1)}, bf16[128,896]{1,0:T(8,128)(2,1)S(1)}, u32[]{:S(2)}, u32[]{:S(2)}) collective-permute-start(bf16[128,896]{1,0:T(8,128)(2,1)} %get-tuple-element.30), channel_id=1, source_target_pairs={{0,2},{1,3},{2,4},{3,5},{4,6},{5,7},{6,0},{7,1},{8,10},{9,11},{10,... | collective-permute-start | bytes 688136 | tf_op jit(solution)/shard_map/ppermute | solution.py:55
  211.4 15.4 %collective-permute-start.22 = (bf16[128,896]{1,0:T(8,128)(2,1)}, bf16[128,896]{1,0:T(8,128)(2,1)S(1)}, u32[]{:S(2)}, u32[]{:S(2)}) collective-permute-start(bf16[128,896]{1,0:T(8,128)(2,1)} %get-tuple-element.31), channel_id=1, source_target_pairs={{0,4},{1,5},{2,6},{3,7},{4,0},{5,1},{6,2},{7,3},{8,12},{9,13},{10,... | collective-permute-start | bytes 688136 | tf_op jit(solution)/shard_map/ppermute | solution.py:55
  215.9 11.0 %collective-permute-start.21 = (bf16[128,896]{1,0:T(8,128)(2,1)S(1)}, bf16[128,896]{1,0:T(8,128)(2,1)S(1)}, u32[]{:S(2)}, u32[]{:S(2)}) collective-permute-start(bf16[128,896]{1,0:T(8,128)(2,1)S(1)} %get-tuple-element.32), channel_id=1, source_target_pairs={{0,6},{1,7},{2,0},{3,1},{4,2},{5,3},{6,4},{7,5},{8,14},{9,15},{10,... | collective-permute-start | bytes 688136 | tf_op jit(solution)/shard_map/ppermute | solution.py:55
  221.5 16.5 %all-to-all-start = ((bf16[4,64,512]{2,0,1:T(4,128)(2,1)}), bf16[4,64,512]{2,0,1:T(4,128)(2,1)S(1)}, u32[]{:S(2)}, u32[]{:S(2)}) async-start(bf16[4,64,512]{2,0,1:T(4,128)(2,1)} %copy.34), calls=%async_computation | async-start | bytes 524288 | tf_op jit(solution)/shard_map/all_to_all | solution.py:510
  227.7 10.2 %collective-permute-start.26 = (bf16[32,896]{1,0:T(8,128)(2,1)S(1)}, bf16[32,896]{1,0:T(8,128)(2,1)S(1)}, u32[]{:S(2)}, u32[]{:S(2)}) collective-permute-start(bf16[32,896]{1,0:T(8,128)(2,1)S(1)} %get-tuple-element.34), channel_id=1, source_target_pairs={{0,8},{8,16},{16,24},{24,0},{32,40},{40,48},{48,56},{56,32},{64,72... | collective-permute-start | bytes 172040 | tf_op jit(solution)/shard_map/ppermute | solution.py:50
  228.3 9.8 %collective-permute-start.25 = (bf16[32,896]{1,0:T(8,128)(2,1)}, bf16[32,896]{1,0:T(8,128)(2,1)S(1)}, u32[]{:S(2)}, u32[]{:S(2)}) collective-permute-start(bf16[32,896]{1,0:T(8,128)(2,1)} %get-tuple-element.35), channel_id=1, source_target_pairs={{0,16},{8,24},{16,0},{24,8},{32,48},{40,56},{48,32},{56,40},{64,80... | collective-permute-start | bytes 172040 | tf_op jit(solution)/shard_map/ppermute | solution.py:50
  231.1 7.0 %collective-permute-start.24 = (bf16[32,896]{1,0:T(8,128)(2,1)}, bf16[32,896]{1,0:T(8,128)(2,1)}, u32[]{:S(2)}, u32[]{:S(2)}) collective-permute-start(bf16[32,896]{1,0:T(8,128)(2,1)} %get-tuple-element.33), channel_id=1, source_target_pairs={{0,24},{8,0},{16,8},{24,16},{32,56},{40,32},{48,40},{56,48},{64,88... | collective-permute-start | bytes 172040 | tf_op jit(solution)/shard_map/ppermute | solution.py:50
  235.7 13.6 %collective-permute-start.28 = (bf16[8,224,128]{2,1,0:T(8,128)(2,1)}, bf16[8,224,128]{2,1,0:T(8,128)(2,1)S(1)}, u32[]{:S(2)}, u32[]{:S(2)}) collective-permute-start(bf16[8,224,128]{2,1,0:T(8,128)(2,1)} %get-tuple-element.27), channel_id=1, source_target_pairs={{0,8},{8,16},{16,24},{24,0},{32,40},{40,48},{48,56},{56,32},{64,72... | collective-permute-start | bytes 1376264 | tf_op jit(solution)/shard_map/ppermute | solution.py:50
  235.8 15.2 %collective-permute-start.29 = (bf16[8,224,128]{2,1,0:T(8,128)(2,1)}, bf16[8,224,128]{2,1,0:T(8,128)(2,1)S(1)}, u32[]{:S(2)}, u32[]{:S(2)}) collective-permute-start(bf16[8,224,128]{2,1,0:T(8,128)(2,1)} %get-tuple-element.26), channel_id=1, source_target_pairs={{0,16},{8,24},{16,0},{24,8},{32,48},{40,56},{48,32},{56,40},{64,80... | collective-permute-start | bytes 1376264 | tf_op jit(solution)/shard_map/ppermute | solution.py:50
  237.8 20.7 %collective-permute-start.30 = (bf16[8,224,128]{2,1,0:T(8,128)(2,1)}, bf16[8,224,128]{2,1,0:T(8,128)(2,1)S(1)}, u32[]{:S(2)}, u32[]{:S(2)}) collective-permute-start(bf16[8,224,128]{2,1,0:T(8,128)(2,1)} %get-tuple-element.25), channel_id=1, source_target_pairs={{0,24},{8,0},{16,8},{24,16},{32,56},{40,32},{48,40},{56,48},{64,88... | collective-permute-start | bytes 1376264 | tf_op jit(solution)/shard_map/ppermute | solution.py:50
  239.1 20.7 %collective-permute-start.27 = (bf16[32,896]{1,0:T(8,128)(2,1)S(1)}, bf16[32,896]{1,0:T(8,128)(2,1)S(1)}, u32[]{:S(2)}, u32[]{:S(2)}) collective-permute-start(bf16[32,896]{1,0:T(8,128)(2,1)S(1)} %add_convert_fusion.4), channel_id=1, source_target_pairs={{0,0},{1,32},{2,64},{3,96},{4,128},{5,160},{6,192},{7,224},{8,8},{... | collective-permute-start | bytes 172040 | tf_op jit(solution)/shard_map/ppermute | solution.py:39
  (37 other events, 828.5 us)

commit v4 on v3

--- a/solution.py
+++ b/solution.py
@@ -179,7 +179,9 @@
     pick = (iota((128, TOP * 128), 0) - META == col // 128).astype(F32).astype(BF)
     spread = jnp.dot(meta, pick, preferred_element_type=F32)
     half = (iota((1, TOP * 128), 1) % 128 // 64).astype(F32)
-    id_ref[...] = (spread - half).astype(BF)
+    tags = (spread - half).astype(BF)
+    for j in range(TOP):
+        id_ref[j] = tags[:, j * 128 : (j + 1) * 128]
     xs = []
     for s in range(NX):
         lane = pl.multiple_of((z_ref[NZ] + NX - s) % NX * GL, GL)
@@ -198,17 +200,19 @@
                 preferred_element_type=F32,
             )
             total = part if total is None else total + part
-        y_ref[:, start : start + size] = total.astype(BF)
+        total = total.astype(BF)
+        for n in range(size // 128):
+            y_ref[start // 128 + n] = total[:, n * 128 : (n + 1) * 128]
     low_half = iota((16, 128), 1) < 64
 
     def body(s, carry):
         r = pl.multiple_of(s * 16, 16)
         z = z_ref[s // 8]
         rr = pl.multiple_of((s % 8) * 16, 16)
-        ids = [id_ref[pl.ds(r, 16), j * 128 : (j + 1) * 128] for j in range(TOP)]
+        ids = [id_ref[j, pl.ds(r, 16), :] for j in range(TOP)]
         kept = [jnp.zeros((16, 128), BF) for _ in range(TOP)]
         for tile in range(NE // 2):
-            y = y_ref[pl.ds(r, 16), tile * 128 : (tile + 1) * 128]
+            y = y_ref[tile, pl.ds(r, 16), :]
             for j in range(TOP):
                 kept[j] = jnp.where(ids[j] == jnp.asarray(2.0 * tile, BF), y, kept[j])
         for q in range(TOP // 2):
@@ -219,7 +223,7 @@
             p_ref[z, pl.ds(q * ZR + rr, 16), :] = jnp.where(low_half, a, b).astype(BF)
         return carry
 
-    lax.fori_loop(0, ROWS // 16, body, 0)
+    lax.fori_loop(0, ROWS // 16, body, 0, unroll=4)
     for n in range(NZ):
         turned = jnp.transpose(x_refs[n][:, 128:256].astype(F32))
         p_ref[z_ref[n], PR:PB, :] = turned[112:128].astype(BF)
@@ -231,8 +235,8 @@
         in_specs=[SMEM] + [VMEM] * (NZ + 5),
         out_shape=jax.ShapeDtypeStruct((NZ, PB, 128), BF),
         scratch_shapes=[
-            pltpu.VMEM((ROWS, TOP * 128), BF),
-            pltpu.VMEM((ROWS, NE * 2 * FX), BF),
+            pltpu.VMEM((TOP, ROWS, 128), BF),
+            pltpu.VMEM((NE // 2, ROWS, 128), BF),
         ],
         compiler_params=pltpu.CompilerParams(vmem_limit_bytes=32 << 20),
         name="project",
@@ -281,12 +285,11 @@
     )(parts, meta)
 
 
-def combine_body(z_ref, a_ref, *refs):
-    x_refs, d_refs = refs[:NZ], refs[NZ : NZ + NX]
-    near_ref, far_ref, id_ref, wide_ref, d_ref = refs[NZ + NX :]
+def combine_body(z_ref, a_ref, m_ref, *refs):
+    d_refs = refs[:NX]
+    near_ref, far_ref, id_ref, wide_ref, d_ref = refs[NX:]
     for s in range(NX):
         d_ref[(z_ref[NZ] + NX - s) % NX] = d_refs[s][...]
-    meta = jnp.concatenate([x[:, 128:256] for x in x_refs], axis=0)
     row = iota((128, TOP * 128), 0) - META
     col = iota((128, TOP * 128), 1)
     q = col // 512
@@ -294,14 +297,16 @@
     block = col % 128 // FX
     origin = (block - k + 4) % 4
     j = 4 * q + jnp.where(origin == 1, 2, jnp.where(origin == 2, 1, origin))
-    spread = jnp.dot(meta, (row == j).astype(F32).astype(BF), preferred_element_type=F32)
-    id_ref[...] = (spread - (iota((1, TOP * 128), 1) % 128 // FX).astype(F32)).astype(BF)
+    spread = jnp.dot(m_ref[...], (row == j).astype(F32).astype(BF), preferred_element_type=F32)
+    tags = (spread - (iota((1, TOP * 128), 1) % 128 // FX).astype(F32)).astype(BF)
+    for n in range(TOP):
+        id_ref[n] = tags[:, n * 128 : (n + 1) * 128]
 
     def body(s, carry):
         r = pl.multiple_of(s * 16, 16)
         z = z_ref[s // 8]
         rr = pl.multiple_of((s % 8) * 16, 16)
-        ids = [id_ref[pl.ds(r, 16), n * 128 : (n + 1) * 128] for n in range(TOP)]
+        ids = [id_ref[n, pl.ds(r, 16), :] for n in range(TOP)]
         turned = []
         for n in range(2):
             a = a_ref[z, pl.ds(n * ZR + rr, 16), :].astype(F32)
@@ -312,36 +317,40 @@
             kept = jnp.zeros((16, 128), BF)
             for n in range(TOP):
                 kept = jnp.where(ids[n] == jnp.asarray(4.0 * g, BF), turned[n], kept)
-            wide_ref[pl.ds(r, 16), g * 128 : (g + 1) * 128] = kept
+            wide_ref[g, pl.ds(r, 16), :] = kept
         return carry
 
-    lax.fori_loop(0, ROWS // 16, body, 0)
+    lax.fori_loop(0, ROWS // 16, body, 0, unroll=4)
     for x in range(NX):
-        out = lax.dot_general(
-            wide_ref[:, : NE * FX],
-            d_ref[x],
-            (((1,), (0,)), ((), ())),
-            preferred_element_type=F32,
-        )
+        out = None
+        for g in range(0, 8, 2):
+            width = min(256, NE * FX - g * 128)
+            wide = jnp.concatenate([wide_ref[g], wide_ref[g + 1]], axis=1)
+            part = jnp.dot(
+                wide[:, :width],
+                d_ref[x, g * 128 : g * 128 + width],
+                preferred_element_type=F32,
+            )
+            out = part if out is None else out + part
         out = out[:, :SLICE].astype(BF)
         near_ref[:, x * SLICE : (x + 1) * SLICE] = out[: ROWS // 2]
         far_ref[:, x * SLICE : (x + 1) * SLICE] = out[ROWS // 2 :]
 
 
-def combine(blocks, acts, rows, down):
+def combine(blocks, acts, metas, down):
     return pl.pallas_call(
         combine_body,
-        in_specs=[SMEM] + [VMEM] * (NZ + 1 + NX),
+        in_specs=[SMEM] + [VMEM] * (2 + NX),
         out_specs=[VMEM] * 2,
         out_shape=[jax.ShapeDtypeStruct((ROWS // 2, WIDE), BF)] * 2,
         scratch_shapes=[
-            pltpu.VMEM((ROWS, TOP * 128), BF),
-            pltpu.VMEM((ROWS, 1024), BF),
+            pltpu.VMEM((TOP, ROWS, 128), BF),
+            pltpu.VMEM((8, ROWS, 128), BF),
             pltpu.VMEM((NX, NE * FX, GL), BF),
         ],
         compiler_params=pltpu.CompilerParams(vmem_limit_bytes=28 << 20),
         name="combine",
-    )(blocks, acts, *rows, *down)
+    )(blocks, acts, metas, *down)
 
 
 def pack_body(h_ref, n_ref, e_ref, r_ref, l_ref, o_ref):
@@ -411,17 +420,9 @@
 
 
 def place_body(own_ref, *refs):
-    pieces, (out_ref, sems) = refs[:NX], refs[NX:]
-    copies = [
-        pltpu.make_async_copy(
-            pieces[s], out_ref.at[:, (own_ref[0] + NX - s) % NX], sems.at[s]
-        )
-        for s in range(NX)
-    ]
-    for copy in copies:
-        copy.start()
-    for copy in copies:
-        copy.wait()
+    pieces, (out_ref,) = refs[:NX], refs[NX:]
+    for s in range(NX):
+        out_ref[:, (own_ref[0] + NX - s) % NX] = pieces[s][...]
 
 
 def move_gate(chosen, own):
@@ -438,14 +439,12 @@
         lax.dynamic_index_in_dim(came, (x + s) % NX, 1, keepdims=False) for s in range(NX)
     ]
     pieces = [pieces[0]] + [shift_x(pieces[s], s) for s in range(1, NX)]
-    anywhere = pl.BlockSpec(memory_space=pl.ANY)
     return pl.pallas_call(
         place_body,
-        in_specs=[SMEM] + [anywhere] * NX,
-        out_specs=anywhere,
+        in_specs=[SMEM] + [VMEM] * NX,
+        out_specs=VMEM,
         out_shape=jax.ShapeDtypeStruct((NZ, NX, SLICE, FT), BF),
-        scratch_shapes=[pltpu.SemaphoreType.DMA((NX,))],
-        compiler_params=pltpu.CompilerParams(vmem_limit_bytes=1 << 20),
+        compiler_params=pltpu.CompilerParams(vmem_limit_bytes=8 << 20),
         name="place_gate",
     )(own, *pieces).reshape(1, DIM, FT)
 
@@ -502,7 +501,7 @@
     metas = jnp.stack([block[:, 128:256] for block in rows])
     meta = lax.dynamic_index_in_dim(metas, places[z], 0, keepdims=False)
     acts = exchange(activate(parts, meta), Z_GROUPS)
-    near, far = combine(blocks, acts, rows, held_down)
+    near, far = combine(blocks, acts, metas.reshape(ROWS, 128), held_down)
     far = other_core(far)
     moe_out = gather_out(near, far)
 

time: 262 us -> 253 us (0.966)
  Pallas kernels: 37.5 us -> 30.8 us
  waiting for transfers between devices: 108 us -> 103 us
  local copies, waits for them, and re-layouts: 24.9 us -> 27.8 us
    pallas_call x2, Pallas kernels: 13.2 us -> 9.51 us  [the longest x1 8.15 us: combine(): pl.pallas_call(combine_body, in_specs=[SMEM] + [VMEM] * (2 + NX), out_spe...]
    pallas_call x1, Pallas kernels: 17 us -> 13.3 us  [project(): pl.pallas_call(project_body, in_specs=[SMEM] + [VMEM] * (NZ + 5), out_sha...]
    unnamed x78 -> x54, local copies, waits for them, and re-layouts: 15.7 us -> 19.3 us
  transfers between devices with their start and end apart: 35 -> 35, of which waited for: 14 -> 13; matrix products, arithmetic and copies ran while one was open for 9% -> 10% of each run, Pallas kernels for 7% -> 6%
where the time goes in v4:
time: 253 us; the launch traced here: 252 us
  waiting for transfers between devices  103 us (41%)
  starting transfers between devices  75.1 us (30%)
  Pallas kernels  30.8 us (12%)
  local copies, waits for them, and re-layouts  27.8 us (11%)
  matrix products  7.01 us (3%)
  other arithmetic  5.12 us (2%)
  between operations  2.83 us (1%)
    ppermute x18, waiting for transfers between devices, shift_x(): return lax.ppermute(value, 'expert', pairs)  54 us
    all_to_all x2, waiting for transfers between devices, exchange(): lax.all_to_all(value, 'expert', split_axis=0, concat_axis=0, tiled=True,...  37.1 us
    ppermute x6, starting transfers between devices, shift_y(): return lax.ppermute(value, 'tensor', pairs)  33.6 us
    ppermute x18, starting transfers between devices, shift_x(): return lax.ppermute(value, 'expert', pairs)  23.8 us
    unnamed x54, local copies, waits for them, and re-layouts  19.3 us
    pallas_call x1, Pallas kernels, project(): pl.pallas_call(project_body, in_specs=[SMEM] + [VMEM] * (NZ + 5), out_sha...  13.3 us
    ppermute x6, waiting for transfers between devices, shift_y(): return lax.ppermute(value, 'tensor', pairs)  11.7 us
    pallas_call x1, Pallas kernels, combine(): pl.pallas_call(combine_body, in_specs=[SMEM] + [VMEM] * (2 + NX), out_spe...  8.15 us
  transfers between devices with their start and end apart: 35, of which 13 were waited for; matrix products, arithmetic and copies ran while one was open for 10% of the time, Pallas kernels for 6%

profile of v4, /device:TPU:2, one launch (start us, length us, event | category | flops | bytes accessed | tf_op | source)
XLA Modules:
  0.0 251.5 jit_solution(4921087684650621724)
XLA Ops:
  5.1 2.3 collective-permute-start.2
  12.9 3.4 %turn_gate_up.1 = (bf16[1920,256]{1,0:T(8,128)(2,1)S(1)}, bf16[1920,256]{1,0:T(8,128)(2,1)}, bf16[1024,256]{1,0:T(8,128)(2,1)S(1)}, bf16[1920,256]{1,0:T(8,128)(2,1)}, bf16[896,256]{1,0:T(8,128)(2,1)S(1)}) custom-call(s32[1]{0:T(128)} %bitcast.3.own_ref, bf16[30,224,128]{2,1,0:T(8,128)(2,1)S(1)} %copy-done.1, bf16[30,224,128]{2,1,0:T(8,128)(2,1)S(1)} %copy-done.4), custom_call_target="tpu_custom_call" | custom-call | tf_op jit(solution)/shard_map/turn_gate_up/pallas_call | solution.py:145
  16.5 1.8 collective-permute-start.12
  19.1 23.8 %collective-permute-start.4 = (bf16[128,1024]{1,0:T(8,128)(2,1)S(1)}, bf16[128,1024]{1,0:T(8,128)(2,1)S(1)}, u32[]{:S(2)}, u32[]{:S(2)}) collective-permute-start(bf16[128,1024]{1,0:T(8,128)(2,1)S(1)} %collective-permute-done.3.refs_0_), channel_id=1, source_target_pairs={{0,2},{1,3},{2,4},{3,5},{4,6},{5,7},{6,0},{7,1},{8,10},{9,11},{10,... | collective-permute-start | bytes 786440 | tf_op jit(solution)/shard_map/ppermute | solution.py:55
  42.9 3.7 %collective-permute-start.5 = (bf16[128,1024]{1,0:T(8,128)(2,1)S(1)}, bf16[128,1024]{1,0:T(8,128)(2,1)}, u32[]{:S(2)}, u32[]{:S(2)}) collective-permute-start(bf16[128,1024]{1,0:T(8,128)(2,1)S(1)} %collective-permute-done.3.refs_0_), channel_id=1, source_target_pairs={{0,4},{1,5},{2,6},{3,7},{4,0},{5,1},{6,2},{7,3},{8,12},{9,13},{10,... | collective-permute-start | bytes 786440 | tf_op jit(solution)/shard_map/ppermute | solution.py:55
  48.6 3.5 %collective-permute-done.4.refs_1_ = bf16[128,1024]{1,0:T(8,128)(2,1)S(1)} collective-permute-done((bf16[128,1024]{1,0:T(8,128)(2,1)S(1)}, bf16[128,1024]{1,0:T(8,128)(2,1)S(1)}, u32[]{:S(2)}, u32[]{:S(2)}) %collective-permute-start.4) | collective-permute-done | bytes 262176 | tf_op jit(solution)/shard_map/ppermute | solution.py:55
  52.8 6.2 %collective-permute-done.5.refs_2_ = bf16[128,1024]{1,0:T(8,128)(2,1)} collective-permute-done((bf16[128,1024]{1,0:T(8,128)(2,1)S(1)}, bf16[128,1024]{1,0:T(8,128)(2,1)}, u32[]{:S(2)}, u32[]{:S(2)}) %collective-permute-start.5) | collective-permute-done | bytes 262176 | tf_op jit(solution)/shard_map/ppermute | solution.py:55
  66.3 15.2 %collective-permute-done.16.refs_12_ = bf16[896,256]{1,0:T(8,128)(2,1)} collective-permute-done((bf16[896,256]{1,0:T(8,128)(2,1)}, bf16[896,256]{1,0:T(8,128)(2,1)}, u32[]{:S(2)}, u32[]{:S(2)}) %collective-permute-start.16) | collective-permute-done | bytes 458784 | tf_op jit(solution)/shard_map/ppermute | solution.py:50
  85.5 13.3 %project.1 = bf16[8,528,128]{2,1,0:T(8,128)(2,1)} custom-call(s32[9]{0:T(128)S(1)} %pad_add_fusion.z_ref, bf16[128,1024]{1,0:T(8,128)(2,1)S(1)} %copy-done.6, bf16[128,1024]{1,0:T(8,128)(2,1)S(1)} %copy-done.8, bf16[128,1024]{1,0:T(8,128)(2,1)} %collective-permute-done.5.refs_2_, bf16[128,1024]{1,0:T(8,128)(2,1)} %collective-permute-done.6.refs_3_, ...), custom_call_target="tpu_custom_call" | custom-call | tf_op jit(solution)/shard_map/project/pallas_call | solution.py:233
  98.8 4.3 %all-to-all-start.1 = ((bf16[8,528,128]{2,1,0:T(8,128)(2,1)}), bf16[8,528,128]{2,1,0:T(8,128)(2,1)}, u32[]{:S(2)}, u32[]{:S(2)}) async-start(bf16[8,528,128]{2,1,0:T(8,128)(2,1)} %project.1), calls=%async_computation.1 | async-start | bytes 2162688 | tf_op jit(solution)/shard_map/all_to_all | solution.py:43
  109.3 22.9 %all-to-all-done.1.p_ref = bf16[8,528,128]{2,1,0:T(8,128)(2,1)} async-done(((bf16[8,528,128]{2,1,0:T(8,128)(2,1)}), bf16[8,528,128]{2,1,0:T(8,128)(2,1)}, u32[]{:S(2)}, u32[]{:S(2)}) %all-to-all-start.1) | async-done | bytes 1081376 | tf_op jit(solution)/shard_map/all_to_all | solution.py:43
  132.2 2.4 activate.1
  134.6 3.5 %all-to-all-start.2 = ((bf16[8,256,128]{2,1,0:T(8,128)(2,1)}), bf16[8,256,128]{2,1,0:T(8,128)(2,1)S(1)}, u32[]{:S(2)}, u32[]{:S(2)}) async-start(bf16[8,256,128]{2,1,0:T(8,128)(2,1)} %activate.1), calls=%async_computation.2 | async-start | bytes 1048576 | tf_op jit(solution)/shard_map/all_to_all | solution.py:43
  139.5 2.1 gather_fusion
  141.7 14.3 %all-to-all-done.2.a_ref = bf16[8,256,128]{2,1,0:T(8,128)(2,1)S(1)} async-done(((bf16[8,256,128]{2,1,0:T(8,128)(2,1)}), bf16[8,256,128]{2,1,0:T(8,128)(2,1)S(1)}, u32[]{:S(2)}, u32[]{:S(2)}) %all-to-all-start.2) | async-done | bytes 524320 | tf_op jit(solution)/shard_map/all_to_all | solution.py:43
  156.0 4.4 %all-to-all-start.3 = ((bf16[8,4,224,128]{3,2,1,0:T(8,128)(2,1)}), bf16[8,4,224,128]{3,2,1,0:T(8,128)(2,1)}, u32[]{:S(2)}, u32[]{:S(2)}) async-start(bf16[8,4,224,128]{3,2,1,0:T(8,128)(2,1)} %bitcast.67), calls=%async_computation.3 | async-start | bytes 3670016 | tf_op jit(solution)/shard_map/all_to_all | solution.py:429
  163.2 2.8 %collective-permute-start.18 = (bf16[960,256]{1,0:T(8,128)(2,1)S(1)}, bf16[960,256]{1,0:T(8,128)(2,1)S(1)}, u32[]{:S(2)}, u32[]{:S(2)}) collective-permute-start(bf16[960,256]{1,0:T(8,128)(2,1)S(1)} %get-tuple-element.21), channel_id=1, source_target_pairs={{0,16},{8,24},{16,0},{24,8},{32,48},{40,56},{48,32},{56,40},{64,80... | collective-permute-start | bytes 1474568 | tf_op jit(solution)/shard_map/ppermute | solution.py:50
  167.2 8.8 %collective-permute-done.17.refs_1_ = bf16[960,256]{1,0:T(8,128)(2,1)S(1)} collective-permute-done((bf16[960,256]{1,0:T(8,128)(2,1)S(1)}, bf16[960,256]{1,0:T(8,128)(2,1)S(1)}, u32[]{:S(2)}, u32[]{:S(2)}) %collective-permute-start.17) | collective-permute-done | bytes 491552 | tf_op jit(solution)/shard_map/ppermute | solution.py:50
  176.0 2.8 %collective-permute-done.18.refs_2_ = bf16[960,256]{1,0:T(8,128)(2,1)S(1)} collective-permute-done((bf16[960,256]{1,0:T(8,128)(2,1)S(1)}, bf16[960,256]{1,0:T(8,128)(2,1)S(1)}, u32[]{:S(2)}, u32[]{:S(2)}) %collective-permute-start.18) | collective-permute-done | bytes 491552 | tf_op jit(solution)/shard_map/ppermute | solution.py:50
  178.8 9.3 %collective-permute-done.19.refs_3_ = bf16[960,256]{1,0:T(8,128)(2,1)S(1)} collective-permute-done((bf16[960,256]{1,0:T(8,128)(2,1)S(1)}, bf16[960,256]{1,0:T(8,128)(2,1)S(1)}, u32[]{:S(2)}, u32[]{:S(2)}) %collective-permute-start.19) | collective-permute-done | bytes 491552 | tf_op jit(solution)/shard_map/ppermute | solution.py:50
  188.7 8.2 %combine.1 = (bf16[512,896]{1,0:T(8,128)(2,1)S(1)}, bf16[512,896]{1,0:T(8,128)(2,1)}) custom-call(s32[9]{0:T(128)S(1)} %copy-done.15, bf16[8,256,128]{2,1,0:T(8,128)(2,1)S(1)} %all-to-all-done.2.a_ref, bf16[1024,128]{1,0:T(8,128)(2,1)S(1)} %bitcast.65, bf16[960,256]{1,0:T(8,128)(2,1)S(1)} %get-tuple-element.19.refs_0_, ...), custom_call_target="tpu_custom_call" | custom-call | tf_op jit(solution)/shard_map/combine/pallas_call | solution.py:341
  197.7 3.8 %fusion.28 = (f32[4,64]{1,0:T(4,128)S(1)}, bf16[4,64,768]{2,1,0:T(8,128)(2,1)}) fusion(pred[4,768]{1,0:T(4,128)(4,1)S(1)} %iota_compare_fusion, bf16[4,64,576]{2,1,0:T(8,128)(2,1)} %param.13, bf16[4,768,576]{1,2,0:T(8,128)(2,1)} %param.14), kind=kOutput, calls=%fused_computation.70 | convolution fusion | flops 227672832 | bytes 4231168 | tf_op jit(solution)/shard_map/sub | solution.py:72
  202.5 4.4 %collective-permute-start.22 = (bf16[128,896]{1,0:T(8,128)(2,1)}, bf16[128,896]{1,0:T(8,128)(2,1)S(1)}, u32[]{:S(2)}, u32[]{:S(2)}) collective-permute-start(bf16[128,896]{1,0:T(8,128)(2,1)} %get-tuple-element.31), channel_id=1, source_target_pairs={{0,4},{1,5},{2,6},{3,7},{4,0},{5,1},{6,2},{7,3},{8,12},{9,13},{10,... | collective-permute-start | bytes 688136 | tf_op jit(solution)/shard_map/ppermute | solution.py:55
  208.7 3.0 %fusion.10 = bf16[4,64,512]{2,1,0:T(8,128)(2,1)S(1)} fusion(bf16[4,768,576]{1,2,0:T(8,128)(2,1)} %param.14, bf16[4,64,768]{2,1,0:T(8,128)(2,1)S(1)} %copy-done.21, f32[4,64]{1,0:T(4,128)S(1)} %get-tuple-element.36), kind=kOutput, calls=%fused_computation.10 | convolution fusion | flops 201588736 | bytes 3802112 | tf_op jit(solution)/shard_map/rhp,rpc->rhc/dot_general | solution.py:74
  212.6 3.4 %all-to-all-start = ((bf16[4,64,512]{2,0,1:T(4,128)(2,1)}), bf16[4,64,512]{2,0,1:T(4,128)(2,1)S(1)}, u32[]{:S(2)}, u32[]{:S(2)}) async-start(bf16[4,64,512]{2,0,1:T(4,128)(2,1)} %copy.34), calls=%async_computation | async-start | bytes 524288 | tf_op jit(solution)/shard_map/all_to_all | solution.py:509
  216.0 2.0 collective-permute-done.22
  219.4 2.8 %collective-permute-start.25 = (bf16[32,896]{1,0:T(8,128)(2,1)}, bf16[32,896]{1,0:T(8,128)(2,1)S(1)}, u32[]{:S(2)}, u32[]{:S(2)}) collective-permute-start(bf16[32,896]{1,0:T(8,128)(2,1)} %get-tuple-element.35), channel_id=1, source_target_pairs={{0,16},{8,24},{16,0},{24,8},{32,48},{40,56},{48,32},{56,40},{64,80... | collective-permute-start | bytes 172040 | tf_op jit(solution)/shard_map/ppermute | solution.py:50
  222.2 2.0 collective-permute-start.24
  224.2 2.5 %dynamic-slice_bitcast_fusion = (bf16[8,224,128]{2,1,0:T(8,128)(2,1)}, bf16[8,224,128]{2,1,0:T(8,128)(2,1)}, bf16[8,224,128]{2,1,0:T(8,128)(2,1)}, bf16[8,224,128]{2,1,0:T(8,128)(2,1)S(1)}) fusion(bf16[8,4,224,128]{3,2,1,0:T(8,128)(2,1)} %all-to-all-done.3, s32[]{:T(128)S(6)} %select_n.101, s32[]{:T(128)S(6)} %select_n.99, s32[]{:T(128)S(6)} %select_n.97, ...), kind=kLoop, calls=%fused_computation.13 | loop fusion | bytes 3670032 | tf_op jit(solution)/shard_map/jit(dynamic_index_in_dim)/squeeze | solution.py:439
  226.8 2.1 collective-permute-start.29
  231.8 8.6 %collective-permute-done.28.refs_1_ = bf16[8,224,128]{2,1,0:T(8,128)(2,1)S(1)} collective-permute-done((bf16[8,224,128]{2,1,0:T(8,128)(2,1)}, bf16[8,224,128]{2,1,0:T(8,128)(2,1)S(1)}, u32[]{:S(2)}, u32[]{:S(2)}) %collective-permute-start.28) | collective-permute-done | bytes 458784 | tf_op jit(solution)/shard_map/ppermute | solution.py:50
  242.0 7.6 %collective-permute-done.30.refs_3_ = bf16[8,224,128]{2,1,0:T(8,128)(2,1)S(1)} collective-permute-done((bf16[8,224,128]{2,1,0:T(8,128)(2,1)}, bf16[8,224,128]{2,1,0:T(8,128)(2,1)S(1)}, u32[]{:S(2)}, u32[]{:S(2)}) %collective-permute-start.30) | collective-permute-done | bytes 458784 | tf_op jit(solution)/shard_map/ppermute | solution.py:50
  (122 shorter events, 47.7 us)
Async XLA Ops:
  5.1 13.2 %collective-permute-start.2 = (bf16[32,1024]{1,0:T(8,128)(2,1)S(1)}, bf16[32,1024]{1,0:T(8,128)(2,1)S(1)}, u32[]{:S(2)}, u32[]{:S(2)}) collective-permute-start(bf16[32,1024]{1,0:T(8,128)(2,1)S(1)} %pack_rows.1), channel_id=1, source_target_pairs={{0,24},{8,0},{16,8},{24,16},{32,56},{40,32},{48,40},{56,48},{64,88... | collective-permute-start | bytes 196616 | tf_op jit(solution)/shard_map/ppermute | solution.py:50
  7.4 10.9 %collective-permute-start.1 = (bf16[32,1024]{1,0:T(8,128)(2,1)S(1)}, bf16[32,1024]{1,0:T(8,128)(2,1)S(1)}, u32[]{:S(2)}, u32[]{:S(2)}) collective-permute-start(bf16[32,1024]{1,0:T(8,128)(2,1)S(1)} %pack_rows.1), channel_id=1, source_target_pairs={{0,16},{8,24},{16,0},{24,8},{32,48},{40,56},{48,32},{56,40},{64,80... | collective-permute-start | bytes 196616 | tf_op jit(solution)/shard_map/ppermute | solution.py:50
  8.1 10.2 %collective-permute-start = (bf16[32,1024]{1,0:T(8,128)(2,1)S(1)}, bf16[32,1024]{1,0:T(8,128)(2,1)S(1)}, u32[]{:S(2)}, u32[]{:S(2)}) collective-permute-start(bf16[32,1024]{1,0:T(8,128)(2,1)S(1)} %pack_rows.1), channel_id=1, source_target_pairs={{0,8},{8,16},{16,24},{24,0},{32,40},{40,48},{48,56},{56,32},{64,72... | collective-permute-start | bytes 196616 | tf_op jit(solution)/shard_map/ppermute | solution.py:50
  16.3 30.5 %collective-permute-start.15 = (bf16[896,256]{1,0:T(8,128)(2,1)S(1)}, bf16[896,256]{1,0:T(8,128)(2,1)}, u32[]{:S(2)}, u32[]{:S(2)}) collective-permute-start(bf16[896,256]{1,0:T(8,128)(2,1)S(1)} %get-tuple-element.18), channel_id=1, source_target_pairs={{0,24},{8,0},{16,8},{24,16},{32,56},{40,32},{48,40},{56,48},{64,88... | collective-permute-start | bytes 1376264 | tf_op jit(solution)/shard_map/ppermute | solution.py:50
  16.5 32.1 %collective-permute-start.12 = (bf16[1024,256]{1,0:T(8,128)(2,1)S(1)}, bf16[1024,256]{1,0:T(8,128)(2,1)}, u32[]{:S(2)}, u32[]{:S(2)}) collective-permute-start(bf16[1024,256]{1,0:T(8,128)(2,1)S(1)} %get-tuple-element.16), channel_id=1, source_target_pairs={{0,8},{8,16},{16,24},{24,0},{32,40},{40,48},{48,56},{56,32},{64,72... | collective-permute-start | bytes 1572872 | tf_op jit(solution)/shard_map/ppermute | solution.py:50
  19.1 33.1 %collective-permute-start.4 = (bf16[128,1024]{1,0:T(8,128)(2,1)S(1)}, bf16[128,1024]{1,0:T(8,128)(2,1)S(1)}, u32[]{:S(2)}, u32[]{:S(2)}) collective-permute-start(bf16[128,1024]{1,0:T(8,128)(2,1)S(1)} %collective-permute-done.3.refs_0_), channel_id=1, source_target_pairs={{0,2},{1,3},{2,4},{3,5},{4,6},{5,7},{6,0},{7,1},{8,10},{9,11},{10,... | collective-permute-start | bytes 786440 | tf_op jit(solution)/shard_map/ppermute | solution.py:55
  42.9 16.1 %collective-permute-start.5 = (bf16[128,1024]{1,0:T(8,128)(2,1)S(1)}, bf16[128,1024]{1,0:T(8,128)(2,1)}, u32[]{:S(2)}, u32[]{:S(2)}) collective-permute-start(bf16[128,1024]{1,0:T(8,128)(2,1)S(1)} %collective-permute-done.3.refs_0_), channel_id=1, source_target_pairs={{0,4},{1,5},{2,6},{3,7},{4,0},{5,1},{6,2},{7,3},{8,12},{9,13},{10,... | collective-permute-start | bytes 786440 | tf_op jit(solution)/shard_map/ppermute | solution.py:55
  46.5 35.0 %collective-permute-start.11 = (bf16[1920,256]{1,0:T(8,128)(2,1)}, bf16[1920,256]{1,0:T(8,128)(2,1)S(1)}, u32[]{:S(2)}, u32[]{:S(2)}) collective-permute-start(bf16[1920,256]{1,0:T(8,128)(2,1)} %get-tuple-element.15), channel_id=1, source_target_pairs={{0,8},{8,16},{16,24},{24,0},{32,40},{40,48},{48,56},{56,32},{64,72... | collective-permute-start | bytes 2949128 | tf_op jit(solution)/shard_map/ppermute | solution.py:50
  46.8 34.7 %collective-permute-start.14 = (bf16[1920,256]{1,0:T(8,128)(2,1)}, bf16[1920,256]{1,0:T(8,128)(2,1)}, u32[]{:S(2)}, u32[]{:S(2)}) collective-permute-start(bf16[1920,256]{1,0:T(8,128)(2,1)} %get-tuple-element.17), channel_id=1, source_target_pairs={{0,24},{8,0},{16,8},{24,16},{32,56},{40,32},{48,40},{56,48},{64,88... | collective-permute-start | bytes 2949128 | tf_op jit(solution)/shard_map/ppermute | solution.py:50
  48.6 11.1 %collective-permute-start.6 = (bf16[128,1024]{1,0:T(8,128)(2,1)S(1)}, bf16[128,1024]{1,0:T(8,128)(2,1)}, u32[]{:S(2)}, u32[]{:S(2)}) collective-permute-start(bf16[128,1024]{1,0:T(8,128)(2,1)S(1)} %collective-permute-done.3.refs_0_), channel_id=1, source_target_pairs={{0,6},{1,7},{2,0},{3,1},{4,2},{5,3},{6,4},{7,5},{8,14},{9,15},{10,... | collective-permute-start | bytes 786440 | tf_op jit(solution)/shard_map/ppermute | solution.py:55
  52.1 8.1 %collective-permute-start.7 = (bf16[128,1024]{1,0:T(8,128)(2,1)S(1)}, bf16[128,1024]{1,0:T(8,128)(2,1)S(1)}, u32[]{:S(2)}, u32[]{:S(2)}) collective-permute-start(bf16[128,1024]{1,0:T(8,128)(2,1)S(1)} %collective-permute-done.3.refs_0_), channel_id=1, source_target_pairs={{0,1},{1,0},{2,3},{3,2},{4,5},{5,4},{6,7},{7,6},{8,9},{9,8},{10,11... | collective-permute-start | bytes 786440 | tf_op jit(solution)/shard_map/ppermute | solution.py:59
  59.7 4.0 %collective-permute-start.9 = (bf16[128,1024]{1,0:T(8,128)(2,1)}, bf16[128,1024]{1,0:T(8,128)(2,1)}, u32[]{:S(2)}, u32[]{:S(2)}) collective-permute-start(bf16[128,1024]{1,0:T(8,128)(2,1)} %collective-permute-done.5.refs_2_), channel_id=1, source_target_pairs={{0,1},{1,0},{2,3},{3,2},{4,5},{5,4},{6,7},{7,6},{8,9},{9,8},{10,11... | collective-permute-start | bytes 786440 | tf_op jit(solution)/shard_map/ppermute | solution.py:59
  60.9 20.7 %collective-permute-start.13 = (bf16[1024,256]{1,0:T(8,128)(2,1)}, bf16[1024,256]{1,0:T(8,128)(2,1)S(1)}, u32[]{:S(2)}, u32[]{:S(2)}) collective-permute-start(bf16[1024,256]{1,0:T(8,128)(2,1)} %collective-permute-done.12), channel_id=1, source_target_pairs={{0,8},{8,16},{16,24},{24,0},{32,40},{40,48},{48,56},{56,32},{64,72... | collective-permute-start | bytes 1572872 | tf_op jit(solution)/shard_map/ppermute | solution.py:50
  61.9 19.6 %collective-permute-start.16 = (bf16[896,256]{1,0:T(8,128)(2,1)}, bf16[896,256]{1,0:T(8,128)(2,1)}, u32[]{:S(2)}, u32[]{:S(2)}) collective-permute-start(bf16[896,256]{1,0:T(8,128)(2,1)} %collective-permute-done.15), channel_id=1, source_target_pairs={{0,24},{8,0},{16,8},{24,16},{32,56},{40,32},{48,40},{56,48},{64,88... | collective-permute-start | bytes 1376264 | tf_op jit(solution)/shard_map/ppermute | solution.py:50
  98.8 33.4 %all-to-all-start.1 = ((bf16[8,528,128]{2,1,0:T(8,128)(2,1)}), bf16[8,528,128]{2,1,0:T(8,128)(2,1)}, u32[]{:S(2)}, u32[]{:S(2)}) async-start(bf16[8,528,128]{2,1,0:T(8,128)(2,1)} %project.1), calls=%async_computation.1 | async-start | bytes 2162688 | tf_op jit(solution)/shard_map/all_to_all | solution.py:43
  134.6 21.4 %all-to-all-start.2 = ((bf16[8,256,128]{2,1,0:T(8,128)(2,1)}), bf16[8,256,128]{2,1,0:T(8,128)(2,1)S(1)}, u32[]{:S(2)}, u32[]{:S(2)}) async-start(bf16[8,256,128]{2,1,0:T(8,128)(2,1)} %activate.1), calls=%async_computation.2 | async-start | bytes 1048576 | tf_op jit(solution)/shard_map/all_to_all | solution.py:43
  156.0 56.6 %all-to-all-start.3 = ((bf16[8,4,224,128]{3,2,1,0:T(8,128)(2,1)}), bf16[8,4,224,128]{3,2,1,0:T(8,128)(2,1)}, u32[]{:S(2)}, u32[]{:S(2)}) async-start(bf16[8,4,224,128]{3,2,1,0:T(8,128)(2,1)} %bitcast.67), calls=%async_computation.3 | async-start | bytes 3670016 | tf_op jit(solution)/shard_map/all_to_all | solution.py:429
  161.8 14.2 %collective-permute-start.17 = (bf16[960,256]{1,0:T(8,128)(2,1)S(1)}, bf16[960,256]{1,0:T(8,128)(2,1)S(1)}, u32[]{:S(2)}, u32[]{:S(2)}) collective-permute-start(bf16[960,256]{1,0:T(8,128)(2,1)S(1)} %get-tuple-element.20), channel_id=1, source_target_pairs={{0,8},{8,16},{16,24},{24,0},{32,40},{40,48},{48,56},{56,32},{64,72... | collective-permute-start | bytes 1474568 | tf_op jit(solution)/shard_map/ppermute | solution.py:50
  163.2 15.6 %collective-permute-start.18 = (bf16[960,256]{1,0:T(8,128)(2,1)S(1)}, bf16[960,256]{1,0:T(8,128)(2,1)S(1)}, u32[]{:S(2)}, u32[]{:S(2)}) collective-permute-start(bf16[960,256]{1,0:T(8,128)(2,1)S(1)} %get-tuple-element.21), channel_id=1, source_target_pairs={{0,16},{8,24},{16,0},{24,8},{32,48},{40,56},{48,32},{56,40},{64,80... | collective-permute-start | bytes 1474568 | tf_op jit(solution)/shard_map/ppermute | solution.py:50
  165.9 22.1 %collective-permute-start.19 = (bf16[960,256]{1,0:T(8,128)(2,1)S(1)}, bf16[960,256]{1,0:T(8,128)(2,1)S(1)}, u32[]{:S(2)}, u32[]{:S(2)}) collective-permute-start(bf16[960,256]{1,0:T(8,128)(2,1)S(1)} %get-tuple-element.22), channel_id=1, source_target_pairs={{0,24},{8,0},{16,8},{24,16},{32,56},{40,32},{48,40},{56,48},{64,88... | collective-permute-start | bytes 1474568 | tf_op jit(solution)/shard_map/ppermute | solution.py:50
  196.9 4.6 %collective-permute-start.20 = (bf16[512,896]{1,0:T(8,128)(2,1)}, bf16[512,896]{1,0:T(8,128)(2,1)S(1)}, u32[]{:S(2)}, u32[]{:S(2)}) collective-permute-start(bf16[512,896]{1,0:T(8,128)(2,1)} %get-tuple-element.24), channel_id=1, source_target_pairs={{0,1},{1,0},{2,3},{3,2},{4,5},{5,4},{6,7},{7,6},{8,9},{9,8},{10,11... | collective-permute-start | bytes 2752520 | tf_op jit(solution)/shard_map/ppermute | solution.py:59
  202.5 13.4 %collective-permute-start.23 = (bf16[128,896]{1,0:T(8,128)(2,1)}, bf16[128,896]{1,0:T(8,128)(2,1)S(1)}, u32[]{:S(2)}, u32[]{:S(2)}) collective-permute-start(bf16[128,896]{1,0:T(8,128)(2,1)} %get-tuple-element.30), channel_id=1, source_target_pairs={{0,2},{1,3},{2,4},{3,5},{4,6},{5,7},{6,0},{7,1},{8,10},{9,11},{10,... | collective-permute-start | bytes 688136 | tf_op jit(solution)/shard_map/ppermute | solution.py:55
  202.5 15.4 %collective-permute-start.22 = (bf16[128,896]{1,0:T(8,128)(2,1)}, bf16[128,896]{1,0:T(8,128)(2,1)S(1)}, u32[]{:S(2)}, u32[]{:S(2)}) collective-permute-start(bf16[128,896]{1,0:T(8,128)(2,1)} %get-tuple-element.31), channel_id=1, source_target_pairs={{0,4},{1,5},{2,6},{3,7},{4,0},{5,1},{6,2},{7,3},{8,12},{9,13},{10,... | collective-permute-start | bytes 688136 | tf_op jit(solution)/shard_map/ppermute | solution.py:55
  207.0 11.0 %collective-permute-start.21 = (bf16[128,896]{1,0:T(8,128)(2,1)S(1)}, bf16[128,896]{1,0:T(8,128)(2,1)S(1)}, u32[]{:S(2)}, u32[]{:S(2)}) collective-permute-start(bf16[128,896]{1,0:T(8,128)(2,1)S(1)} %get-tuple-element.32), channel_id=1, source_target_pairs={{0,6},{1,7},{2,0},{3,1},{4,2},{5,3},{6,4},{7,5},{8,14},{9,15},{10,... | collective-permute-start | bytes 688136 | tf_op jit(solution)/shard_map/ppermute | solution.py:55
  212.6 16.4 %all-to-all-start = ((bf16[4,64,512]{2,0,1:T(4,128)(2,1)}), bf16[4,64,512]{2,0,1:T(4,128)(2,1)S(1)}, u32[]{:S(2)}, u32[]{:S(2)}) async-start(bf16[4,64,512]{2,0,1:T(4,128)(2,1)} %copy.34), calls=%async_computation | async-start | bytes 524288 | tf_op jit(solution)/shard_map/all_to_all | solution.py:509
  218.8 10.1 %collective-permute-start.26 = (bf16[32,896]{1,0:T(8,128)(2,1)S(1)}, bf16[32,896]{1,0:T(8,128)(2,1)S(1)}, u32[]{:S(2)}, u32[]{:S(2)}) collective-permute-start(bf16[32,896]{1,0:T(8,128)(2,1)S(1)} %get-tuple-element.34), channel_id=1, source_target_pairs={{0,8},{8,16},{16,24},{24,0},{32,40},{40,48},{48,56},{56,32},{64,72... | collective-permute-start | bytes 172040 | tf_op jit(solution)/shard_map/ppermute | solution.py:50
  219.4 9.8 %collective-permute-start.25 = (bf16[32,896]{1,0:T(8,128)(2,1)}, bf16[32,896]{1,0:T(8,128)(2,1)S(1)}, u32[]{:S(2)}, u32[]{:S(2)}) collective-permute-start(bf16[32,896]{1,0:T(8,128)(2,1)} %get-tuple-element.35), channel_id=1, source_target_pairs={{0,16},{8,24},{16,0},{24,8},{32,48},{40,56},{48,32},{56,40},{64,80... | collective-permute-start | bytes 172040 | tf_op jit(solution)/shard_map/ppermute | solution.py:50
  222.2 7.0 %collective-permute-start.24 = (bf16[32,896]{1,0:T(8,128)(2,1)}, bf16[32,896]{1,0:T(8,128)(2,1)}, u32[]{:S(2)}, u32[]{:S(2)}) collective-permute-start(bf16[32,896]{1,0:T(8,128)(2,1)} %get-tuple-element.33), channel_id=1, source_target_pairs={{0,24},{8,0},{16,8},{24,16},{32,56},{40,32},{48,40},{56,48},{64,88... | collective-permute-start | bytes 172040 | tf_op jit(solution)/shard_map/ppermute | solution.py:50
  226.7 13.7 %collective-permute-start.28 = (bf16[8,224,128]{2,1,0:T(8,128)(2,1)}, bf16[8,224,128]{2,1,0:T(8,128)(2,1)S(1)}, u32[]{:S(2)}, u32[]{:S(2)}) collective-permute-start(bf16[8,224,128]{2,1,0:T(8,128)(2,1)} %get-tuple-element.27), channel_id=1, source_target_pairs={{0,8},{8,16},{16,24},{24,0},{32,40},{40,48},{48,56},{56,32},{64,72... | collective-permute-start | bytes 1376264 | tf_op jit(solution)/shard_map/ppermute | solution.py:50
  226.8 15.2 %collective-permute-start.29 = (bf16[8,224,128]{2,1,0:T(8,128)(2,1)}, bf16[8,224,128]{2,1,0:T(8,128)(2,1)S(1)}, u32[]{:S(2)}, u32[]{:S(2)}) collective-permute-start(bf16[8,224,128]{2,1,0:T(8,128)(2,1)} %get-tuple-element.26), channel_id=1, source_target_pairs={{0,16},{8,24},{16,0},{24,8},{32,48},{40,56},{48,32},{56,40},{64,80... | collective-permute-start | bytes 1376264 | tf_op jit(solution)/shard_map/ppermute | solution.py:50
  228.9 20.7 %collective-permute-start.30 = (bf16[8,224,128]{2,1,0:T(8,128)(2,1)}, bf16[8,224,128]{2,1,0:T(8,128)(2,1)S(1)}, u32[]{:S(2)}, u32[]{:S(2)}) collective-permute-start(bf16[8,224,128]{2,1,0:T(8,128)(2,1)} %get-tuple-element.25), channel_id=1, source_target_pairs={{0,24},{8,0},{16,8},{24,16},{32,56},{40,32},{48,40},{56,48},{64,88... | collective-permute-start | bytes 1376264 | tf_op jit(solution)/shard_map/ppermute | solution.py:50
  230.2 20.7 %collective-permute-start.27 = (bf16[32,896]{1,0:T(8,128)(2,1)S(1)}, bf16[32,896]{1,0:T(8,128)(2,1)S(1)}, u32[]{:S(2)}, u32[]{:S(2)}) collective-permute-start(bf16[32,896]{1,0:T(8,128)(2,1)S(1)} %add_convert_fusion.4), channel_id=1, source_target_pairs={{0,0},{1,32},{2,64},{3,96},{4,128},{5,160},{6,192},{7,224},{8,8},{... | collective-permute-start | bytes 172040 | tf_op jit(solution)/shard_map/ppermute | solution.py:39
  (25 other events, 358.7 us)

commit v5 on v4

--- a/solution.py
+++ b/solution.py
@@ -389,8 +389,9 @@
 
 
 def gather_rows(packed):
-    came = [shift_x(packed, s) for s in range(1, NX)]
-    ring = swap_zt(jnp.concatenate([packed] + came, axis=0))
+    moved = swap_zt(packed)
+    came = [shift_x(moved, s) for s in range(1, NX)]
+    ring = jnp.concatenate([moved] + came, axis=0)
     mine = [ring] + [shift_y(ring, s) for s in range(1, NY)]
     return mine + [other_core(block) for block in mine]
 

time: 253 us -> 252 us (level)
  starting transfers between devices: 75.1 us -> 72.1 us
  waiting for transfers between devices: 103 us -> 106 us
    ppermute x18, waiting for transfers between devices: 54 us -> 71 us  [shift_x(): return lax.ppermute(value, 'expert', pairs)]
    ppermute x6, waiting for transfers between devices: 11.7 us -> 3.5 us  [shift_y(): return lax.ppermute(value, 'tensor', pairs)]
    all_to_all x2, waiting for transfers between devices: 37.1 us -> 31.7 us  [exchange(): lax.all_to_all(value, 'expert', split_axis=0, concat_axis=0, tiled=True,...]
    ppermute x6, starting transfers between devices: 33.6 us -> 29.4 us  [shift_y(): return lax.ppermute(value, 'tensor', pairs)]
    unnamed x54 -> x53, local copies, waits for them, and re-layouts: 19.3 us -> 17 us
  transfers between devices with their start and end apart: 35 -> 35, of which waited for: 13 -> 17; matrix products, arithmetic and copies ran while one was open for 10% -> 10% of each run, Pallas kernels for 6% -> 6%
where the time goes in v5:
time: 252 us; the launch traced here: 250 us
  waiting for transfers between devices  106 us (42%)
  starting transfers between devices  72.1 us (29%)
  Pallas kernels  30.9 us (12%)
  local copies, waits for them, and re-layouts  25.5 us (10%)
  matrix products  7.01 us (3%)
  other arithmetic  5.04 us (2%)
  between operations  2.82 us (1%)
    ppermute x18, waiting for transfers between devices, shift_x(): return lax.ppermute(value, 'expert', pairs)  71 us
    all_to_all x2, waiting for transfers between devices, exchange(): lax.all_to_all(value, 'expert', split_axis=0, concat_axis=0, tiled=True,...  31.7 us
    ppermute x6, starting transfers between devices, shift_y(): return lax.ppermute(value, 'tensor', pairs)  29.4 us
    ppermute x18, starting transfers between devices, shift_x(): return lax.ppermute(value, 'expert', pairs)  24.8 us
    unnamed x53, local copies, waits for them, and re-layouts  17 us
    pallas_call x1, Pallas kernels, project(): pl.pallas_call(project_body, in_specs=[SMEM] + [VMEM] * (NZ + 5), out_sha...  13.4 us
    all_to_all x2, starting transfers between devices, exchange(): lax.all_to_all(value, 'expert', split_axis=0, concat_axis=0, tiled=True,...  8.78 us
    pallas_call x1, Pallas kernels, combine(): pl.pallas_call(combine_body, in_specs=[SMEM] + [VMEM] * (2 + NX), out_spe...  8.17 us
  transfers between devices with their start and end apart: 35, of which 17 were waited for; matrix products, arithmetic and copies ran while one was open for 10% of the time, Pallas kernels for 6%

profile of v5, /device:TPU:2, one launch (start us, length us, event | category | flops | bytes accessed | tf_op | source)
XLA Modules:
  0.0 249.7 jit_solution(9449081770473541396)
XLA Ops:
  7.4 2.8 %collective-permute-start.2 = (bf16[32,1024]{1,0:T(8,128)(2,1)S(1)}, bf16[32,1024]{1,0:T(8,128)(2,1)S(1)}, u32[]{:S(2)}, u32[]{:S(2)}) collective-permute-start(bf16[32,1024]{1,0:T(8,128)(2,1)S(1)} %collective-permute-done), channel_id=1, source_target_pairs={{0,16},{8,24},{16,0},{24,8},{32,48},{40,56},{48,32},{56,40},{64,80... | collective-permute-start | bytes 196616 | tf_op jit(solution)/shard_map/ppermute | solution.py:50
  10.7 2.5 collective-permute-done.2
  14.5 9.8 %collective-permute-start.4 = (bf16[128,1024]{1,0:T(8,128)(2,1)S(1)}, bf16[128,1024]{1,0:T(8,128)(2,1)}, u32[]{:S(2)}, u32[]{:S(2)}) collective-permute-start(bf16[128,1024]{1,0:T(8,128)(2,1)S(1)} %constant_dynamic-update-slice_fusion.refs_0_), channel_id=1, source_target_pairs={{0,2},{1,3},{2,4},{3,5},{4,6},{5,7},{6,0},{7,1},{8,10},{9,11},{10,... | collective-permute-start | bytes 786440 | tf_op jit(solution)/shard_map/ppermute | solution.py:55
  24.3 5.5 %collective-permute-start.5 = (bf16[128,1024]{1,0:T(8,128)(2,1)S(1)}, bf16[128,1024]{1,0:T(8,128)(2,1)}, u32[]{:S(2)}, u32[]{:S(2)}) collective-permute-start(bf16[128,1024]{1,0:T(8,128)(2,1)S(1)} %constant_dynamic-update-slice_fusion.refs_0_), channel_id=1, source_target_pairs={{0,4},{1,5},{2,6},{3,7},{4,0},{5,1},{6,2},{7,3},{8,12},{9,13},{10,... | collective-permute-start | bytes 786440 | tf_op jit(solution)/shard_map/ppermute | solution.py:55
  34.2 3.4 %turn_gate_up.1 = (bf16[1920,256]{1,0:T(8,128)(2,1)S(1)}, bf16[1920,256]{1,0:T(8,128)(2,1)}, bf16[1024,256]{1,0:T(8,128)(2,1)S(1)}, bf16[1920,256]{1,0:T(8,128)(2,1)}, bf16[896,256]{1,0:T(8,128)(2,1)S(1)}) custom-call(s32[1]{0:T(128)} %bitcast.3.own_ref, bf16[30,224,128]{2,1,0:T(8,128)(2,1)S(1)} %copy-done.1, bf16[30,224,128]{2,1,0:T(8,128)(2,1)S(1)} %copy-done.4), custom_call_target="tpu_custom_call" | custom-call | tf_op jit(solution)/shard_map/turn_gate_up/pallas_call | solution.py:145
  39.6 2.2 collective-permute-done.5.refs_2_
  44.5 6.1 %collective-permute-done.15 = bf16[896,256]{1,0:T(8,128)(2,1)} collective-permute-done((bf16[896,256]{1,0:T(8,128)(2,1)S(1)}, bf16[896,256]{1,0:T(8,128)(2,1)}, u32[]{:S(2)}, u32[]{:S(2)}) %collective-permute-start.15) | collective-permute-done | bytes 458784 | tf_op jit(solution)/shard_map/ppermute | solution.py:50
  50.7 3.9 %collective-permute-done.12 = bf16[1024,256]{1,0:T(8,128)(2,1)} collective-permute-done((bf16[1024,256]{1,0:T(8,128)(2,1)S(1)}, bf16[1024,256]{1,0:T(8,128)(2,1)}, u32[]{:S(2)}, u32[]{:S(2)}) %collective-permute-start.12) | collective-permute-done | bytes 524320 | tf_op jit(solution)/shard_map/ppermute | solution.py:50
  55.3 3.2 %collective-permute-start.16 = (bf16[896,256]{1,0:T(8,128)(2,1)}, bf16[896,256]{1,0:T(8,128)(2,1)}, u32[]{:S(2)}, u32[]{:S(2)}) collective-permute-start(bf16[896,256]{1,0:T(8,128)(2,1)} %collective-permute-done.15), channel_id=1, source_target_pairs={{0,24},{8,0},{16,8},{24,16},{32,56},{40,32},{48,40},{56,48},{64,88... | collective-permute-start | bytes 1376264 | tf_op jit(solution)/shard_map/ppermute | solution.py:50
  61.2 17.9 %collective-permute-done.16.refs_12_ = bf16[896,256]{1,0:T(8,128)(2,1)} collective-permute-done((bf16[896,256]{1,0:T(8,128)(2,1)}, bf16[896,256]{1,0:T(8,128)(2,1)}, u32[]{:S(2)}, u32[]{:S(2)}) %collective-permute-start.16) | collective-permute-done | bytes 458784 | tf_op jit(solution)/shard_map/ppermute | solution.py:50
  79.1 4.1 %collective-permute-done.13.refs_10_ = bf16[1024,256]{1,0:T(8,128)(2,1)S(1)} collective-permute-done((bf16[1024,256]{1,0:T(8,128)(2,1)}, bf16[1024,256]{1,0:T(8,128)(2,1)S(1)}, u32[]{:S(2)}, u32[]{:S(2)}) %collective-permute-start.13) | collective-permute-done | bytes 524320 | tf_op jit(solution)/shard_map/ppermute | solution.py:50
  86.0 13.4 %project.1 = bf16[8,528,128]{2,1,0:T(8,128)(2,1)} custom-call(s32[9]{0:T(128)S(1)} %pad_add_fusion.z_ref, bf16[128,1024]{1,0:T(8,128)(2,1)S(1)} %copy-done.6, bf16[128,1024]{1,0:T(8,128)(2,1)} %collective-permute-done.4.refs_1_, bf16[128,1024]{1,0:T(8,128)(2,1)} %collective-permute-done.5.refs_2_, bf16[128,1024]{1,0:T(8,128)(2,1)} %collective-permute-done.6.refs_3_, ...), custom_call_target="tpu_custom_call" | custom-call | tf_op jit(solution)/shard_map/project/pallas_call | solution.py:233
  99.5 5.3 %all-to-all-start.1 = ((bf16[8,528,128]{2,1,0:T(8,128)(2,1)}), bf16[8,528,128]{2,1,0:T(8,128)(2,1)}, u32[]{:S(2)}, u32[]{:S(2)}) async-start(bf16[8,528,128]{2,1,0:T(8,128)(2,1)} %project.1), calls=%async_computation.1 | async-start | bytes 2162688 | tf_op jit(solution)/shard_map/all_to_all | solution.py:43
  111.0 20.6 %all-to-all-done.1.p_ref = bf16[8,528,128]{2,1,0:T(8,128)(2,1)} async-done(((bf16[8,528,128]{2,1,0:T(8,128)(2,1)}), bf16[8,528,128]{2,1,0:T(8,128)(2,1)}, u32[]{:S(2)}, u32[]{:S(2)}) %all-to-all-start.1) | async-done | bytes 1081376 | tf_op jit(solution)/shard_map/all_to_all | solution.py:43
  131.6 2.4 activate.1
  134.0 3.5 %all-to-all-start.2 = ((bf16[8,256,128]{2,1,0:T(8,128)(2,1)}), bf16[8,256,128]{2,1,0:T(8,128)(2,1)S(1)}, u32[]{:S(2)}, u32[]{:S(2)}) async-start(bf16[8,256,128]{2,1,0:T(8,128)(2,1)} %activate.1), calls=%async_computation.2 | async-start | bytes 1048576 | tf_op jit(solution)/shard_map/all_to_all | solution.py:43
  139.0 2.1 gather_fusion
  141.1 11.1 %all-to-all-done.2.a_ref = bf16[8,256,128]{2,1,0:T(8,128)(2,1)S(1)} async-done(((bf16[8,256,128]{2,1,0:T(8,128)(2,1)}), bf16[8,256,128]{2,1,0:T(8,128)(2,1)S(1)}, u32[]{:S(2)}, u32[]{:S(2)}) %all-to-all-start.2) | async-done | bytes 524320 | tf_op jit(solution)/shard_map/all_to_all | solution.py:43
  152.2 4.5 %all-to-all-start.3 = ((bf16[8,4,224,128]{3,2,1,0:T(8,128)(2,1)}), bf16[8,4,224,128]{3,2,1,0:T(8,128)(2,1)}, u32[]{:S(2)}, u32[]{:S(2)}) async-start(bf16[8,4,224,128]{3,2,1,0:T(8,128)(2,1)} %bitcast.67), calls=%async_computation.3 | async-start | bytes 3670016 | tf_op jit(solution)/shard_map/all_to_all | solution.py:430
  158.2 4.5 %collective-permute-start.18 = (bf16[960,256]{1,0:T(8,128)(2,1)S(1)}, bf16[960,256]{1,0:T(8,128)(2,1)S(1)}, u32[]{:S(2)}, u32[]{:S(2)}) collective-permute-start(bf16[960,256]{1,0:T(8,128)(2,1)S(1)} %get-tuple-element.21), channel_id=1, source_target_pairs={{0,16},{8,24},{16,0},{24,8},{32,48},{40,56},{48,32},{56,40},{64,80... | collective-permute-start | bytes 1474568 | tf_op jit(solution)/shard_map/ppermute | solution.py:50
  162.7 10.0 %collective-permute-done.17.refs_1_ = bf16[960,256]{1,0:T(8,128)(2,1)S(1)} collective-permute-done((bf16[960,256]{1,0:T(8,128)(2,1)S(1)}, bf16[960,256]{1,0:T(8,128)(2,1)S(1)}, u32[]{:S(2)}, u32[]{:S(2)}) %collective-permute-start.17) | collective-permute-done | bytes 491552 | tf_op jit(solution)/shard_map/ppermute | solution.py:50
  174.7 5.3 %collective-permute-done.19.refs_3_ = bf16[960,256]{1,0:T(8,128)(2,1)S(1)} collective-permute-done((bf16[960,256]{1,0:T(8,128)(2,1)S(1)}, bf16[960,256]{1,0:T(8,128)(2,1)S(1)}, u32[]{:S(2)}, u32[]{:S(2)}) %collective-permute-start.19) | collective-permute-done | bytes 491552 | tf_op jit(solution)/shard_map/ppermute | solution.py:50
  180.7 8.2 %combine.1 = (bf16[512,896]{1,0:T(8,128)(2,1)S(1)}, bf16[512,896]{1,0:T(8,128)(2,1)}) custom-call(s32[9]{0:T(128)S(1)} %copy-done.13, bf16[8,256,128]{2,1,0:T(8,128)(2,1)S(1)} %all-to-all-done.2.a_ref, bf16[1024,128]{1,0:T(8,128)(2,1)S(1)} %bitcast.65, bf16[960,256]{1,0:T(8,128)(2,1)S(1)} %get-tuple-element.19.refs_0_, ...), custom_call_target="tpu_custom_call" | custom-call | tf_op jit(solution)/shard_map/combine/pallas_call | solution.py:341
  189.6 3.8 %fusion.28 = (f32[4,64]{1,0:T(4,128)S(1)}, bf16[4,64,768]{2,1,0:T(8,128)(2,1)}) fusion(pred[4,768]{1,0:T(4,128)(4,1)S(1)} %iota_compare_fusion, bf16[4,64,576]{2,1,0:T(8,128)(2,1)} %param.13, bf16[4,768,576]{1,2,0:T(8,128)(2,1)} %param.14), kind=kOutput, calls=%fused_computation.73 | convolution fusion | flops 227672832 | bytes 4231168 | tf_op jit(solution)/shard_map/sub | solution.py:72
  194.4 9.9 %collective-permute-start.23 = (bf16[128,896]{1,0:T(8,128)(2,1)}, bf16[128,896]{1,0:T(8,128)(2,1)S(1)}, u32[]{:S(2)}, u32[]{:S(2)}) collective-permute-start(bf16[128,896]{1,0:T(8,128)(2,1)} %get-tuple-element.30), channel_id=1, source_target_pairs={{0,2},{1,3},{2,4},{3,5},{4,6},{5,7},{6,0},{7,1},{8,10},{9,11},{10,... | collective-permute-start | bytes 688136 | tf_op jit(solution)/shard_map/ppermute | solution.py:55
  204.3 2.7 %collective-permute-start.21 = (bf16[128,896]{1,0:T(8,128)(2,1)S(1)}, bf16[128,896]{1,0:T(8,128)(2,1)S(1)}, u32[]{:S(2)}, u32[]{:S(2)}) collective-permute-start(bf16[128,896]{1,0:T(8,128)(2,1)S(1)} %get-tuple-element.32), channel_id=1, source_target_pairs={{0,6},{1,7},{2,0},{3,1},{4,2},{5,3},{6,4},{7,5},{8,14},{9,15},{10,... | collective-permute-start | bytes 688136 | tf_op jit(solution)/shard_map/ppermute | solution.py:55
  207.0 3.0 %fusion.10 = bf16[4,64,512]{2,1,0:T(8,128)(2,1)S(1)} fusion(bf16[4,768,576]{1,2,0:T(8,128)(2,1)} %param.14, bf16[4,64,768]{2,1,0:T(8,128)(2,1)S(1)} %copy-done.19, f32[4,64]{1,0:T(4,128)S(1)} %get-tuple-element.36), kind=kOutput, calls=%fused_computation.10 | convolution fusion | flops 201588736 | bytes 3802112 | tf_op jit(solution)/shard_map/rhp,rpc->rhc/dot_general | solution.py:74
  210.8 3.4 %all-to-all-start = ((bf16[4,64,512]{2,0,1:T(4,128)(2,1)}), bf16[4,64,512]{2,0,1:T(4,128)(2,1)S(1)}, u32[]{:S(2)}, u32[]{:S(2)}) async-start(bf16[4,64,512]{2,0,1:T(4,128)(2,1)} %copy.34), calls=%async_computation | async-start | bytes 524288 | tf_op jit(solution)/shard_map/all_to_all | solution.py:510
  217.0 3.2 %collective-permute-start.25 = (bf16[32,896]{1,0:T(8,128)(2,1)}, bf16[32,896]{1,0:T(8,128)(2,1)S(1)}, u32[]{:S(2)}, u32[]{:S(2)}) collective-permute-start(bf16[32,896]{1,0:T(8,128)(2,1)} %get-tuple-element.35), channel_id=1, source_target_pairs={{0,16},{8,24},{16,0},{24,8},{32,48},{40,56},{48,32},{56,40},{64,80... | collective-permute-start | bytes 172040 | tf_op jit(solution)/shard_map/ppermute | solution.py:50
  221.9 2.5 %dynamic-slice_bitcast_fusion = (bf16[8,224,128]{2,1,0:T(8,128)(2,1)}, bf16[8,224,128]{2,1,0:T(8,128)(2,1)}, bf16[8,224,128]{2,1,0:T(8,128)(2,1)}, bf16[8,224,128]{2,1,0:T(8,128)(2,1)S(1)}) fusion(bf16[8,4,224,128]{3,2,1,0:T(8,128)(2,1)} %all-to-all-done.3, s32[]{:T(128)S(6)} %select_n.101, s32[]{:T(128)S(6)} %select_n.99, s32[]{:T(128)S(6)} %select_n.97, ...), kind=kLoop, calls=%fused_computation.13 | loop fusion | bytes 3670032 | tf_op jit(solution)/shard_map/jit(dynamic_index_in_dim)/squeeze | solution.py:440
  229.8 8.3 %collective-permute-done.28.refs_1_ = bf16[8,224,128]{2,1,0:T(8,128)(2,1)S(1)} collective-permute-done((bf16[8,224,128]{2,1,0:T(8,128)(2,1)}, bf16[8,224,128]{2,1,0:T(8,128)(2,1)S(1)}, u32[]{:S(2)}, u32[]{:S(2)}) %collective-permute-start.28) | collective-permute-done | bytes 458784 | tf_op jit(solution)/shard_map/ppermute | solution.py:50
  240.0 7.8 %collective-permute-done.30.refs_3_ = bf16[8,224,128]{2,1,0:T(8,128)(2,1)S(1)} collective-permute-done((bf16[8,224,128]{2,1,0:T(8,128)(2,1)}, bf16[8,224,128]{2,1,0:T(8,128)(2,1)S(1)}, u32[]{:S(2)}, u32[]{:S(2)}) %collective-permute-start.30) | collective-permute-done | bytes 458784 | tf_op jit(solution)/shard_map/ppermute | solution.py:50
  (121 shorter events, 50.1 us)
Async XLA Ops:
  5.8 4.8 %collective-permute-start.1 = (bf16[32,1024]{1,0:T(8,128)(2,1)S(1)}, bf16[32,1024]{1,0:T(8,128)(2,1)S(1)}, u32[]{:S(2)}, u32[]{:S(2)}) collective-permute-start(bf16[32,1024]{1,0:T(8,128)(2,1)S(1)} %collective-permute-done), channel_id=1, source_target_pairs={{0,8},{8,16},{16,24},{24,0},{32,40},{40,48},{48,56},{56,32},{64,72... | collective-permute-start | bytes 196616 | tf_op jit(solution)/shard_map/ppermute | solution.py:50
  7.4 5.8 %collective-permute-start.2 = (bf16[32,1024]{1,0:T(8,128)(2,1)S(1)}, bf16[32,1024]{1,0:T(8,128)(2,1)S(1)}, u32[]{:S(2)}, u32[]{:S(2)}) collective-permute-start(bf16[32,1024]{1,0:T(8,128)(2,1)S(1)} %collective-permute-done), channel_id=1, source_target_pairs={{0,16},{8,24},{16,0},{24,8},{32,48},{40,56},{48,32},{56,40},{64,80... | collective-permute-start | bytes 196616 | tf_op jit(solution)/shard_map/ppermute | solution.py:50
  10.2 4.3 %collective-permute-start.3 = (bf16[32,1024]{1,0:T(8,128)(2,1)S(1)}, bf16[32,1024]{1,0:T(8,128)(2,1)S(1)}, u32[]{:S(2)}, u32[]{:S(2)}) collective-permute-start(bf16[32,1024]{1,0:T(8,128)(2,1)S(1)} %collective-permute-done), channel_id=1, source_target_pairs={{0,24},{8,0},{16,8},{24,16},{32,56},{40,32},{48,40},{56,48},{64,88... | collective-permute-start | bytes 196616 | tf_op jit(solution)/shard_map/ppermute | solution.py:50
  14.5 25.2 %collective-permute-start.4 = (bf16[128,1024]{1,0:T(8,128)(2,1)S(1)}, bf16[128,1024]{1,0:T(8,128)(2,1)}, u32[]{:S(2)}, u32[]{:S(2)}) collective-permute-start(bf16[128,1024]{1,0:T(8,128)(2,1)S(1)} %constant_dynamic-update-slice_fusion.refs_0_), channel_id=1, source_target_pairs={{0,2},{1,3},{2,4},{3,5},{4,6},{5,7},{6,0},{7,1},{8,10},{9,11},{10,... | collective-permute-start | bytes 786440 | tf_op jit(solution)/shard_map/ppermute | solution.py:55
  24.3 17.5 %collective-permute-start.5 = (bf16[128,1024]{1,0:T(8,128)(2,1)S(1)}, bf16[128,1024]{1,0:T(8,128)(2,1)}, u32[]{:S(2)}, u32[]{:S(2)}) collective-permute-start(bf16[128,1024]{1,0:T(8,128)(2,1)S(1)} %constant_dynamic-update-slice_fusion.refs_0_), channel_id=1, source_target_pairs={{0,4},{1,5},{2,6},{3,7},{4,0},{5,1},{6,2},{7,3},{8,12},{9,13},{10,... | collective-permute-start | bytes 786440 | tf_op jit(solution)/shard_map/ppermute | solution.py:55
  29.8 12.9 %collective-permute-start.6 = (bf16[128,1024]{1,0:T(8,128)(2,1)S(1)}, bf16[128,1024]{1,0:T(8,128)(2,1)}, u32[]{:S(2)}, u32[]{:S(2)}) collective-permute-start(bf16[128,1024]{1,0:T(8,128)(2,1)S(1)} %constant_dynamic-update-slice_fusion.refs_0_), channel_id=1, source_target_pairs={{0,6},{1,7},{2,0},{3,1},{4,2},{5,3},{6,4},{7,5},{8,14},{9,15},{10,... | collective-permute-start | bytes 786440 | tf_op jit(solution)/shard_map/ppermute | solution.py:55
  37.6 13.1 %collective-permute-start.15 = (bf16[896,256]{1,0:T(8,128)(2,1)S(1)}, bf16[896,256]{1,0:T(8,128)(2,1)}, u32[]{:S(2)}, u32[]{:S(2)}) collective-permute-start(bf16[896,256]{1,0:T(8,128)(2,1)S(1)} %get-tuple-element.18), channel_id=1, source_target_pairs={{0,24},{8,0},{16,8},{24,16},{32,56},{40,32},{48,40},{56,48},{64,88... | collective-permute-start | bytes 1376264 | tf_op jit(solution)/shard_map/ppermute | solution.py:50
  39.1 15.5 %collective-permute-start.12 = (bf16[1024,256]{1,0:T(8,128)(2,1)S(1)}, bf16[1024,256]{1,0:T(8,128)(2,1)}, u32[]{:S(2)}, u32[]{:S(2)}) collective-permute-start(bf16[1024,256]{1,0:T(8,128)(2,1)S(1)} %get-tuple-element.16), channel_id=1, source_target_pairs={{0,8},{8,16},{16,24},{24,0},{32,40},{40,48},{48,56},{56,32},{64,72... | collective-permute-start | bytes 1572872 | tf_op jit(solution)/shard_map/ppermute | solution.py:50
  41.8 37.3 %collective-permute-start.11 = (bf16[1920,256]{1,0:T(8,128)(2,1)}, bf16[1920,256]{1,0:T(8,128)(2,1)S(1)}, u32[]{:S(2)}, u32[]{:S(2)}) collective-permute-start(bf16[1920,256]{1,0:T(8,128)(2,1)} %get-tuple-element.15), channel_id=1, source_target_pairs={{0,8},{8,16},{16,24},{24,0},{32,40},{40,48},{48,56},{56,32},{64,72... | collective-permute-start | bytes 2949128 | tf_op jit(solution)/shard_map/ppermute | solution.py:50
  42.7 36.5 %collective-permute-start.14 = (bf16[1920,256]{1,0:T(8,128)(2,1)}, bf16[1920,256]{1,0:T(8,128)(2,1)}, u32[]{:S(2)}, u32[]{:S(2)}) collective-permute-start(bf16[1920,256]{1,0:T(8,128)(2,1)} %get-tuple-element.17), channel_id=1, source_target_pairs={{0,24},{8,0},{16,8},{24,16},{32,56},{40,32},{48,40},{56,48},{64,88... | collective-permute-start | bytes 2949128 | tf_op jit(solution)/shard_map/ppermute | solution.py:50
  44.5 10.0 %collective-permute-start.8 = (bf16[128,1024]{1,0:T(8,128)(2,1)}, bf16[128,1024]{1,0:T(8,128)(2,1)S(1)}, u32[]{:S(2)}, u32[]{:S(2)}) collective-permute-start(bf16[128,1024]{1,0:T(8,128)(2,1)} %collective-permute-done.4.refs_1_), channel_id=1, source_target_pairs={{0,1},{1,0},{2,3},{3,2},{4,5},{5,4},{6,7},{7,6},{8,9},{9,8},{10,11... | collective-permute-start | bytes 786440 | tf_op jit(solution)/shard_map/ppermute | solution.py:59
  50.7 7.8 %collective-permute-start.9 = (bf16[128,1024]{1,0:T(8,128)(2,1)}, bf16[128,1024]{1,0:T(8,128)(2,1)}, u32[]{:S(2)}, u32[]{:S(2)}) collective-permute-start(bf16[128,1024]{1,0:T(8,128)(2,1)} %collective-permute-done.5.refs_2_), channel_id=1, source_target_pairs={{0,1},{1,0},{2,3},{3,2},{4,5},{5,4},{6,7},{7,6},{8,9},{9,8},{10,11... | collective-permute-start | bytes 786440 | tf_op jit(solution)/shard_map/ppermute | solution.py:59
  54.6 28.6 %collective-permute-start.13 = (bf16[1024,256]{1,0:T(8,128)(2,1)}, bf16[1024,256]{1,0:T(8,128)(2,1)S(1)}, u32[]{:S(2)}, u32[]{:S(2)}) collective-permute-start(bf16[1024,256]{1,0:T(8,128)(2,1)} %collective-permute-done.12), channel_id=1, source_target_pairs={{0,8},{8,16},{16,24},{24,0},{32,40},{40,48},{48,56},{56,32},{64,72... | collective-permute-start | bytes 1572872 | tf_op jit(solution)/shard_map/ppermute | solution.py:50
  55.3 23.8 %collective-permute-start.16 = (bf16[896,256]{1,0:T(8,128)(2,1)}, bf16[896,256]{1,0:T(8,128)(2,1)}, u32[]{:S(2)}, u32[]{:S(2)}) collective-permute-start(bf16[896,256]{1,0:T(8,128)(2,1)} %collective-permute-done.15), channel_id=1, source_target_pairs={{0,24},{8,0},{16,8},{24,16},{32,56},{40,32},{48,40},{56,48},{64,88... | collective-permute-start | bytes 1376264 | tf_op jit(solution)/shard_map/ppermute | solution.py:50
  99.5 32.1 %all-to-all-start.1 = ((bf16[8,528,128]{2,1,0:T(8,128)(2,1)}), bf16[8,528,128]{2,1,0:T(8,128)(2,1)}, u32[]{:S(2)}, u32[]{:S(2)}) async-start(bf16[8,528,128]{2,1,0:T(8,128)(2,1)} %project.1), calls=%async_computation.1 | async-start | bytes 2162688 | tf_op jit(solution)/shard_map/all_to_all | solution.py:43
  134.0 18.2 %all-to-all-start.2 = ((bf16[8,256,128]{2,1,0:T(8,128)(2,1)}), bf16[8,256,128]{2,1,0:T(8,128)(2,1)S(1)}, u32[]{:S(2)}, u32[]{:S(2)}) async-start(bf16[8,256,128]{2,1,0:T(8,128)(2,1)} %activate.1), calls=%async_computation.2 | async-start | bytes 1048576 | tf_op jit(solution)/shard_map/all_to_all | solution.py:43
  152.2 58.6 %all-to-all-start.3 = ((bf16[8,4,224,128]{3,2,1,0:T(8,128)(2,1)}), bf16[8,4,224,128]{3,2,1,0:T(8,128)(2,1)}, u32[]{:S(2)}, u32[]{:S(2)}) async-start(bf16[8,4,224,128]{3,2,1,0:T(8,128)(2,1)} %bitcast.67), calls=%async_computation.3 | async-start | bytes 3670016 | tf_op jit(solution)/shard_map/all_to_all | solution.py:430
  158.1 14.6 %collective-permute-start.17 = (bf16[960,256]{1,0:T(8,128)(2,1)S(1)}, bf16[960,256]{1,0:T(8,128)(2,1)S(1)}, u32[]{:S(2)}, u32[]{:S(2)}) collective-permute-start(bf16[960,256]{1,0:T(8,128)(2,1)S(1)} %get-tuple-element.20), channel_id=1, source_target_pairs={{0,8},{8,16},{16,24},{24,0},{32,40},{40,48},{48,56},{56,32},{64,72... | collective-permute-start | bytes 1474568 | tf_op jit(solution)/shard_map/ppermute | solution.py:50
  158.2 16.5 %collective-permute-start.18 = (bf16[960,256]{1,0:T(8,128)(2,1)S(1)}, bf16[960,256]{1,0:T(8,128)(2,1)S(1)}, u32[]{:S(2)}, u32[]{:S(2)}) collective-permute-start(bf16[960,256]{1,0:T(8,128)(2,1)S(1)} %get-tuple-element.21), channel_id=1, source_target_pairs={{0,16},{8,24},{16,0},{24,8},{32,48},{40,56},{48,32},{56,40},{64,80... | collective-permute-start | bytes 1474568 | tf_op jit(solution)/shard_map/ppermute | solution.py:50
  162.7 17.3 %collective-permute-start.19 = (bf16[960,256]{1,0:T(8,128)(2,1)S(1)}, bf16[960,256]{1,0:T(8,128)(2,1)S(1)}, u32[]{:S(2)}, u32[]{:S(2)}) collective-permute-start(bf16[960,256]{1,0:T(8,128)(2,1)S(1)} %get-tuple-element.22), channel_id=1, source_target_pairs={{0,24},{8,0},{16,8},{24,16},{32,56},{40,32},{48,40},{56,48},{64,88... | collective-permute-start | bytes 1474568 | tf_op jit(solution)/shard_map/ppermute | solution.py:50
  188.8 4.5 %collective-permute-start.20 = (bf16[512,896]{1,0:T(8,128)(2,1)}, bf16[512,896]{1,0:T(8,128)(2,1)S(1)}, u32[]{:S(2)}, u32[]{:S(2)}) collective-permute-start(bf16[512,896]{1,0:T(8,128)(2,1)} %get-tuple-element.24), channel_id=1, source_target_pairs={{0,1},{1,0},{2,3},{3,2},{4,5},{5,4},{6,7},{7,6},{8,9},{9,8},{10,11... | collective-permute-start | bytes 2752520 | tf_op jit(solution)/shard_map/ppermute | solution.py:59
  194.4 19.9 %collective-permute-start.23 = (bf16[128,896]{1,0:T(8,128)(2,1)}, bf16[128,896]{1,0:T(8,128)(2,1)S(1)}, u32[]{:S(2)}, u32[]{:S(2)}) collective-permute-start(bf16[128,896]{1,0:T(8,128)(2,1)} %get-tuple-element.30), channel_id=1, source_target_pairs={{0,2},{1,3},{2,4},{3,5},{4,6},{5,7},{6,0},{7,1},{8,10},{9,11},{10,... | collective-permute-start | bytes 688136 | tf_op jit(solution)/shard_map/ppermute | solution.py:55
  204.3 10.7 %collective-permute-start.22 = (bf16[128,896]{1,0:T(8,128)(2,1)}, bf16[128,896]{1,0:T(8,128)(2,1)S(1)}, u32[]{:S(2)}, u32[]{:S(2)}) collective-permute-start(bf16[128,896]{1,0:T(8,128)(2,1)} %get-tuple-element.31), channel_id=1, source_target_pairs={{0,4},{1,5},{2,6},{3,7},{4,0},{5,1},{6,2},{7,3},{8,12},{9,13},{10,... | collective-permute-start | bytes 688136 | tf_op jit(solution)/shard_map/ppermute | solution.py:55
  204.3 11.3 %collective-permute-start.21 = (bf16[128,896]{1,0:T(8,128)(2,1)S(1)}, bf16[128,896]{1,0:T(8,128)(2,1)S(1)}, u32[]{:S(2)}, u32[]{:S(2)}) collective-permute-start(bf16[128,896]{1,0:T(8,128)(2,1)S(1)} %get-tuple-element.32), channel_id=1, source_target_pairs={{0,6},{1,7},{2,0},{3,1},{4,2},{5,3},{6,4},{7,5},{8,14},{9,15},{10,... | collective-permute-start | bytes 688136 | tf_op jit(solution)/shard_map/ppermute | solution.py:55
  210.8 16.2 %all-to-all-start = ((bf16[4,64,512]{2,0,1:T(4,128)(2,1)}), bf16[4,64,512]{2,0,1:T(4,128)(2,1)S(1)}, u32[]{:S(2)}, u32[]{:S(2)}) async-start(bf16[4,64,512]{2,0,1:T(4,128)(2,1)} %copy.34), calls=%async_computation | async-start | bytes 524288 | tf_op jit(solution)/shard_map/all_to_all | solution.py:510
  216.4 10.3 %collective-permute-start.26 = (bf16[32,896]{1,0:T(8,128)(2,1)S(1)}, bf16[32,896]{1,0:T(8,128)(2,1)S(1)}, u32[]{:S(2)}, u32[]{:S(2)}) collective-permute-start(bf16[32,896]{1,0:T(8,128)(2,1)S(1)} %get-tuple-element.34), channel_id=1, source_target_pairs={{0,8},{8,16},{16,24},{24,0},{32,40},{40,48},{48,56},{56,32},{64,72... | collective-permute-start | bytes 172040 | tf_op jit(solution)/shard_map/ppermute | solution.py:50
  217.0 10.3 %collective-permute-start.25 = (bf16[32,896]{1,0:T(8,128)(2,1)}, bf16[32,896]{1,0:T(8,128)(2,1)S(1)}, u32[]{:S(2)}, u32[]{:S(2)}) collective-permute-start(bf16[32,896]{1,0:T(8,128)(2,1)} %get-tuple-element.35), channel_id=1, source_target_pairs={{0,16},{8,24},{16,0},{24,8},{32,48},{40,56},{48,32},{56,40},{64,80... | collective-permute-start | bytes 172040 | tf_op jit(solution)/shard_map/ppermute | solution.py:50
  220.2 7.0 %collective-permute-start.24 = (bf16[32,896]{1,0:T(8,128)(2,1)}, bf16[32,896]{1,0:T(8,128)(2,1)}, u32[]{:S(2)}, u32[]{:S(2)}) collective-permute-start(bf16[32,896]{1,0:T(8,128)(2,1)} %get-tuple-element.33), channel_id=1, source_target_pairs={{0,24},{8,0},{16,8},{24,16},{32,56},{40,32},{48,40},{56,48},{64,88... | collective-permute-start | bytes 172040 | tf_op jit(solution)/shard_map/ppermute | solution.py:50
  224.5 13.7 %collective-permute-start.28 = (bf16[8,224,128]{2,1,0:T(8,128)(2,1)}, bf16[8,224,128]{2,1,0:T(8,128)(2,1)S(1)}, u32[]{:S(2)}, u32[]{:S(2)}) collective-permute-start(bf16[8,224,128]{2,1,0:T(8,128)(2,1)} %get-tuple-element.27), channel_id=1, source_target_pairs={{0,8},{8,16},{16,24},{24,0},{32,40},{40,48},{48,56},{56,32},{64,72... | collective-permute-start | bytes 1376264 | tf_op jit(solution)/shard_map/ppermute | solution.py:50
  224.9 15.1 %collective-permute-start.29 = (bf16[8,224,128]{2,1,0:T(8,128)(2,1)}, bf16[8,224,128]{2,1,0:T(8,128)(2,1)S(1)}, u32[]{:S(2)}, u32[]{:S(2)}) collective-permute-start(bf16[8,224,128]{2,1,0:T(8,128)(2,1)} %get-tuple-element.26), channel_id=1, source_target_pairs={{0,16},{8,24},{16,0},{24,8},{32,48},{40,56},{48,32},{56,40},{64,80... | collective-permute-start | bytes 1376264 | tf_op jit(solution)/shard_map/ppermute | solution.py:50
  226.7 21.1 %collective-permute-start.30 = (bf16[8,224,128]{2,1,0:T(8,128)(2,1)}, bf16[8,224,128]{2,1,0:T(8,128)(2,1)S(1)}, u32[]{:S(2)}, u32[]{:S(2)}) collective-permute-start(bf16[8,224,128]{2,1,0:T(8,128)(2,1)} %get-tuple-element.25), channel_id=1, source_target_pairs={{0,24},{8,0},{16,8},{24,16},{32,56},{40,32},{48,40},{56,48},{64,88... | collective-permute-start | bytes 1376264 | tf_op jit(solution)/shard_map/ppermute | solution.py:50
  228.2 20.9 %collective-permute-start.27 = (bf16[32,896]{1,0:T(8,128)(2,1)S(1)}, bf16[32,896]{1,0:T(8,128)(2,1)S(1)}, u32[]{:S(2)}, u32[]{:S(2)}) collective-permute-start(bf16[32,896]{1,0:T(8,128)(2,1)S(1)} %add_convert_fusion.4), channel_id=1, source_target_pairs={{0,0},{1,32},{2,64},{3,96},{4,128},{5,160},{6,192},{7,224},{8,8},{... | collective-permute-start | bytes 172040 | tf_op jit(solution)/shard_map/ppermute | solution.py:39
  (23 other events, 410.1 us)

commit v6 on v5

--- a/solution.py
+++ b/solution.py
@@ -173,7 +173,9 @@
 
 def project_body(z_ref, *refs):
     x_refs, w_refs = refs[:NZ], refs[NZ : NZ + 5]
-    p_ref, id_ref, y_ref = refs[NZ + 5 :]
+    p_ref, m_ref, id_ref, y_ref = refs[NZ + 5 :]
+    for n in range(NZ):
+        m_ref[z_ref[n]] = x_refs[n][:, 128:256]
     meta = jnp.concatenate([x[:, 128:256] for x in x_refs], axis=0)
     col = iota((128, TOP * 128), 1)
     pick = (iota((128, TOP * 128), 0) - META == col // 128).astype(F32).astype(BF)
@@ -233,7 +235,11 @@
     return pl.pallas_call(
         project_body,
         in_specs=[SMEM] + [VMEM] * (NZ + 5),
-        out_shape=jax.ShapeDtypeStruct((NZ, PB, 128), BF),
+        out_specs=[VMEM] * 2,
+        out_shape=[
+            jax.ShapeDtypeStruct((NZ, PB, 128), BF),
+            jax.ShapeDtypeStruct((NZ, ZR, 128), BF),
+        ],
         scratch_shapes=[
             pltpu.VMEM((TOP, ROWS, 128), BF),
             pltpu.VMEM((NE // 2, ROWS, 128), BF),
@@ -243,7 +249,7 @@
     )(blocks, *rows, *weights)
 
 
-def activate_body(p_ref, m_ref, o_ref):
+def activate_body(z_ref, p_ref, m_ref, o_ref):
     row = iota((128, 5 * 128), 0)
     col = iota((128, 5 * 128), 1)
     j = 2 * (col // 128) + (col % 128) // 64
@@ -252,7 +258,7 @@
         (row >= HIGH) & (row < LOW), 64.0, jnp.where((row >= LOW) & (row < SQ), 1.0, 0.0)
     )
     pick = jnp.where(col < 512, single, every).astype(BF)
-    weights = jnp.dot(m_ref[...], pick, preferred_element_type=F32)
+    weights = jnp.dot(m_ref[z_ref[0]], pick, preferred_element_type=F32)
     scale = ROUTE_SCALE / weights[:, 512:640]
     squares = jnp.zeros((16, 128), F32)
     for z in range(NZ):
@@ -276,13 +282,14 @@
             o_ref[z, q * ZR : (q + 1) * ZR, :] = packed
 
 
-def activate(parts, meta):
+def activate(z, parts, metas):
     return pl.pallas_call(
         activate_body,
+        in_specs=[SMEM] + [VMEM] * 2,
         out_shape=jax.ShapeDtypeStruct((NZ, 2 * ZR, 128), BF),
         compiler_params=pltpu.CompilerParams(vmem_limit_bytes=12 << 20),
         name="activate",
-    )(parts, meta)
+    )(z, parts, metas)
 
 
 def combine_body(z_ref, a_ref, m_ref, *refs):
@@ -297,7 +304,8 @@
     block = col % 128 // FX
     origin = (block - k + 4) % 4
     j = 4 * q + jnp.where(origin == 1, 2, jnp.where(origin == 2, 1, origin))
-    spread = jnp.dot(m_ref[...], (row == j).astype(F32).astype(BF), preferred_element_type=F32)
+    meta = jnp.concatenate([m_ref[z_ref[n]] for n in range(NZ)], axis=0)
+    spread = jnp.dot(meta, (row == j).astype(F32).astype(BF), preferred_element_type=F32)
     tags = (spread - (iota((1, TOP * 128), 1) % 128 // FX).astype(F32)).astype(BF)
     for n in range(TOP):
         id_ref[n] = tags[:, n * 128 : (n + 1) * 128]
@@ -397,14 +405,9 @@
 
 
 def block_places():
-    t = lax.axis_index("tensor")
-    y, c = t // 2, t % 2
-    s = jnp.arange(NY, dtype=jnp.int32)
-    turn = (y - s) % NY * 2
-    blocks = jnp.concatenate([turn + c, turn + 1 - c]).astype(jnp.int32)
-    zs = jnp.arange(NZ, dtype=jnp.int32)
-    places = (y - zs // 2) % NY + NY * (zs % 2 != c).astype(jnp.int32)
-    return blocks, places.astype(jnp.int32)
+    t = lax.axis_index("tensor").astype(jnp.int32)
+    n = jnp.arange(NZ, dtype=jnp.int32)
+    return ((t // 2 + NY - n % NY) % NY) * 2 + (t + n // NY) % 2
 
 
 def move_gate_up(pieces):
@@ -486,8 +489,7 @@
     own = (lax.axis_index("expert") % NX).astype(jnp.int32)[None]
     held = move_gate_up(turn_gate_up(own, learner_gate, learner_up))
     rows = gather_rows(pack_rows(hidden_in, norm_gain, expert_ids, route_weight, updated_list))
-    blocks, places = block_places()
-    blocks = jnp.concatenate([blocks, own])
+    blocks = jnp.concatenate([block_places(), own])
 
     entry_range = jnp.arange(NE, dtype=jnp.int32)
     learner_entry = jnp.sum(
@@ -497,12 +499,11 @@
     slot_gate = move_gate(jnp.take(learner_gate, learner_entry, axis=0, mode="clip"), own)
 
     held_down = move_down(turn_down(own, learner_down))
-    parts = exchange(project(blocks, rows, held), Z_GROUPS)
-    z = lax.axis_index("expert") // NX
-    metas = jnp.stack([block[:, 128:256] for block in rows])
-    meta = lax.dynamic_index_in_dim(metas, places[z], 0, keepdims=False)
-    acts = exchange(activate(parts, meta), Z_GROUPS)
-    near, far = combine(blocks, acts, metas.reshape(ROWS, 128), held_down)
+    sums, metas = project(blocks, rows, held)
+    parts = exchange(sums, Z_GROUPS)
+    z = (lax.axis_index("expert") // NX).astype(jnp.int32)[None]
+    acts = exchange(activate(z, parts, metas), Z_GROUPS)
+    near, far = combine(blocks, acts, metas, held_down)
     far = other_core(far)
     moe_out = gather_out(near, far)
 

time: 252 us -> 255 us (1.012)
  waiting for transfers between devices: 106 us -> 115 us
    all_to_all x2, waiting for transfers between devices: 31.7 us -> 38.7 us  [exchange(): lax.all_to_all(value, 'expert', split_axis=0, concat_axis=0, tiled=True,...]
    unnamed x53 -> x58, local copies, waits for them, and re-layouts: 17 us -> 17.3 us
  transfers between devices with their start and end apart: 35 -> 35, of which waited for: 17 -> 17; matrix products, arithmetic and copies ran while one was open for 10% -> 8% of each run, Pallas kernels for 6% -> 6%
where the time goes in v6:
time: 255 us; the launch traced here: 253 us
  waiting for transfers between devices  115 us (45%)
  starting transfers between devices  69.9 us (27%)
  Pallas kernels  30.1 us (12%)
  local copies, waits for them, and re-layouts  24.5 us (10%)
  matrix products  7.01 us (3%)
  other arithmetic  6.31 us (2%)
    ppermute x18, waiting for transfers between devices, shift_x(): return lax.ppermute(value, 'expert', pairs)  70.7 us
    all_to_all x2, waiting for transfers between devices, exchange(): lax.all_to_all(value, 'expert', split_axis=0, concat_axis=0, tiled=True,...  38.7 us
    ppermute x6, starting transfers between devices, shift_y(): return lax.ppermute(value, 'tensor', pairs)  28.1 us
    ppermute x18, starting transfers between devices, shift_x(): return lax.ppermute(value, 'expert', pairs)  24.7 us
    unnamed x58, local copies, waits for them, and re-layouts  17.3 us
    pallas_call x1, Pallas kernels, project(): pl.pallas_call(project_body, in_specs=[SMEM] + [VMEM] * (NZ + 5), out_spe...  13.4 us
    pallas_call x1, Pallas kernels, combine(): pl.pallas_call(combine_body, in_specs=[SMEM] + [VMEM] * (2 + NX), out_spe...  8.16 us
    all_to_all x2, starting transfers between devices, exchange(): lax.all_to_all(value, 'expert', split_axis=0, concat_axis=0, tiled=True,...  7.94 us
  transfers between devices with their start and end apart: 35, of which 17 were waited for; matrix products, arithmetic and copies ran while one was open for 8% of the time, Pallas kernels for 6%

profile of v6, /device:TPU:2, one launch (start us, length us, event | category | flops | bytes accessed | tf_op | source)
XLA Modules:
  0.0 253.4 jit_solution(12584581898031858701)
XLA Ops:
  7.4 2.8 %collective-permute-start.2 = (bf16[32,1024]{1,0:T(8,128)(2,1)S(1)}, bf16[32,1024]{1,0:T(8,128)(2,1)S(1)}, u32[]{:S(2)}, u32[]{:S(2)}) collective-permute-start(bf16[32,1024]{1,0:T(8,128)(2,1)S(1)} %collective-permute-done), channel_id=1, source_target_pairs={{0,16},{8,24},{16,0},{24,8},{32,48},{40,56},{48,32},{56,40},{64,80... | collective-permute-start | bytes 196616 | tf_op jit(solution)/shard_map/ppermute | solution.py:50
  10.7 2.5 collective-permute-done.2
  14.5 9.8 %collective-permute-start.4 = (bf16[128,1024]{1,0:T(8,128)(2,1)S(1)}, bf16[128,1024]{1,0:T(8,128)(2,1)}, u32[]{:S(2)}, u32[]{:S(2)}) collective-permute-start(bf16[128,1024]{1,0:T(8,128)(2,1)S(1)} %constant_dynamic-update-slice_fusion.refs_0_), channel_id=1, source_target_pairs={{0,2},{1,3},{2,4},{3,5},{4,6},{5,7},{6,0},{7,1},{8,10},{9,11},{10,... | collective-permute-start | bytes 786440 | tf_op jit(solution)/shard_map/ppermute | solution.py:55
  24.3 5.5 %collective-permute-start.5 = (bf16[128,1024]{1,0:T(8,128)(2,1)S(1)}, bf16[128,1024]{1,0:T(8,128)(2,1)}, u32[]{:S(2)}, u32[]{:S(2)}) collective-permute-start(bf16[128,1024]{1,0:T(8,128)(2,1)S(1)} %constant_dynamic-update-slice_fusion.refs_0_), channel_id=1, source_target_pairs={{0,4},{1,5},{2,6},{3,7},{4,0},{5,1},{6,2},{7,3},{8,12},{9,13},{10,... | collective-permute-start | bytes 786440 | tf_op jit(solution)/shard_map/ppermute | solution.py:55
  34.2 3.4 %turn_gate_up.1 = (bf16[1920,256]{1,0:T(8,128)(2,1)S(1)}, bf16[1920,256]{1,0:T(8,128)(2,1)}, bf16[1024,256]{1,0:T(8,128)(2,1)S(1)}, bf16[1920,256]{1,0:T(8,128)(2,1)}, bf16[896,256]{1,0:T(8,128)(2,1)S(1)}) custom-call(s32[1]{0:T(128)} %bitcast.3.own_ref, bf16[30,224,128]{2,1,0:T(8,128)(2,1)S(1)} %copy-done.1, bf16[30,224,128]{2,1,0:T(8,128)(2,1)S(1)} %copy-done.5), custom_call_target="tpu_custom_call" | custom-call | tf_op jit(solution)/shard_map/turn_gate_up/pallas_call | solution.py:145
  39.6 2.2 collective-permute-done.5.refs_2_
  44.6 8.0 %collective-permute-done.15 = bf16[896,256]{1,0:T(8,128)(2,1)} collective-permute-done((bf16[896,256]{1,0:T(8,128)(2,1)S(1)}, bf16[896,256]{1,0:T(8,128)(2,1)}, u32[]{:S(2)}, u32[]{:S(2)}) %collective-permute-start.15) | collective-permute-done | bytes 458784 | tf_op jit(solution)/shard_map/ppermute | solution.py:50
  52.6 2.1 collective-permute-start.13
  58.5 21.4 %collective-permute-done.16.refs_12_ = bf16[896,256]{1,0:T(8,128)(2,1)} collective-permute-done((bf16[896,256]{1,0:T(8,128)(2,1)}, bf16[896,256]{1,0:T(8,128)(2,1)}, u32[]{:S(2)}, u32[]{:S(2)}) %collective-permute-start.16) | collective-permute-done | bytes 458784 | tf_op jit(solution)/shard_map/ppermute | solution.py:50
  87.5 13.4 %project.1 = (bf16[8,528,128]{2,1,0:T(8,128)(2,1)}, bf16[8,128,128]{2,1,0:T(8,128)(2,1)S(1)}) custom-call(s32[9]{0:T(128)S(1)} %pad_add_fusion.z_ref, bf16[128,1024]{1,0:T(8,128)(2,1)S(1)} %copy-done.9, bf16[128,1024]{1,0:T(8,128)(2,1)} %collective-permute-done.4.refs_1_, bf16[128,1024]{1,0:T(8,128)(2,1)} %collective-permute-done.5.refs_2_, ...), custom_call_target="tpu_custom_call" | custom-call | tf_op jit(solution)/shard_map/project/pallas_call | solution.py:235
  101.3 4.5 %all-to-all-start.1 = ((bf16[8,528,128]{2,1,0:T(8,128)(2,1)}), bf16[8,528,128]{2,1,0:T(8,128)(2,1)}, u32[]{:S(2)}, u32[]{:S(2)}) async-start(bf16[8,528,128]{2,1,0:T(8,128)(2,1)} %get-tuple-element.21), calls=%async_computation.1 | async-start | bytes 2162688 | tf_op jit(solution)/shard_map/all_to_all | solution.py:43
  105.8 27.0 %all-to-all-done.1.p_ref = bf16[8,528,128]{2,1,0:T(8,128)(2,1)} async-done(((bf16[8,528,128]{2,1,0:T(8,128)(2,1)}), bf16[8,528,128]{2,1,0:T(8,128)(2,1)}, u32[]{:S(2)}, u32[]{:S(2)}) %all-to-all-start.1) | async-done | bytes 1081376 | tf_op jit(solution)/shard_map/all_to_all | solution.py:43
  135.3 3.5 %all-to-all-start.2 = ((bf16[8,256,128]{2,1,0:T(8,128)(2,1)}), bf16[8,256,128]{2,1,0:T(8,128)(2,1)S(1)}, u32[]{:S(2)}, u32[]{:S(2)}) async-start(bf16[8,256,128]{2,1,0:T(8,128)(2,1)} %copy-done.3), calls=%async_computation.2 | async-start | bytes 1048576 | tf_op jit(solution)/shard_map/all_to_all | solution.py:43
  140.2 2.1 gather_fusion
  142.4 11.7 %all-to-all-done.2.a_ref = bf16[8,256,128]{2,1,0:T(8,128)(2,1)S(1)} async-done(((bf16[8,256,128]{2,1,0:T(8,128)(2,1)}), bf16[8,256,128]{2,1,0:T(8,128)(2,1)S(1)}, u32[]{:S(2)}, u32[]{:S(2)}) %all-to-all-start.2) | async-done | bytes 524320 | tf_op jit(solution)/shard_map/all_to_all | solution.py:43
  154.1 4.5 %all-to-all-start.3 = ((bf16[8,4,224,128]{3,2,1,0:T(8,128)(2,1)}), bf16[8,4,224,128]{3,2,1,0:T(8,128)(2,1)}, u32[]{:S(2)}, u32[]{:S(2)}) async-start(bf16[8,4,224,128]{3,2,1,0:T(8,128)(2,1)} %bitcast.31), calls=%async_computation.3 | async-start | bytes 3670016 | tf_op jit(solution)/shard_map/all_to_all | solution.py:433
  160.2 4.7 %collective-permute-start.18 = (bf16[960,256]{1,0:T(8,128)(2,1)S(1)}, bf16[960,256]{1,0:T(8,128)(2,1)S(1)}, u32[]{:S(2)}, u32[]{:S(2)}) collective-permute-start(bf16[960,256]{1,0:T(8,128)(2,1)S(1)} %get-tuple-element.25), channel_id=1, source_target_pairs={{0,16},{8,24},{16,0},{24,8},{32,48},{40,56},{48,32},{56,40},{64,80... | collective-permute-start | bytes 1474568 | tf_op jit(solution)/shard_map/ppermute | solution.py:50
  165.5 9.4 %collective-permute-done.17.refs_1_ = bf16[960,256]{1,0:T(8,128)(2,1)S(1)} collective-permute-done((bf16[960,256]{1,0:T(8,128)(2,1)S(1)}, bf16[960,256]{1,0:T(8,128)(2,1)S(1)}, u32[]{:S(2)}, u32[]{:S(2)}) %collective-permute-start.17) | collective-permute-done | bytes 491552 | tf_op jit(solution)/shard_map/ppermute | solution.py:50
  174.9 2.1 collective-permute-done.18.refs_2_
  177.0 6.0 %collective-permute-done.19.refs_3_ = bf16[960,256]{1,0:T(8,128)(2,1)S(1)} collective-permute-done((bf16[960,256]{1,0:T(8,128)(2,1)S(1)}, bf16[960,256]{1,0:T(8,128)(2,1)S(1)}, u32[]{:S(2)}, u32[]{:S(2)}) %collective-permute-start.19) | collective-permute-done | bytes 491552 | tf_op jit(solution)/shard_map/ppermute | solution.py:50
  183.6 8.2 %combine.1 = (bf16[512,896]{1,0:T(8,128)(2,1)S(1)}, bf16[512,896]{1,0:T(8,128)(2,1)}) custom-call(s32[9]{0:T(128)S(1)} %copy-done.18, bf16[8,256,128]{2,1,0:T(8,128)(2,1)S(1)} %all-to-all-done.2.a_ref, bf16[8,128,128]{2,1,0:T(8,128)(2,1)S(1)} %get-tuple-element.22.m_ref, bf16[960,256]{1,0:T(8,128)(2,1)S(1)} %get-tuple-element.23.refs_0_, ...), custom_call_target="tpu_custom_call" | custom-call | tf_op jit(solution)/shard_map/combine/pallas_call | solution.py:349
  192.5 3.8 %fusion.21 = (f32[4,64]{1,0:T(4,128)S(1)}, bf16[4,64,768]{2,1,0:T(8,128)(2,1)}) fusion(pred[4,768]{1,0:T(4,128)(4,1)S(1)} %iota_compare_fusion, bf16[4,64,576]{2,1,0:T(8,128)(2,1)} %param.13, bf16[4,768,576]{1,2,0:T(8,128)(2,1)} %param.14), kind=kOutput, calls=%fused_computation.53 | convolution fusion | flops 227672832 | bytes 4231168 | tf_op jit(solution)/shard_map/sub | solution.py:72
  197.2 2.3 add_convert_fusion.3
  199.6 8.6 %collective-permute-start.23 = (bf16[128,896]{1,0:T(8,128)(2,1)}, bf16[128,896]{1,0:T(8,128)(2,1)S(1)}, u32[]{:S(2)}, u32[]{:S(2)}) collective-permute-start(bf16[128,896]{1,0:T(8,128)(2,1)} %get-tuple-element.34), channel_id=1, source_target_pairs={{0,2},{1,3},{2,4},{3,5},{4,6},{5,7},{6,0},{7,1},{8,10},{9,11},{10,... | collective-permute-start | bytes 688136 | tf_op jit(solution)/shard_map/ppermute | solution.py:55
  208.2 2.7 %collective-permute-start.21 = (bf16[128,896]{1,0:T(8,128)(2,1)S(1)}, bf16[128,896]{1,0:T(8,128)(2,1)S(1)}, u32[]{:S(2)}, u32[]{:S(2)}) collective-permute-start(bf16[128,896]{1,0:T(8,128)(2,1)S(1)} %get-tuple-element.36), channel_id=1, source_target_pairs={{0,6},{1,7},{2,0},{3,1},{4,2},{5,3},{6,4},{7,5},{8,14},{9,15},{10,... | collective-permute-start | bytes 688136 | tf_op jit(solution)/shard_map/ppermute | solution.py:55
  210.9 3.0 %fusion.10 = bf16[4,64,512]{2,1,0:T(8,128)(2,1)S(1)} fusion(bf16[4,768,576]{1,2,0:T(8,128)(2,1)} %param.14, bf16[4,64,768]{2,1,0:T(8,128)(2,1)S(1)} %copy-done.25, f32[4,64]{1,0:T(4,128)S(1)} %get-tuple-element.40), kind=kOutput, calls=%fused_computation.10 | convolution fusion | flops 201588736 | bytes 3802112 | tf_op jit(solution)/shard_map/rhp,rpc->rhc/dot_general | solution.py:74
  214.8 3.4 %all-to-all-start = ((bf16[4,64,512]{2,0,1:T(4,128)(2,1)}), bf16[4,64,512]{2,0,1:T(4,128)(2,1)S(1)}, u32[]{:S(2)}, u32[]{:S(2)}) async-start(bf16[4,64,512]{2,0,1:T(4,128)(2,1)} %copy.34), calls=%async_computation | async-start | bytes 524288 | tf_op jit(solution)/shard_map/all_to_all | solution.py:511
  220.9 2.9 %collective-permute-start.25 = (bf16[32,896]{1,0:T(8,128)(2,1)}, bf16[32,896]{1,0:T(8,128)(2,1)S(1)}, u32[]{:S(2)}, u32[]{:S(2)}) collective-permute-start(bf16[32,896]{1,0:T(8,128)(2,1)} %get-tuple-element.39), channel_id=1, source_target_pairs={{0,16},{8,24},{16,0},{24,8},{32,48},{40,56},{48,32},{56,40},{64,80... | collective-permute-start | bytes 172040 | tf_op jit(solution)/shard_map/ppermute | solution.py:50
  225.8 2.5 %dynamic-slice_bitcast_fusion = (bf16[8,224,128]{2,1,0:T(8,128)(2,1)}, bf16[8,224,128]{2,1,0:T(8,128)(2,1)}, bf16[8,224,128]{2,1,0:T(8,128)(2,1)}, bf16[8,224,128]{2,1,0:T(8,128)(2,1)S(1)}) fusion(bf16[8,4,224,128]{3,2,1,0:T(8,128)(2,1)} %all-to-all-done.3, s32[]{:T(128)S(6)} %select_n.85, s32[]{:T(128)S(6)} %select_n.83, s32[]{:T(128)S(6)} %select_n.81, ...), kind=kLoop, calls=%fused_computation.13 | loop fusion | bytes 3670032 | tf_op jit(solution)/shard_map/jit(dynamic_index_in_dim)/squeeze | solution.py:443
  228.4 2.1 collective-permute-start.29
  233.3 8.6 %collective-permute-done.28.refs_1_ = bf16[8,224,128]{2,1,0:T(8,128)(2,1)S(1)} collective-permute-done((bf16[8,224,128]{2,1,0:T(8,128)(2,1)}, bf16[8,224,128]{2,1,0:T(8,128)(2,1)S(1)}, u32[]{:S(2)}, u32[]{:S(2)}) %collective-permute-start.28) | collective-permute-done | bytes 458784 | tf_op jit(solution)/shard_map/ppermute | solution.py:50
  243.6 7.8 %collective-permute-done.30.refs_3_ = bf16[8,224,128]{2,1,0:T(8,128)(2,1)S(1)} collective-permute-done((bf16[8,224,128]{2,1,0:T(8,128)(2,1)}, bf16[8,224,128]{2,1,0:T(8,128)(2,1)S(1)}, u32[]{:S(2)}, u32[]{:S(2)}) %collective-permute-start.30) | collective-permute-done | bytes 458784 | tf_op jit(solution)/shard_map/ppermute | solution.py:50
  (122 shorter events, 50.1 us)
Async XLA Ops:
  5.8 4.8 %collective-permute-start.1 = (bf16[32,1024]{1,0:T(8,128)(2,1)S(1)}, bf16[32,1024]{1,0:T(8,128)(2,1)S(1)}, u32[]{:S(2)}, u32[]{:S(2)}) collective-permute-start(bf16[32,1024]{1,0:T(8,128)(2,1)S(1)} %collective-permute-done), channel_id=1, source_target_pairs={{0,8},{8,16},{16,24},{24,0},{32,40},{40,48},{48,56},{56,32},{64,72... | collective-permute-start | bytes 196616 | tf_op jit(solution)/shard_map/ppermute | solution.py:50
  7.4 5.8 %collective-permute-start.2 = (bf16[32,1024]{1,0:T(8,128)(2,1)S(1)}, bf16[32,1024]{1,0:T(8,128)(2,1)S(1)}, u32[]{:S(2)}, u32[]{:S(2)}) collective-permute-start(bf16[32,1024]{1,0:T(8,128)(2,1)S(1)} %collective-permute-done), channel_id=1, source_target_pairs={{0,16},{8,24},{16,0},{24,8},{32,48},{40,56},{48,32},{56,40},{64,80... | collective-permute-start | bytes 196616 | tf_op jit(solution)/shard_map/ppermute | solution.py:50
  10.2 4.3 %collective-permute-start.3 = (bf16[32,1024]{1,0:T(8,128)(2,1)S(1)}, bf16[32,1024]{1,0:T(8,128)(2,1)S(1)}, u32[]{:S(2)}, u32[]{:S(2)}) collective-permute-start(bf16[32,1024]{1,0:T(8,128)(2,1)S(1)} %collective-permute-done), channel_id=1, source_target_pairs={{0,24},{8,0},{16,8},{24,16},{32,56},{40,32},{48,40},{56,48},{64,88... | collective-permute-start | bytes 196616 | tf_op jit(solution)/shard_map/ppermute | solution.py:50
  14.5 25.1 %collective-permute-start.4 = (bf16[128,1024]{1,0:T(8,128)(2,1)S(1)}, bf16[128,1024]{1,0:T(8,128)(2,1)}, u32[]{:S(2)}, u32[]{:S(2)}) collective-permute-start(bf16[128,1024]{1,0:T(8,128)(2,1)S(1)} %constant_dynamic-update-slice_fusion.refs_0_), channel_id=1, source_target_pairs={{0,2},{1,3},{2,4},{3,5},{4,6},{5,7},{6,0},{7,1},{8,10},{9,11},{10,... | collective-permute-start | bytes 786440 | tf_op jit(solution)/shard_map/ppermute | solution.py:55
  24.3 17.5 %collective-permute-start.5 = (bf16[128,1024]{1,0:T(8,128)(2,1)S(1)}, bf16[128,1024]{1,0:T(8,128)(2,1)}, u32[]{:S(2)}, u32[]{:S(2)}) collective-permute-start(bf16[128,1024]{1,0:T(8,128)(2,1)S(1)} %constant_dynamic-update-slice_fusion.refs_0_), channel_id=1, source_target_pairs={{0,4},{1,5},{2,6},{3,7},{4,0},{5,1},{6,2},{7,3},{8,12},{9,13},{10,... | collective-permute-start | bytes 786440 | tf_op jit(solution)/shard_map/ppermute | solution.py:55
  29.8 12.9 %collective-permute-start.6 = (bf16[128,1024]{1,0:T(8,128)(2,1)S(1)}, bf16[128,1024]{1,0:T(8,128)(2,1)}, u32[]{:S(2)}, u32[]{:S(2)}) collective-permute-start(bf16[128,1024]{1,0:T(8,128)(2,1)S(1)} %constant_dynamic-update-slice_fusion.refs_0_), channel_id=1, source_target_pairs={{0,6},{1,7},{2,0},{3,1},{4,2},{5,3},{6,4},{7,5},{8,14},{9,15},{10,... | collective-permute-start | bytes 786440 | tf_op jit(solution)/shard_map/ppermute | solution.py:55
  37.6 15.0 %collective-permute-start.12 = (bf16[1024,256]{1,0:T(8,128)(2,1)S(1)}, bf16[1024,256]{1,0:T(8,128)(2,1)}, u32[]{:S(2)}, u32[]{:S(2)}) collective-permute-start(bf16[1024,256]{1,0:T(8,128)(2,1)S(1)} %get-tuple-element.18), channel_id=1, source_target_pairs={{0,8},{8,16},{16,24},{24,0},{32,40},{40,48},{48,56},{56,32},{64,72... | collective-permute-start | bytes 1572872 | tf_op jit(solution)/shard_map/ppermute | solution.py:50
  38.6 14.0 %collective-permute-start.15 = (bf16[896,256]{1,0:T(8,128)(2,1)S(1)}, bf16[896,256]{1,0:T(8,128)(2,1)}, u32[]{:S(2)}, u32[]{:S(2)}) collective-permute-start(bf16[896,256]{1,0:T(8,128)(2,1)S(1)} %get-tuple-element.20), channel_id=1, source_target_pairs={{0,24},{8,0},{16,8},{24,16},{32,56},{40,32},{48,40},{56,48},{64,88... | collective-permute-start | bytes 1376264 | tf_op jit(solution)/shard_map/ppermute | solution.py:50
  39.6 4.2 %collective-permute-start.7 = (bf16[128,1024]{1,0:T(8,128)(2,1)S(1)}, bf16[128,1024]{1,0:T(8,128)(2,1)S(1)}, u32[]{:S(2)}, u32[]{:S(2)}) collective-permute-start(bf16[128,1024]{1,0:T(8,128)(2,1)S(1)} %constant_dynamic-update-slice_fusion.refs_0_), channel_id=1, source_target_pairs={{0,1},{1,0},{2,3},{3,2},{4,5},{5,4},{6,7},{7,6},{8,9},{9,8},{10,11... | collective-permute-start | bytes 786440 | tf_op jit(solution)/shard_map/ppermute | solution.py:59
  41.8 38.1 %collective-permute-start.11 = (bf16[1920,256]{1,0:T(8,128)(2,1)}, bf16[1920,256]{1,0:T(8,128)(2,1)S(1)}, u32[]{:S(2)}, u32[]{:S(2)}) collective-permute-start(bf16[1920,256]{1,0:T(8,128)(2,1)} %get-tuple-element.17), channel_id=1, source_target_pairs={{0,8},{8,16},{16,24},{24,0},{32,40},{40,48},{48,56},{56,32},{64,72... | collective-permute-start | bytes 2949128 | tf_op jit(solution)/shard_map/ppermute | solution.py:50
  42.7 37.2 %collective-permute-start.14 = (bf16[1920,256]{1,0:T(8,128)(2,1)}, bf16[1920,256]{1,0:T(8,128)(2,1)}, u32[]{:S(2)}, u32[]{:S(2)}) collective-permute-start(bf16[1920,256]{1,0:T(8,128)(2,1)} %get-tuple-element.19), channel_id=1, source_target_pairs={{0,24},{8,0},{16,8},{24,16},{32,56},{40,32},{48,40},{56,48},{64,88... | collective-permute-start | bytes 2949128 | tf_op jit(solution)/shard_map/ppermute | solution.py:50
  44.6 10.1 %collective-permute-start.8 = (bf16[128,1024]{1,0:T(8,128)(2,1)}, bf16[128,1024]{1,0:T(8,128)(2,1)S(1)}, u32[]{:S(2)}, u32[]{:S(2)}) collective-permute-start(bf16[128,1024]{1,0:T(8,128)(2,1)} %collective-permute-done.4.refs_1_), channel_id=1, source_target_pairs={{0,1},{1,0},{2,3},{3,2},{4,5},{5,4},{6,7},{7,6},{8,9},{9,8},{10,11... | collective-permute-start | bytes 786440 | tf_op jit(solution)/shard_map/ppermute | solution.py:59
  52.6 29.2 %collective-permute-start.13 = (bf16[1024,256]{1,0:T(8,128)(2,1)}, bf16[1024,256]{1,0:T(8,128)(2,1)S(1)}, u32[]{:S(2)}, u32[]{:S(2)}) collective-permute-start(bf16[1024,256]{1,0:T(8,128)(2,1)} %collective-permute-done.12), channel_id=1, source_target_pairs={{0,8},{8,16},{16,24},{24,0},{32,40},{40,48},{48,56},{56,32},{64,72... | collective-permute-start | bytes 1572872 | tf_op jit(solution)/shard_map/ppermute | solution.py:50
  55.4 24.5 %collective-permute-start.16 = (bf16[896,256]{1,0:T(8,128)(2,1)}, bf16[896,256]{1,0:T(8,128)(2,1)}, u32[]{:S(2)}, u32[]{:S(2)}) collective-permute-start(bf16[896,256]{1,0:T(8,128)(2,1)} %collective-permute-done.15), channel_id=1, source_target_pairs={{0,24},{8,0},{16,8},{24,16},{32,56},{40,32},{48,40},{56,48},{64,88... | collective-permute-start | bytes 1376264 | tf_op jit(solution)/shard_map/ppermute | solution.py:50
  101.3 31.5 %all-to-all-start.1 = ((bf16[8,528,128]{2,1,0:T(8,128)(2,1)}), bf16[8,528,128]{2,1,0:T(8,128)(2,1)}, u32[]{:S(2)}, u32[]{:S(2)}) async-start(bf16[8,528,128]{2,1,0:T(8,128)(2,1)} %get-tuple-element.21), calls=%async_computation.1 | async-start | bytes 2162688 | tf_op jit(solution)/shard_map/all_to_all | solution.py:43
  135.3 18.8 %all-to-all-start.2 = ((bf16[8,256,128]{2,1,0:T(8,128)(2,1)}), bf16[8,256,128]{2,1,0:T(8,128)(2,1)S(1)}, u32[]{:S(2)}, u32[]{:S(2)}) async-start(bf16[8,256,128]{2,1,0:T(8,128)(2,1)} %copy-done.3), calls=%async_computation.2 | async-start | bytes 1048576 | tf_op jit(solution)/shard_map/all_to_all | solution.py:43
  154.1 60.7 %all-to-all-start.3 = ((bf16[8,4,224,128]{3,2,1,0:T(8,128)(2,1)}), bf16[8,4,224,128]{3,2,1,0:T(8,128)(2,1)}, u32[]{:S(2)}, u32[]{:S(2)}) async-start(bf16[8,4,224,128]{3,2,1,0:T(8,128)(2,1)} %bitcast.31), calls=%async_computation.3 | async-start | bytes 3670016 | tf_op jit(solution)/shard_map/all_to_all | solution.py:433
  160.0 14.9 %collective-permute-start.17 = (bf16[960,256]{1,0:T(8,128)(2,1)S(1)}, bf16[960,256]{1,0:T(8,128)(2,1)S(1)}, u32[]{:S(2)}, u32[]{:S(2)}) collective-permute-start(bf16[960,256]{1,0:T(8,128)(2,1)S(1)} %get-tuple-element.24), channel_id=1, source_target_pairs={{0,8},{8,16},{16,24},{24,0},{32,40},{40,48},{48,56},{56,32},{64,72... | collective-permute-start | bytes 1474568 | tf_op jit(solution)/shard_map/ppermute | solution.py:50
  160.2 16.8 %collective-permute-start.18 = (bf16[960,256]{1,0:T(8,128)(2,1)S(1)}, bf16[960,256]{1,0:T(8,128)(2,1)S(1)}, u32[]{:S(2)}, u32[]{:S(2)}) collective-permute-start(bf16[960,256]{1,0:T(8,128)(2,1)S(1)} %get-tuple-element.25), channel_id=1, source_target_pairs={{0,16},{8,24},{16,0},{24,8},{32,48},{40,56},{48,32},{56,40},{64,80... | collective-permute-start | bytes 1474568 | tf_op jit(solution)/shard_map/ppermute | solution.py:50
  164.9 18.1 %collective-permute-start.19 = (bf16[960,256]{1,0:T(8,128)(2,1)S(1)}, bf16[960,256]{1,0:T(8,128)(2,1)S(1)}, u32[]{:S(2)}, u32[]{:S(2)}) collective-permute-start(bf16[960,256]{1,0:T(8,128)(2,1)S(1)} %get-tuple-element.26), channel_id=1, source_target_pairs={{0,24},{8,0},{16,8},{24,16},{32,56},{40,32},{48,40},{56,48},{64,88... | collective-permute-start | bytes 1474568 | tf_op jit(solution)/shard_map/ppermute | solution.py:50
  191.8 4.5 %collective-permute-start.20 = (bf16[512,896]{1,0:T(8,128)(2,1)}, bf16[512,896]{1,0:T(8,128)(2,1)S(1)}, u32[]{:S(2)}, u32[]{:S(2)}) collective-permute-start(bf16[512,896]{1,0:T(8,128)(2,1)} %get-tuple-element.28), channel_id=1, source_target_pairs={{0,1},{1,0},{2,3},{3,2},{4,5},{5,4},{6,7},{7,6},{8,9},{9,8},{10,11... | collective-permute-start | bytes 2752520 | tf_op jit(solution)/shard_map/ppermute | solution.py:59
  199.6 18.6 %collective-permute-start.23 = (bf16[128,896]{1,0:T(8,128)(2,1)}, bf16[128,896]{1,0:T(8,128)(2,1)S(1)}, u32[]{:S(2)}, u32[]{:S(2)}) collective-permute-start(bf16[128,896]{1,0:T(8,128)(2,1)} %get-tuple-element.34), channel_id=1, source_target_pairs={{0,2},{1,3},{2,4},{3,5},{4,6},{5,7},{6,0},{7,1},{8,10},{9,11},{10,... | collective-permute-start | bytes 688136 | tf_op jit(solution)/shard_map/ppermute | solution.py:55
  208.2 10.6 %collective-permute-start.22 = (bf16[128,896]{1,0:T(8,128)(2,1)}, bf16[128,896]{1,0:T(8,128)(2,1)S(1)}, u32[]{:S(2)}, u32[]{:S(2)}) collective-permute-start(bf16[128,896]{1,0:T(8,128)(2,1)} %get-tuple-element.35), channel_id=1, source_target_pairs={{0,4},{1,5},{2,6},{3,7},{4,0},{5,1},{6,2},{7,3},{8,12},{9,13},{10,... | collective-permute-start | bytes 688136 | tf_op jit(solution)/shard_map/ppermute | solution.py:55
  208.2 11.4 %collective-permute-start.21 = (bf16[128,896]{1,0:T(8,128)(2,1)S(1)}, bf16[128,896]{1,0:T(8,128)(2,1)S(1)}, u32[]{:S(2)}, u32[]{:S(2)}) collective-permute-start(bf16[128,896]{1,0:T(8,128)(2,1)S(1)} %get-tuple-element.36), channel_id=1, source_target_pairs={{0,6},{1,7},{2,0},{3,1},{4,2},{5,3},{6,4},{7,5},{8,14},{9,15},{10,... | collective-permute-start | bytes 688136 | tf_op jit(solution)/shard_map/ppermute | solution.py:55
  214.8 15.8 %all-to-all-start = ((bf16[4,64,512]{2,0,1:T(4,128)(2,1)}), bf16[4,64,512]{2,0,1:T(4,128)(2,1)S(1)}, u32[]{:S(2)}, u32[]{:S(2)}) async-start(bf16[4,64,512]{2,0,1:T(4,128)(2,1)} %copy.34), calls=%async_computation | async-start | bytes 524288 | tf_op jit(solution)/shard_map/all_to_all | solution.py:511
  220.3 10.2 %collective-permute-start.26 = (bf16[32,896]{1,0:T(8,128)(2,1)S(1)}, bf16[32,896]{1,0:T(8,128)(2,1)S(1)}, u32[]{:S(2)}, u32[]{:S(2)}) collective-permute-start(bf16[32,896]{1,0:T(8,128)(2,1)S(1)} %get-tuple-element.38), channel_id=1, source_target_pairs={{0,8},{8,16},{16,24},{24,0},{32,40},{40,48},{48,56},{56,32},{64,72... | collective-permute-start | bytes 172040 | tf_op jit(solution)/shard_map/ppermute | solution.py:50
  220.9 9.8 %collective-permute-start.25 = (bf16[32,896]{1,0:T(8,128)(2,1)}, bf16[32,896]{1,0:T(8,128)(2,1)S(1)}, u32[]{:S(2)}, u32[]{:S(2)}) collective-permute-start(bf16[32,896]{1,0:T(8,128)(2,1)} %get-tuple-element.39), channel_id=1, source_target_pairs={{0,16},{8,24},{16,0},{24,8},{32,48},{40,56},{48,32},{56,40},{64,80... | collective-permute-start | bytes 172040 | tf_op jit(solution)/shard_map/ppermute | solution.py:50
  223.8 6.9 %collective-permute-start.24 = (bf16[32,896]{1,0:T(8,128)(2,1)}, bf16[32,896]{1,0:T(8,128)(2,1)}, u32[]{:S(2)}, u32[]{:S(2)}) collective-permute-start(bf16[32,896]{1,0:T(8,128)(2,1)} %get-tuple-element.37), channel_id=1, source_target_pairs={{0,24},{8,0},{16,8},{24,16},{32,56},{40,32},{48,40},{56,48},{64,88... | collective-permute-start | bytes 172040 | tf_op jit(solution)/shard_map/ppermute | solution.py:50
  228.4 13.6 %collective-permute-start.28 = (bf16[8,224,128]{2,1,0:T(8,128)(2,1)}, bf16[8,224,128]{2,1,0:T(8,128)(2,1)S(1)}, u32[]{:S(2)}, u32[]{:S(2)}) collective-permute-start(bf16[8,224,128]{2,1,0:T(8,128)(2,1)} %get-tuple-element.31), channel_id=1, source_target_pairs={{0,8},{8,16},{16,24},{24,0},{32,40},{40,48},{48,56},{56,32},{64,72... | collective-permute-start | bytes 1376264 | tf_op jit(solution)/shard_map/ppermute | solution.py:50
  228.4 15.2 %collective-permute-start.29 = (bf16[8,224,128]{2,1,0:T(8,128)(2,1)}, bf16[8,224,128]{2,1,0:T(8,128)(2,1)S(1)}, u32[]{:S(2)}, u32[]{:S(2)}) collective-permute-start(bf16[8,224,128]{2,1,0:T(8,128)(2,1)} %get-tuple-element.30), channel_id=1, source_target_pairs={{0,16},{8,24},{16,0},{24,8},{32,48},{40,56},{48,32},{56,40},{64,80... | collective-permute-start | bytes 1376264 | tf_op jit(solution)/shard_map/ppermute | solution.py:50
  230.5 20.9 %collective-permute-start.30 = (bf16[8,224,128]{2,1,0:T(8,128)(2,1)}, bf16[8,224,128]{2,1,0:T(8,128)(2,1)S(1)}, u32[]{:S(2)}, u32[]{:S(2)}) collective-permute-start(bf16[8,224,128]{2,1,0:T(8,128)(2,1)} %get-tuple-element.29), channel_id=1, source_target_pairs={{0,24},{8,0},{16,8},{24,16},{32,56},{40,32},{48,40},{56,48},{64,88... | collective-permute-start | bytes 1376264 | tf_op jit(solution)/shard_map/ppermute | solution.py:50
  231.7 21.0 %collective-permute-start.27 = (bf16[32,896]{1,0:T(8,128)(2,1)S(1)}, bf16[32,896]{1,0:T(8,128)(2,1)S(1)}, u32[]{:S(2)}, u32[]{:S(2)}) collective-permute-start(bf16[32,896]{1,0:T(8,128)(2,1)S(1)} %add_convert_fusion.4), channel_id=1, source_target_pairs={{0,0},{1,32},{2,64},{3,96},{4,128},{5,160},{6,192},{7,224},{8,8},{... | collective-permute-start | bytes 172040 | tf_op jit(solution)/shard_map/ppermute | solution.py:39
  (29 other events, 383.8 us)
